TPU v7x, 256 devices: a whole 4x4x8 slice. The times are simulated.
256 devices in a mesh: section: 4 (over y_hi, core), expert: 64 (over y_lo, x, z).
Axes of the slice: x: 4, y: 4 (y_hi: 2, y_lo: 2; y = y_hi * 2 + y_lo), z: 8, core: 2. Of those that a mesh axis runs over, the one named last changes fastest.
Arguments:
- grad_out: bfloat16 [4, 2, 4096, 3584], P('section', None, 'expert'), may hold values from -6 to 6
- gate_probs: bfloat16 [4, 2, 4096, 2], P('section', None, 'expert'), may hold values from 0.049804688 to 1
- routes: int32 [4, 2, 4096, 2], P('section', None, 'expert'), may hold values from 0 to 15, all different within a row; in each aligned block of 64 rows (0 to 63, 64 to 127, ..., all dimensions but the last counted through in order) at most 12 rows name the same one
- saved_preacts: bfloat16 [4, 2, 64, 64, 12, 512], P('section', None, 'expert'), may hold values from -6 to 6
- w_gate_up: bfloat16 [4, 64, 3584, 512], P('section', 'expert'), may hold values from -0.09375 to 0.09375
- w_down: bfloat16 [4, 64, 256, 3584], P('section', 'expert'), may hold values from -0.1875 to 0.1875
Outputs:
- from_above: bfloat16 [4, 4096, 3584], P('section', 'expert')
- from_below: bfloat16 [4, 4096, 3584], P('section', 'expert')
- prob_grad: float32 [4, 2, 4096, 2], P('section', None, 'expert')
- down_grad: bfloat16 [4, 64, 256, 3584], P('section', 'expert')
Inputs may be any that keep to these rules, and one draw needn't show every extreme that they name: `routes`: each row names 2 different experts; within the 64 rows of one device for one section and stretch no expert is named by more than 12 rows, a bound that some block reaches.
All inputs are finite; a program needn't handle non-finite values.
Results may differ from a plain program's by a relative error of at most 0.015.
Values may be sent and summed in bfloat16 or wider, within the bound.
No kernel may reach another device: no remote copies, remote signals or barrier semaphores. Data moves between devices by JAX's collectives and lax.ppermute only.
A program may use at most 192 MiB of HBM per device.

v0:
```python
import jax
import jax.numpy as jnp
from jax import lax
from jax.sharding import PartitionSpec as P

SHARE = 4


def shifted(block, axis, distance):
    devices = range(lax.axis_size(axis))
    route = [(i - distance, i) for i in devices if i - distance in devices]
    return lax.ppermute(block, axis, route)


def slot_targets(expert_ids, experts, capacity):
    flat_ids = expert_ids.reshape(-1)
    onehot = (flat_ids[:, None] == jnp.arange(experts, dtype=jnp.int32)[None, :]).astype(jnp.int32)
    before = jnp.cumsum(onehot, axis=0) - onehot
    slot_index = jnp.sum(before * onehot, axis=1)
    return flat_ids * capacity + slot_index


def pack_block(grad_rows, gate_rows, expert_ids, experts, capacity):
    tok_rows = grad_rows.shape[0]
    top_count = expert_ids.shape[1]
    targets = slot_targets(expert_ids, experts, capacity)
    matches = targets[:, None] == jnp.arange(experts * capacity, dtype=jnp.int32)[None, :]
    token_ids = jnp.repeat(jnp.arange(tok_rows, dtype=jnp.int32), top_count)
    source_row = jnp.sum(jnp.where(matches, token_ids[:, None], 0), axis=0)
    filled = jnp.any(matches, axis=0)
    gathered = jnp.where(
        filled[:, None], jnp.take(grad_rows, source_row, axis=0), jnp.zeros((), grad_rows.dtype)
    )
    weights = jnp.sum(
        jnp.where(matches, gate_rows.reshape(-1)[:, None], jnp.zeros((), gate_rows.dtype)), axis=0
    )
    return (gathered.reshape(experts, capacity, -1), weights.reshape(experts, capacity), targets)


def spread(values):
    shape_rest = values.shape[1:]
    widened = jnp.broadcast_to(values[:, None], (values.shape[0], SHARE) + shape_rest)
    return widened.reshape((values.shape[0] * SHARE,) + shape_rest)


def expert_slice(received, gate_vals, preacts, gate_up, down_proj):
    hidden_width = down_proj.shape[0]
    back_proj = lax.dot_general(
        received, down_proj, (((1,), (1,)), ((), ())), preferred_element_type=jnp.float32
    )
    gate_pre = preacts[:, :hidden_width].astype(jnp.float32)
    up_pre = preacts[:, hidden_width:].astype(jnp.float32)
    sigmoid_gate = 1.0 / (1.0 + jnp.exp(-gate_pre))
    activation = gate_pre * sigmoid_gate
    hidden = activation * up_pre
    prob_part = jnp.sum(hidden * back_proj, axis=1).astype(jnp.bfloat16)
    scale_vals = gate_vals.astype(jnp.float32)[:, None]
    d_hidden = scale_vals * back_proj
    d_gate = d_hidden * up_pre * sigmoid_gate * (1.0 + gate_pre * (1.0 - sigmoid_gate))
    d_up = d_hidden * activation
    d_both = jnp.concatenate([d_gate, d_up], axis=1).astype(jnp.bfloat16)
    grad_part = lax.dot_general(
        d_both, gate_up, (((1,), (1,)), ((), ())), preferred_element_type=jnp.float32
    ).astype(jnp.bfloat16)
    scaled = (scale_vals * hidden).astype(jnp.bfloat16)
    weight_part = lax.dot_general(
        scaled, received, (((0,), (0,)), ((), ())), preferred_element_type=jnp.float32
    )
    return (grad_part, prob_part, weight_part)


def share_out(stretch_packs):
    rows = jnp.concatenate([spread(item[0]) for item in stretch_packs], axis=1)
    gates = jnp.concatenate([spread(item[1]) for item in stretch_packs], axis=1)
    return (rows, gates)


def share_in(got_rows, got_gates):
    return (got_rows, got_gates)


def share_back(grad_part, prob_part, slice_count, groups, capacity):
    width = grad_part.shape[-1]
    return (
        grad_part.reshape(slice_count, groups * capacity, width),
        prob_part.reshape(slice_count, groups * capacity),
    )


def unpack(grad_back, prob_back, targets, tok_rows, top_count):
    width = grad_back.shape[-1]
    folded = grad_back.astype(jnp.float32).reshape(-1, SHARE, grad_back.shape[1], width).sum(axis=1)
    folded = lax.optimization_barrier(folded.astype(jnp.bfloat16)).astype(jnp.float32)
    prob_fold = prob_back.astype(jnp.float32).reshape(-1, SHARE, prob_back.shape[1]).sum(axis=1)
    prob_fold = lax.optimization_barrier(prob_fold.astype(jnp.bfloat16)).astype(jnp.float32)
    table = folded.reshape(-1, width)
    token_grad = (
        jnp.take(table, targets, axis=0)
        .reshape(tok_rows, top_count, width)
        .sum(axis=1)
        .astype(jnp.bfloat16)
    )
    prob_grad = jnp.take(prob_fold.reshape(-1), targets, axis=0).reshape(tok_rows, top_count)
    return (token_grad, prob_grad)


def shards(grad_out, gate_probs, routes, saved_preacts, w_gate_up, w_down):
    slice_count = lax.axis_size("expert")
    experts = slice_count // SHARE
    capacity = saved_preacts.shape[4]
    tok_rows = grad_out.shape[2]
    width = grad_out.shape[3]
    top_count = routes.shape[3]
    gate_up = w_gate_up[0, 0]
    down_proj = w_down[0, 0]
    preact_width = saved_preacts.shape[5]
    packed = [
        pack_block(
            grad_out[0, stretch], gate_probs[0, stretch], routes[0, stretch], experts, capacity
        )
        for stretch in range(2)
    ]
    results = []
    sent_rows, sent_gates = share_out(packed)
    got_rows, got_gates = (
        lax.all_to_all(sent_rows, "expert", split_axis=0, concat_axis=0, tiled=True),
        lax.all_to_all(sent_gates, "expert", split_axis=0, concat_axis=0, tiled=True),
    )
    full_rows, full_gates = share_in(got_rows, got_gates)
    preacts = jnp.concatenate([saved_preacts[0, 0, 0], saved_preacts[0, 1, 0]], axis=1)
    grad_part, prob_part, weight_sum = expert_slice(
        full_rows.reshape(-1, width),
        full_gates.reshape(-1),
        preacts.reshape(-1, preact_width),
        gate_up,
        down_proj,
    )
    out_rows, out_probs = share_back(grad_part, prob_part, slice_count, 2, capacity)
    back_rows, back_probs = (
        lax.all_to_all(out_rows, "expert", split_axis=0, concat_axis=0, tiled=True),
        lax.all_to_all(out_probs, "expert", split_axis=0, concat_axis=0, tiled=True),
    )
    span = back_rows.shape[1] // 2
    for stretch in range(2):
        lower = stretch * span
        results.append(
            unpack(
                back_rows[:, lower : lower + span],
                back_probs[:, lower : lower + span],
                packed[stretch][2],
                tok_rows,
                top_count,
            )
        )
    first_grad, first_prob = results[0]
    second_grad, second_prob = results[1]
    from_above = shifted(first_grad, "section", -1)
    from_below = shifted(second_grad, "section", 1)
    prob_grad = jnp.stack([first_prob, second_prob])[None]
    down_grad = weight_sum.astype(jnp.bfloat16)[None, None]
    return (from_above[None], from_below[None], prob_grad, down_grad)


def solution(mesh):
    in_specs = (
        P("section", None, "expert", None),
        P("section", None, "expert", None),
        P("section", None, "expert", None),
        P("section", None, "expert", None, None, None),
        P("section", "expert", None, None),
        P("section", "expert", None, None),
    )
    out_specs = (
        P("section", "expert", None),
        P("section", "expert", None),
        P("section", None, "expert", None),
        P("section", "expert", None, None),
    )
    return jax.shard_map(shards, mesh=mesh, in_specs=in_specs, out_specs=out_specs, check_vma=False)
```

profile of v0, /device:TPU:1, one launch (start us, length us, event | category | flops | bytes accessed | tf_op | source)
XLA Modules:
  0.0 686.3 jit_solution(6535520333226831526)
XLA Ops:
  6.0 13.5 %all-to-all-start = ((bf16[64,1,24]{2,1,0:T(2,128)(2,1)}), bf16[64,1,24]{2,1,0:T(2,128)(2,1)S(1)}, u32[]{:S(2)}, u32[]{:S(2)}) async-start(bf16[64,1,24]{2,1,0:T(2,128)(2,1)} %copy.156), calls=%async_computation | async-start | bytes 65536 | tf_op jit(solution)/shard_map/all_to_all | solution.py:127
  26.5 3.3 broadcast_in_dim.156
  29.8 3.3 copy.157
  40.9 4.1 broadcast_in_dim.160
  45.0 9.3 %reshape.154 = bf16[64,12,3584]{2,0,1:T(8,128)(2,1)} reshape(bf16[16,4,12,3584]{3,1,0,2:T(4,128)(2,1)} %broadcast_in_dim.160) | data formatting | bytes 11010048 | tf_op jit(solution)/shard_map/reshape | solution.py:43
  54.3 4.0 broadcast_in_dim.157
  58.3 9.3 %reshape.153 = bf16[64,12,3584]{2,0,1:T(8,128)(2,1)} reshape(bf16[16,4,12,3584]{3,1,0,2:T(4,128)(2,1)} %broadcast_in_dim.157) | data formatting | bytes 11010048 | tf_op jit(solution)/shard_map/reshape | solution.py:43
  67.6 5.9 pad_maximum_fusion
  73.5 17.5 %copy.159 = bf16[64,24,3584]{2,1,0:T(8,128)(2,1)} copy(bf16[64,24,3584]{2,0,1:T(8,128)(2,1)S(1)} %pad_maximum_fusion) | data formatting | bytes 22020096 | tf_op jit(solution)/shard_map/concatenate | solution.py:73
  91.6 11.0 %all-to-all-start.1 = ((bf16[64,24,3584]{2,1,0:T(8,128)(2,1)}), bf16[64,24,3584]{2,1,0:T(8,128)(2,1)}, u32[]{:S(2)}, u32[]{:S(2)}) async-start(bf16[64,24,3584]{2,1,0:T(8,128)(2,1)} %copy.159), calls=%async_computation.1 | async-start | bytes 22020096 | tf_op jit(solution)/shard_map/all_to_all | solution.py:126
  106.7 234.0 %all-to-all-done.1 = bf16[64,24,3584]{2,1,0:T(8,128)(2,1)} async-done(((bf16[64,24,3584]{2,1,0:T(8,128)(2,1)}), bf16[64,24,3584]{2,1,0:T(8,128)(2,1)}, u32[]{:S(2)}, u32[]{:S(2)}) %all-to-all-start.1) | async-done | bytes 11010080 | tf_op jit(solution)/shard_map/all_to_all | solution.py:126
  340.6 8.8 %multiply_reduce_fusion = (bf16[1536]{0:T(1024)(128)(2,1)S(1)}, bf16[1536,256]{0,1:T(8,128)(2,1)S(1)}, bf16[1536,256]{0,1:T(8,128)(2,1)}) fusion(bf16[1536,256]{0,1:T(8,128)(2,1)} %copy.172, bf16[1536,256]{0,1:T(8,128)(2,1)S(1)} %copy.173, f32[1536]{0:T(1024)S(1)} %reshape.176, bf16[1536,3584]{1,0:T(8,128)(2,1)} %bitcast.5, ...), kind=kOutput, calls=%fused_computation.32 | convolution fusion | flops 2826041856 | bytes 16000000 | tf_op jit(solution)/shard_map/dot_general | solution.py:48
  350.1 13.5 %all-to-all-start.3 = ((bf16[64,1,24]{2,1,0:T(2,128)(2,1)}), bf16[64,1,24]{2,1,0:T(2,128)(2,1)S(1)}, u32[]{:S(2)}, u32[]{:S(2)}) async-start(bf16[64,1,24]{2,1,0:T(2,128)(2,1)} %convert_element_type.94), calls=%async_computation.3 | async-start | bytes 65536 | tf_op jit(solution)/shard_map/all_to_all | solution.py:141
  363.6 10.4 %convolution_convert_fusion = bf16[1536,3584]{1,0:T(8,128)(2,1)} fusion(bf16[1,1,3584,512]{3,2,1,0:T(8,128)(2,1)} %param.16, bf16[1536,256]{0,1:T(8,128)(2,1)} %get-tuple-element.33, bf16[1536,256]{0,1:T(8,128)(2,1)S(1)} %get-tuple-element.32), kind=kOutput, calls=%fused_computation.6 | convolution fusion | flops 5645795328 | bytes 16252928 | tf_op jit(solution)/shard_map/dot_general | solution.py:62
  374.0 11.3 %all-to-all-start.2 = ((bf16[64,24,3584]{2,1,0:T(8,128)(2,1)}), bf16[64,24,3584]{2,1,0:T(8,128)(2,1)}, u32[]{:S(2)}, u32[]{:S(2)}) async-start(bf16[64,24,3584]{2,1,0:T(8,128)(2,1)} %bitcast.50), calls=%async_computation.2 | async-start | bytes 22020096 | tf_op jit(solution)/shard_map/all_to_all | solution.py:140
  389.7 233.6 %all-to-all-done.2 = bf16[64,24,3584]{2,1,0:T(8,128)(2,1)} async-done(((bf16[64,24,3584]{2,1,0:T(8,128)(2,1)}), bf16[64,24,3584]{2,1,0:T(8,128)(2,1)}, u32[]{:S(2)}, u32[]{:S(2)}) %all-to-all-start.2) | async-done | bytes 11010080 | tf_op jit(solution)/shard_map/all_to_all | solution.py:140
  623.3 12.5 %bitcast_reduce_fusion = (bf16[16,12,3584]{2,1,0:T(8,128)(2,1)}, bf16[16,12,3584]{2,1,0:T(8,128)(2,1)}) fusion(bf16[64,24,3584]{2,1,0:T(8,128)(2,1)} %all-to-all-done.2), kind=kLoop, calls=%fused_computation.8 | loop fusion | flops 4128768 | bytes 13762560 | tf_op jit(solution)/shard_map/reduce_sum | solution.py:92
  640.6 3.0 broadcast_select_fusion.1
  646.0 3.2 reduce_sum.130
  649.2 5.6 collective-permute-start
  659.8 3.0 broadcast_select_fusion
  665.2 3.2 reduce_sum.132
  668.4 4.2 collective-permute-start.1
  672.7 8.5 %fusion = bf16[1,1,256,3584]{3,2,1,0:T(8,128)(2,1)} fusion(bf16[1536,3584]{1,0:T(8,128)(2,1)} %bitcast.5, bf16[1536,256]{0,1:T(8,128)(2,1)S(1)} %copy-done.4, f32[1536]{0:T(1024)S(1)} %reshape.176, bf16[1536,256]{0,1:T(8,128)(2,1)S(1)} %copy.173), kind=kOutput, calls=%fused_computation.11 | convolution fusion | flops 2823028736 | bytes 14424064 | tf_op jit(solution)/shard_map/dot_general | solution.py:66
  (112 shorter events, 48.9 us)
Async XLA Ops:
  0.6 340.0 %copy-start = (bf16[1,1,256,3584]{3,2,1,0:T(8,128)(2,1)S(1)}, bf16[1,1,256,3584]{3,2,1,0:T(8,128)(2,1)}, u32[]{:S(2)}) copy-start(bf16[1,1,256,3584]{3,2,1,0:T(8,128)(2,1)} %param.17) | copy-start | bytes 5505028
  3.6 16.5 %copy-start.6 = (s32[128]{0:T(128)}, s32[128]{0:T(128)S(1)}, u32[]{:S(2)}) copy-start(s32[128]{0:T(128)S(1)} %get-tuple-element.30) | copy-start | bytes 1540
  4.9 15.2 %copy-start.8 = (s32[128]{0:T(128)}, s32[128]{0:T(128)S(1)}, u32[]{:S(2)}) copy-start(s32[128]{0:T(128)S(1)} %get-tuple-element.28) | copy-start | bytes 1540
  6.0 85.0 %all-to-all-start = ((bf16[64,1,24]{2,1,0:T(2,128)(2,1)}), bf16[64,1,24]{2,1,0:T(2,128)(2,1)S(1)}, u32[]{:S(2)}, u32[]{:S(2)}) async-start(bf16[64,1,24]{2,1,0:T(2,128)(2,1)} %copy.156), calls=%async_computation | async-start | bytes 65536 | tf_op jit(solution)/shard_map/all_to_all | solution.py:127
  45.0 9.3 %copy-start.2 = (bf16[16,12,3584]{2,0,1:T(8,128)(2,1)S(1)}, bf16[16,12,3584]{2,0,1:T(8,128)(2,1)}, u32[]{:S(2)}) copy-start(bf16[16,12,3584]{2,0,1:T(8,128)(2,1)} %copy.157) | copy-start | bytes 4128772
  91.0 11.6 %copy-start.3 = (bf16[1,2,1,64,12,512]{5,3,4,2,1,0:T(8,128)(2,1)S(1)}, bf16[1,2,1,64,12,512]{5,3,4,2,1,0:T(8,128)(2,1)}, u32[]{:S(2)}) copy-start(bf16[1,2,1,64,12,512]{5,3,4,2,1,0:T(8,128)(2,1)} %param.15) | copy-start | bytes 4718596
  91.0 0.6 copy-start.5
  91.6 249.0 %all-to-all-start.1 = ((bf16[64,24,3584]{2,1,0:T(8,128)(2,1)}), bf16[64,24,3584]{2,1,0:T(8,128)(2,1)}, u32[]{:S(2)}, u32[]{:S(2)}) async-start(bf16[64,24,3584]{2,1,0:T(8,128)(2,1)} %copy.159), calls=%async_computation.1 | async-start | bytes 22020096 | tf_op jit(solution)/shard_map/all_to_all | solution.py:126
  350.1 23.9 %all-to-all-start.3 = ((bf16[64,1,24]{2,1,0:T(2,128)(2,1)}), bf16[64,1,24]{2,1,0:T(2,128)(2,1)S(1)}, u32[]{:S(2)}, u32[]{:S(2)}) async-start(bf16[64,1,24]{2,1,0:T(2,128)(2,1)} %convert_element_type.94), calls=%async_computation.3 | async-start | bytes 65536 | tf_op jit(solution)/shard_map/all_to_all | solution.py:141
  374.0 11.4 %copy-start.12 = (s32[128]{0:T(128)S(1)}, s32[128]{0:T(128)}, u32[]{:S(2)}) copy-start(s32[128]{0:T(128)} %get-tuple-element.27) | copy-start | bytes 1540
  374.0 14.5 %copy-start.9 = (s32[128]{0:T(128)S(1)}, s32[128]{0:T(128)}, u32[]{:S(2)}) copy-start(s32[128]{0:T(128)} %copy-done.8) | copy-start | bytes 1540
  374.0 15.2 %copy-start.7 = (s32[128]{0:T(128)S(1)}, s32[128]{0:T(128)}, u32[]{:S(2)}) copy-start(s32[128]{0:T(128)} %copy-done.6) | copy-start | bytes 1540
  374.0 249.3 %all-to-all-start.2 = ((bf16[64,24,3584]{2,1,0:T(8,128)(2,1)}), bf16[64,24,3584]{2,1,0:T(8,128)(2,1)}, u32[]{:S(2)}, u32[]{:S(2)}) async-start(bf16[64,24,3584]{2,1,0:T(8,128)(2,1)} %bitcast.50), calls=%async_computation.2 | async-start | bytes 22020096 | tf_op jit(solution)/shard_map/all_to_all | solution.py:140
  649.2 33.0 %collective-permute-start = (bf16[64,3584]{1,0:T(8,128)(2,1)}, bf16[64,3584]{1,0:T(8,128)(2,1)}, u32[]{:S(2)}, u32[]{:S(2)}) collective-permute-start(bf16[64,3584]{1,0:T(8,128)(2,1)} %reduce_sum.130), channel_id=1, source_target_pairs={{64,0},{128,64},{192,128},{65,1},{129,65},{193,129},{66,2},{130,66... | collective-permute-start | bytes 1376264 | tf_op jit(solution)/shard_map/ppermute | solution.py:12
  657.4 2.4 copy-start.13
  665.2 7.4 %copy-start.4 = (bf16[1536,256]{0,1:T(8,128)(2,1)S(1)}, bf16[1536,256]{0,1:T(8,128)(2,1)}, u32[]{:S(2)}) copy-start(bf16[1536,256]{0,1:T(8,128)(2,1)} %copy.172) | copy-start | bytes 2359300
  668.4 12.8 %copy-start.11 = (f32[128]{0:T(128)S(1)}, f32[128]{0:T(128)}, u32[]{:S(2)}) copy-start(f32[128]{0:T(128)} %get-tuple-element.23) | copy-start | bytes 1540
  668.4 13.0 %copy-start.10 = (f32[128]{0:T(128)S(1)}, f32[128]{0:T(128)}, u32[]{:S(2)}) copy-start(f32[128]{0:T(128)} %get-tuple-element.25) | copy-start | bytes 1540
  668.4 13.8 %collective-permute-start.1 = (bf16[64,3584]{1,0:T(8,128)(2,1)}, bf16[64,3584]{1,0:T(8,128)(2,1)}, u32[]{:S(2)}, u32[]{:S(2)}) collective-permute-start(bf16[64,3584]{1,0:T(8,128)(2,1)} %reduce_sum.132), channel_id=1, source_target_pairs={{0,64},{64,128},{128,192},{1,65},{65,129},{129,193},{2,66},{66,130... | collective-permute-start | bytes 1376264 | tf_op jit(solution)/shard_map/ppermute | solution.py:12
  672.6 13.2 %copy-start.1 = (bf16[1,1,256,3584]{3,2,1,0:T(8,128)(2,1)S(1)}, bf16[1,1,256,3584]{3,2,1,0:T(8,128)(2,1)}, u32[]{:S(2)}) copy-start(bf16[1,1,256,3584]{3,2,1,0:T(8,128)(2,1)} %param.17) | copy-start | bytes 5505028
where the time goes:
time: 698 us; the launch traced here: 686 us
  waiting for transfers between devices  468 us (67%)
  local copies, waits for them, and re-layouts  90.1 us (13%)
  starting transfers between devices  59.1 us (8%)
  other arithmetic  40.4 us (6%)
  matrix products  27.7 us (4%)
    all_to_all x1, waiting for transfers between devices, shards(): lax.all_to_all(sent_rows, 'expert', split_axis=0, concat_axis=0, tiled=True)  234 us
    all_to_all x1, waiting for transfers between devices, shards(): lax.all_to_all(out_rows, 'expert', split_axis=0, concat_axis=0, tiled=True)  234 us
    reshape x4, local copies, waits for them, and re-layouts, spread(): return widened.reshape((values.shape[0] * SHARE,) + shape_rest)  18.7 us
    broadcast_in_dim x10, local copies, waits for them, and re-layouts, spread(): jnp.broadcast_to(values[:, None], (values.shape[0], SHARE) + shape_rest)  18.6 us
    concatenate x1, local copies, waits for them, and re-layouts, share_out(): rows = jnp.concatenate([spread(item[0]) for item in stretch_packs], axis=1)  17.5 us
  transfers between devices with their start and end apart: 6, of which 2 were waited for; matrix products, arithmetic and copies ran while one was open for 16% of the time, Pallas kernels for 0%

commit v1 on v0

v1 whole, which is shorter than its diff:
```python
import functools

import jax
import jax.numpy as jnp
from jax import lax
from jax.experimental import pallas as pl
from jax.experimental.pallas import tpu as pltpu
from jax.sharding import Mesh, PartitionSpec as P

SHARE = 4
DEPTH = 2 * SHARE
CHUNKS = 4
HALF = 64
LANES = 128
META = 8
VMEM_LIMIT = 48 * 1024 * 1024

f32 = jnp.float32
bf16 = jnp.bfloat16


def shifted(block, distance):
    devices = range(lax.axis_size("section"))
    route = [(i - distance, i) for i in devices if i - distance in devices]
    return lax.ppermute(block, "section", route)


def slot_keys(meta, first, stride, count, capacity):
    ids = (first + stride * lax.broadcasted_iota(jnp.int32, (count, LANES), 0)).astype(f32)
    named = (meta[0:1, :] == ids) | (meta[1:2, :] == ids)
    row = lax.broadcasted_iota(jnp.int32, (LANES, LANES), 0)
    col = lax.broadcasted_iota(jnp.int32, (LANES, LANES), 1)
    earlier = (row < col) & (row // HALF == col // HALF)
    before = lax.dot_general(
        named.astype(f32).astype(bf16),
        earlier.astype(f32).astype(bf16),
        (((1,), (0,)), ((), ())),
        preferred_element_type=f32,
    )
    stretch = lax.broadcasted_iota(jnp.int32, (count, LANES), 1) // HALF
    return jnp.where(named, before + (stretch * capacity).astype(f32), -1.0)


def slot_matrix(meta, first, stride, count, capacity):
    keys = slot_keys(meta, first, stride, count, capacity)
    span = 2 * capacity
    slot = lax.broadcasted_iota(jnp.int32, (count, span, LANES), 1).astype(f32)
    hit = jnp.where(slot == keys[:, None, :], 1.0, 0.0)
    return hit.reshape(count * span, LANES).astype(bf16)


def pack_kernel(capacity, place, meta, rows, out):
    columns = out.shape[0]
    hits = slot_matrix(meta[0, 0], place[1], 2, columns, capacity)
    packed = jnp.dot(hits, rows[0], preferred_element_type=f32)
    out[:, 0] = packed.astype(bf16).reshape(columns, 2 * capacity, rows.shape[2])


def pack(place, meta, rows, columns, capacity):
    depth, tokens, width = rows.shape
    span = 2 * capacity
    return pl.pallas_call(
        functools.partial(pack_kernel, capacity),
        out_shape=jax.ShapeDtypeStruct((columns, depth, span, width), bf16),
        grid_spec=pltpu.PrefetchScalarGridSpec(
            num_scalar_prefetch=1,
            grid=(depth,),
            in_specs=[
                pl.BlockSpec((1, 1, META, LANES), lambda z, place: (place[0], z, 0, 0)),
                pl.BlockSpec((1, tokens, width), lambda z, place: (z, 0, 0)),
            ],
            out_specs=pl.BlockSpec((columns, 1, span, width), lambda z, place: (0, z, 0, 0)),
        ),
        compiler_params=pltpu.CompilerParams(vmem_limit_bytes=VMEM_LIMIT),
        name="pack_rows",
    )(place, meta, rows)


def fold_kernel(capacity, place, meta, rows, out):
    columns = rows.shape[0]
    hits = slot_matrix(meta[0, 0], place[1], 2, columns, capacity)
    flat = rows[:, 0].reshape(columns * 2 * capacity, rows.shape[3])
    total = lax.dot_general(hits, flat, (((0,), (0,)), ((), ())), preferred_element_type=f32)
    out[0] = total.astype(bf16)


def fold(place, meta, rows, capacity):
    columns, depth, span, width = rows.shape
    return pl.pallas_call(
        functools.partial(fold_kernel, capacity),
        out_shape=jax.ShapeDtypeStruct((depth, LANES, width), bf16),
        grid_spec=pltpu.PrefetchScalarGridSpec(
            num_scalar_prefetch=1,
            grid=(depth,),
            in_specs=[
                pl.BlockSpec((1, 1, META, LANES), lambda z, place: (place[0], z, 0, 0)),
                pl.BlockSpec((columns, 1, span, width), lambda z, place: (0, z, 0, 0)),
            ],
            out_specs=pl.BlockSpec((1, LANES, width), lambda z, place: (z, 0, 0)),
        ),
        compiler_params=pltpu.CompilerParams(vmem_limit_bytes=VMEM_LIMIT),
        name="fold_rows",
    )(place, meta, rows)


def weights_kernel(capacity, place, meta, preacts, scaled, gate_fac, up_fac, hidden):
    depth = meta.shape[1]
    span = 2 * capacity
    width = hidden.shape[1]
    columns = []
    for z in range(depth):
        block = meta[0, z]
        keys = slot_keys(block, place[2], 0, 8, capacity)[0:1]
        own = place[2].astype(f32)
        gates = jnp.where(block[0:1] == own, block[2:3], 0.0) + jnp.where(block[1:2] == own, block[3:4], 0.0)
        slot = lax.broadcasted_iota(jnp.int32, (span, LANES), 0).astype(f32)
        columns.append(jnp.sum(jnp.where(slot == keys, gates, 0.0), axis=1, keepdims=True))
    scale = jnp.concatenate(columns, axis=0)
    gate_pre = preacts[:, :width].astype(f32)
    up_pre = preacts[:, width:].astype(f32)
    sig = 1.0 / (1.0 + jnp.exp(-gate_pre))
    act = gate_pre * sig
    both = act * up_pre
    hidden[...] = both
    scaled[...] = (scale * both).astype(bf16)
    gate_fac[...] = scale * (up_pre * sig * (1.0 + gate_pre * (1.0 - sig)))
    up_fac[...] = scale * act


def slot_weights(place, meta, preacts, capacity):
    columns, depth = meta.shape[:2]
    rows = depth * 2 * capacity
    total, both = preacts.shape
    width = both // 2
    block = pl.BlockSpec((rows, width), lambda i, place: (i, 0))
    shape = functools.partial(jax.ShapeDtypeStruct, (total, width))
    return pl.pallas_call(
        functools.partial(weights_kernel, capacity),
        out_shape=[shape(bf16), shape(f32), shape(f32), shape(f32)],
        grid_spec=pltpu.PrefetchScalarGridSpec(
            num_scalar_prefetch=1,
            grid=(columns,),
            in_specs=[
                pl.BlockSpec((1, depth, META, LANES), lambda i, place: (i, 0, 0, 0)),
                pl.BlockSpec((rows, both), lambda i, place: (i, 0)),
            ],
            out_specs=[block] * 4,
        ),
        compiler_params=pltpu.CompilerParams(vmem_limit_bytes=VMEM_LIMIT),
        name="slot_weights",
    )(place, meta, preacts)


def shards(grad_out, gate_probs, routes, saved_preacts, w_gate_up, w_down):
    columns = lax.axis_size("column")
    depth = lax.axis_size("depth")
    capacity = saved_preacts.shape[4]
    span = 2 * capacity
    sources = columns * depth
    width = grad_out.shape[3]
    tokens = grad_out.shape[2]
    step = width // CHUNKS
    column = lax.axis_index("column")
    level = lax.axis_index("depth")
    half = level // SHARE
    own = 2 * column + half
    place = jnp.stack([column, half, own]).astype(jnp.int32)
    gate_up = w_gate_up[0, 0]
    down_proj = w_down[0, 0]

    picks = jnp.moveaxis(routes[0], 2, 0).reshape(2, 2 * tokens).astype(f32)
    gates = jnp.moveaxis(gate_probs[0], 2, 0).reshape(2, 2 * tokens).astype(f32)
    own_meta = jnp.concatenate([picks, gates, jnp.zeros((META - 4, 2 * tokens), f32)])
    meta = lax.all_gather(own_meta, ("column", "depth"), axis=0, tiled=False)
    meta = meta.reshape(columns, depth, META, LANES)

    rows_in = grad_out[0].reshape(2 * tokens, width)
    got = []
    back = None
    for c in range(CHUNKS):
        part = rows_in[:, c * step : (c + 1) * step]
        gathered = lax.all_gather(part, "depth", axis=0, tiled=False)
        sent = pack(place, meta, gathered, columns, capacity)
        got.append(
            lax.all_to_all(sent, "column", split_axis=0, concat_axis=0, tiled=True).reshape(
                sources * span, step
            )
        )
    preacts = jnp.concatenate([saved_preacts[0, 0, 0], saved_preacts[0, 1, 0]], axis=1)
    scaled, gate_fac, up_fac, hidden = slot_weights(
        place, meta, preacts.reshape(sources * span, -1), capacity
    )
    for c in range(CHUNKS):
        piece = lax.dot_general(
            got[c],
            down_proj[:, c * step : (c + 1) * step],
            (((1,), (1,)), ((), ())),
            preferred_element_type=f32,
        )
        back = piece if back is None else back + piece
    prob_part = jnp.sum(hidden * back, axis=1).astype(bf16)
    d_both = jnp.concatenate([back * gate_fac, back * up_fac], axis=1).astype(bf16)

    above, below, down_parts = [], [], []
    for c in range(CHUNKS):
        part = lax.dot_general(
            d_both,
            gate_up[c * step : (c + 1) * step],
            (((1,), (1,)), ((), ())),
            preferred_element_type=f32,
        ).astype(bf16)
        returned = lax.all_to_all(
            part.reshape(columns, depth, span, step), "column", split_axis=0, concat_axis=0, tiled=True
        )
        folded = fold(place, meta, returned, capacity)
        token_grad = lax.psum_scatter(folded, "depth", scatter_dimension=0, tiled=False)
        above.append(shifted(token_grad[:tokens], -1))
        below.append(shifted(token_grad[tokens:], 1))
    for c in range(CHUNKS):
        down_parts.append(
            lax.dot_general(
                scaled, got[c], (((0,), (0,)), ((), ())), preferred_element_type=f32
            ).astype(bf16)
        )

    prob_all = lax.all_gather(
        jnp.pad(prob_part, (0, 2048 - sources * span)).reshape(16, LANES), ("column", "depth"), axis=0, tiled=False
    ).reshape(sources, 2048)
    mine = lax.dynamic_slice(prob_all, (0, (column * depth + level) * span), (sources, span))
    group_prob = mine.astype(f32).reshape(sources // SHARE, SHARE, span).sum(axis=1)
    group_prob = lax.optimization_barrier(group_prob.astype(bf16)).astype(f32)
    keys = slot_keys(own_meta, 0, 1, sources // SHARE, capacity)
    slot = jnp.arange(span, dtype=jnp.int32).astype(f32)
    by_expert = jnp.sum(
        jnp.where(keys[:, None, :] == slot[None, :, None], group_prob[:, :, None], 0.0), axis=1
    )
    expert = jnp.arange(sources // SHARE, dtype=jnp.int32).astype(f32)
    prob_grad = jnp.sum(
        jnp.where(picks[:, None, :] == expert[None, :, None], by_expert[None], 0.0), axis=1
    )
    prob_grad = jnp.moveaxis(prob_grad.reshape(2, 2, tokens), 0, 2)
    return (
        jnp.concatenate(above, axis=1)[None],
        jnp.concatenate(below, axis=1)[None],
        prob_grad[None],
        jnp.concatenate(down_parts, axis=1)[None, None],
    )


def solution(mesh):
    sections, slices = mesh.devices.shape
    grid = Mesh(mesh.devices.reshape(sections, slices // DEPTH, DEPTH), ("section", "column", "depth"))
    spread = ("column", "depth")
    in_specs = (
        P("section", None, spread, None),
        P("section", None, spread, None),
        P("section", None, spread, None),
        P("section", None, spread, None, None, None),
        P("section", spread, None, None),
        P("section", spread, None, None),
    )
    out_specs = (
        P("section", spread, None),
        P("section", spread, None),
        P("section", None, spread, None),
        P("section", spread, None, None),
    )
    return jax.shard_map(shards, mesh=grid, in_specs=in_specs, out_specs=out_specs, check_vma=False)
```

time: 698 us -> 691 us (0.990); the launches traced: 686 us -> 690 us
  blocking collectives: 0 us -> 391 us
  waiting for transfers between devices: 468 us -> 107 us
  local copies, waits for them, and re-layouts: 90.1 us -> 18.6 us
  Pallas kernels: 0 us -> 50 us
  other arithmetic: 40.4 us -> 4.89 us
  between operations: 1.52 us -> 14.6 us
  starting transfers between devices: 59.1 us -> 70.8 us
    all_to_all x4, waiting for transfers between devices: 468 us -> 30.2 us  [shards(): lax.all_to_all(sent, 'column', split_axis=0, concat_axis=0, tiled=True)]
    all_gather x0 -> x2, blocking collectives: none -> 273 us  [the longest x1 140 us: shards(): lax.all_gather(jnp.pad(prob_part, (0, 2048 - sources * span)).reshape(16,...]
    all_to_all x0 -> x4, blocking collectives: none -> 118 us  [shards(): lax.all_to_all(part.reshape(columns, depth, span, step), 'column', split_...]
    all_gather x0 -> x4, waiting for transfers between devices: none -> 70.1 us  [shards(): gathered = lax.all_gather(part, 'depth', axis=0, tiled=False)]
    pallas_call x0 -> x9, Pallas kernels: none -> 50 us  [the longest x4 22.2 us: fold(): pl.pallas_call(functools.partial(fold_kernel, capacity), out_shape=jax.Sh...]
    ppermute x2 -> x8, starting transfers between devices: 9.78 us -> 52.4 us  [shifted(): return lax.ppermute(block, 'section', route)]
    all_to_all x4, starting transfers between devices: 49.3 us -> 18 us  [shards(): lax.all_to_all(sent, 'column', split_axis=0, concat_axis=0, tiled=True)]
    reshape x10 -> x1, local copies, waits for them, and re-layouts: 28.7 us -> 0.08 us  [shards(): prob_grad = jnp.moveaxis(prob_grad.reshape(2, 2, tokens), 0, 2)]
  transfers between devices with their start and end apart: 6 -> 20, of which waited for: 2 -> 7; matrix products, arithmetic and copies ran while one was open for 16% -> 5% of each run, Pallas kernels for 0% -> 6%
where the time goes in v1:
time: 691 us; the launch traced here: 690 us
  blocking collectives  391 us (57%)
  waiting for transfers between devices  107 us (15%)
  starting transfers between devices  70.8 us (10%)
  Pallas kernels  50 us (7%)
  matrix products  32.6 us (5%)
  local copies, waits for them, and re-layouts  18.6 us (3%)
  between operations  14.6 us (2%)
    all_gather x1, blocking collectives, shards(): lax.all_gather(jnp.pad(prob_part, (0, 2048 - sources * span)).reshape(16,...  140 us
    all_gather x1, blocking collectives, shards(): meta = lax.all_gather(own_meta, ('column', 'depth'), axis=0, tiled=False)  133 us
    all_to_all x4, blocking collectives, shards(): lax.all_to_all(part.reshape(columns, depth, span, step), 'column', split_...  118 us
    all_gather x4, waiting for transfers between devices, shards(): gathered = lax.all_gather(part, 'depth', axis=0, tiled=False)  70.1 us
    ppermute x8, starting transfers between devices, shifted(): return lax.ppermute(block, 'section', route)  52.4 us
    all_to_all x4, waiting for transfers between devices, shards(): lax.all_to_all(sent, 'column', split_axis=0, concat_axis=0, tiled=True)  30.2 us
    pallas_call x4, Pallas kernels, fold(): pl.pallas_call(functools.partial(fold_kernel, capacity), out_shape=jax.Sh...  22.2 us
    pallas_call x4, Pallas kernels, pack(): pl.pallas_call(functools.partial(pack_kernel, capacity), out_shape=jax.Sh...  21.8 us
  transfers between devices with their start and end apart: 20, of which 7 were waited for; matrix products, arithmetic and copies ran while one was open for 5% of the time, Pallas kernels for 6%

profile of v1, /device:TPU:1, one launch (start us, length us, event | category | flops | bytes accessed | tf_op | source)
XLA Modules:
  0.0 689.7 jit_solution(15248800977539968107)
XLA Ops:
  12.0 133.2 %all-gather = f32[512,128]{1,0:T(8,128)S(1)} all-gather(f32[8,128]{1,0:T(8,128)S(1)} %maximum_maximum_fusion), channel_id=2, replica_groups=mesh['section'=4,'column'=8,'depth'=8] {'column','depth'}, dimensions={0}, use_global_device_ids=true | all-gather | bytes 266240 | tf_op jit(solution)/shard_map/all_gather | solution.py:174
  146.7 5.4 pack_rows.4
  158.1 5.4 pack_rows.5
  163.5 12.1 %all-to-all-done = bf16[8,8,24,896]{3,2,1,0:T(8,128)(2,1)S(1)} async-done(((bf16[8,8,24,896]{3,2,1,0:T(8,128)(2,1)}), bf16[8,8,24,896]{3,2,1,0:T(8,128)(2,1)S(1)}, u32[]{:S(2)}, u32[]{:S(2)}) %all-to-all-start) | async-done | bytes 2752544 | tf_op jit(solution)/shard_map/all_to_all | solution.py:185
  177.1 4.5 all-to-all-start.1
  182.2 40.5 %all-gather.14.cloned.1.call-done = bf16[1024,896]{1,0:T(8,128)(2,1)} async-done(((bf16[128,896]{1,0:T(8,128)(2,1)}), bf16[1024,896]{1,0:T(8,128)(2,1)}) %all-gather.14.cloned.1.call-update) | async-done | bytes 1835024 | tf_op jit(solution)/shard_map/all_gather | solution.py:182
  224.2 5.4 pack_rows.6
  229.7 4.8 all-to-all-start.2
  234.5 29.6 %all-gather.16.cloned.1.call-done = bf16[1024,896]{1,0:T(8,128)(2,1)} async-done(((bf16[128,896]{1,0:T(8,128)(2,1)}), bf16[1024,896]{1,0:T(8,128)(2,1)}) %all-gather.16.cloned.1.call-update) | async-done | bytes 1835024 | tf_op jit(solution)/shard_map/all_gather | solution.py:182
  265.6 5.5 pack_rows.7
  271.1 5.0 all-to-all-start.3
  278.4 6.1 slot_weights.1
  292.1 18.1 %all-to-all-done.3 = bf16[8,8,24,896]{3,2,1,0:T(8,128)(2,1)} async-done(((bf16[8,8,24,896]{3,2,1,0:T(8,128)(2,1)}), bf16[8,8,24,896]{3,2,1,0:T(8,128)(2,1)}, u32[]{:S(2)}, u32[]{:S(2)}) %all-to-all-start.3) | async-done | bytes 2752544 | tf_op jit(solution)/shard_map/all_to_all | solution.py:185
  310.2 4.1 multiply_reduce_fusion
  318.0 30.6 %all_to_all.40.rows = bf16[8,8,24,896]{3,2,1,0:T(8,128)(2,1)S(1)} all-to-all(bf16[8,8,24,896]{3,2,1,0:T(8,128)(2,1)S(1)} %bitcast.107), channel_id=1, replica_groups=mesh['section'=4,'column'=8,'depth'=8] {'column'}, dimensions={0} | all-to-all | bytes 5505024 | tf_op jit(solution)/shard_map/all_to_all | solution.py:212
  348.6 5.6 fold_rows.5
  357.3 30.1 %all_to_all.41.rows = bf16[8,8,24,896]{3,2,1,0:T(8,128)(2,1)S(1)} all-to-all(bf16[8,8,24,896]{3,2,1,0:T(8,128)(2,1)S(1)} %bitcast.108), channel_id=1, replica_groups=mesh['section'=4,'column'=8,'depth'=8] {'column'}, dimensions={0} | all-to-all | bytes 5505024 | tf_op jit(solution)/shard_map/all_to_all | solution.py:212
  387.4 5.6 fold_rows.6
  396.3 29.0 %all_to_all.42.rows = bf16[8,8,24,896]{3,2,1,0:T(8,128)(2,1)S(1)} all-to-all(bf16[8,8,24,896]{3,2,1,0:T(8,128)(2,1)S(1)} %bitcast.109), channel_id=1, replica_groups=mesh['section'=4,'column'=8,'depth'=8] {'column'}, dimensions={0} | all-to-all | bytes 5505024 | tf_op jit(solution)/shard_map/all_to_all | solution.py:212
  425.3 5.5 fold_rows.7
  434.0 27.8 %all_to_all.43.rows = bf16[8,8,24,896]{3,2,1,0:T(8,128)(2,1)S(1)} all-to-all(bf16[8,8,24,896]{3,2,1,0:T(8,128)(2,1)S(1)} %bitcast.106), channel_id=1, replica_groups=mesh['section'=4,'column'=8,'depth'=8] {'column'}, dimensions={0} | all-to-all | bytes 5505024 | tf_op jit(solution)/shard_map/all_to_all | solution.py:212
  461.8 5.5 fold_rows.4
  467.8 140.1 %all_gather.43 = bf16[64,16,128]{2,1,0:T(8,128)(2,1)S(1)} all-gather(bf16[1,16,128]{2,1,0:T(8,128)(2,1)S(1)} %pad_bitcast_fusion), channel_id=1, replica_groups=mesh['section'=4,'column'=8,'depth'=8] {'column','depth'}, dimensions={0}, use_global_device_ids=true | all-gather | bytes 266240 | tf_op jit(solution)/shard_map/all_gather | solution.py:226
  620.0 38.4 %collective-permute-start.5 = (bf16[64,896]{1,0:T(8,128)(2,1)S(1)}, bf16[64,896]{1,0:T(8,128)(2,1)S(1)}, u32[]{:S(2)}, u32[]{:S(2)}) collective-permute-start(bf16[64,896]{1,0:T(8,128)(2,1)S(1)} %get-tuple-element.37), channel_id=1, source_target_pairs={{0,64},{64,128},{128,192},{1,65},{65,129},{129,193},{2,66},{66,130... | collective-permute-start | bytes 344072 | tf_op jit(solution)/shard_map/ppermute | solution.py:25
  (125 shorter events, 77.0 us)
Async XLA Ops:
  7.2 138.1 %all-gather.10.cloned.1.call-start = ((), (), s32[]{:S(2)}) async-start(), calls=%async_computation.16 | async-start | bytes 2064384 | tf_op jit(solution)/shard_map/all_gather | solution.py:182
  9.5 147.1 %all-gather.12.cloned.1.call-start = ((), (), s32[]{:S(2)}) async-start(), calls=%async_computation.17 | async-start | bytes 2064384 | tf_op jit(solution)/shard_map/all_gather | solution.py:182
  152.2 23.4 %all-to-all-start = ((bf16[8,8,24,896]{3,2,1,0:T(8,128)(2,1)}), bf16[8,8,24,896]{3,2,1,0:T(8,128)(2,1)S(1)}, u32[]{:S(2)}, u32[]{:S(2)}) async-start(bf16[8,8,24,896]{3,2,1,0:T(8,128)(2,1)} %pack_rows.4), calls=%async_computation | async-start | bytes 5505024 | tf_op jit(solution)/shard_map/all_to_all | solution.py:185
  155.8 66.9 %all-gather.14.cloned.1.call-start = ((), (), s32[]{:S(2)}) async-start(), calls=%async_computation.18 | async-start | bytes 2064384 | tf_op jit(solution)/shard_map/all_gather | solution.py:182
  177.1 52.5 %all-to-all-start.1 = ((bf16[8,8,24,896]{3,2,1,0:T(8,128)(2,1)}), bf16[8,8,24,896]{3,2,1,0:T(8,128)(2,1)S(1)}, u32[]{:S(2)}, u32[]{:S(2)}) async-start(bf16[8,8,24,896]{3,2,1,0:T(8,128)(2,1)} %pack_rows.5), calls=%async_computation.1 | async-start | bytes 5505024 | tf_op jit(solution)/shard_map/all_to_all | solution.py:185
  181.6 82.4 %all-gather.16.cloned.1.call-start = ((), (), s32[]{:S(2)}) async-start(), calls=%async_computation.19 | async-start | bytes 2064384 | tf_op jit(solution)/shard_map/all_gather | solution.py:182
  229.7 34.4 %copy-start.7 = (bf16[8,8,24,896]{3,2,1,0:T(8,128)(2,1)}, bf16[8,8,24,896]{3,2,1,0:T(8,128)(2,1)S(1)}, u32[]{:S(2)}) copy-start(bf16[8,8,24,896]{3,2,1,0:T(8,128)(2,1)S(1)} %all-to-all-done.1) | copy-start | bytes 8257540
  229.7 41.4 %all-to-all-start.2 = ((bf16[8,8,24,896]{3,2,1,0:T(8,128)(2,1)}), bf16[8,8,24,896]{3,2,1,0:T(8,128)(2,1)}, u32[]{:S(2)}, u32[]{:S(2)}) async-start(bf16[8,8,24,896]{3,2,1,0:T(8,128)(2,1)} %pack_rows.6), calls=%async_computation.2 | async-start | bytes 5505024 | tf_op jit(solution)/shard_map/all_to_all | solution.py:185
  271.1 39.1 %all-to-all-start.3 = ((bf16[8,8,24,896]{3,2,1,0:T(8,128)(2,1)}), bf16[8,8,24,896]{3,2,1,0:T(8,128)(2,1)}, u32[]{:S(2)}, u32[]{:S(2)}) async-start(bf16[8,8,24,896]{3,2,1,0:T(8,128)(2,1)} %pack_rows.7), calls=%async_computation.3 | async-start | bytes 5505024 | tf_op jit(solution)/shard_map/all_to_all | solution.py:185
  276.1 343.0 %reduce-scatter.7.cloned.1.call-start = ((), (), s32[]{:S(2)}) async-start(), calls=%async_computation.13 | async-start | bytes 2064384 | tf_op jit(solution)/shard_map/reduce_scatter | solution.py:216
  276.4 8.1 %copy-start.10 = (bf16[8,8,24,896]{3,2,1,0:T(8,128)(2,1)S(1)}, bf16[8,8,24,896]{3,2,1,0:T(8,128)(2,1)}, u32[]{:S(2)}) copy-start(bf16[8,8,24,896]{3,2,1,0:T(8,128)(2,1)} %copy-done.9) | copy-start | bytes 8257540
  276.4 8.1 %copy-start.12 = (bf16[1,1,256,3584]{3,2,1,0:T(8,128)(2,1)S(1)}, bf16[1,1,256,3584]{3,2,1,0:T(8,128)(2,1)}, u32[]{:S(2)}) copy-start(bf16[1,1,256,3584]{3,2,1,0:T(8,128)(2,1)} %param.11) | copy-start | bytes 5505028
  354.2 304.3 %reduce-scatter.9.cloned.1.call-start = ((), (), s32[]{:S(2)}) async-start(), calls=%async_computation.14 | async-start | bytes 2064384 | tf_op jit(solution)/shard_map/reduce_scatter | solution.py:216
  393.0 268.4 %reduce-scatter.11.cloned.1.call-start = ((), (), s32[]{:S(2)}) async-start(), calls=%async_computation.15 | async-start | bytes 2064384 | tf_op jit(solution)/shard_map/reduce_scatter | solution.py:216
  430.9 233.5 %reduce-scatter.5.cloned.1.call-start = ((), (), s32[]{:S(2)}) async-start(), calls=%async_computation.12 | async-start | bytes 2064384 | tf_op jit(solution)/shard_map/reduce_scatter | solution.py:216
  461.8 146.4 %copy-start.6 = (bf16[1536,256]{1,0:T(8,128)(2,1)S(1)}, bf16[1536,256]{1,0:T(8,128)(2,1)}, u32[]{:S(2)}) copy-start(bf16[1536,256]{1,0:T(8,128)(2,1)} %copy-done.5) | copy-start | bytes 2359300
  620.0 50.5 %collective-permute-start.5 = (bf16[64,896]{1,0:T(8,128)(2,1)S(1)}, bf16[64,896]{1,0:T(8,128)(2,1)S(1)}, u32[]{:S(2)}, u32[]{:S(2)}) collective-permute-start(bf16[64,896]{1,0:T(8,128)(2,1)S(1)} %get-tuple-element.37), channel_id=1, source_target_pairs={{0,64},{64,128},{128,192},{1,65},{65,129},{129,193},{2,66},{66,130... | collective-permute-start | bytes 344072 | tf_op jit(solution)/shard_map/ppermute | solution.py:25
  659.5 13.0 %collective-permute-start.6 = (bf16[64,896]{1,0:T(8,128)(2,1)S(1)}, bf16[64,896]{1,0:T(8,128)(2,1)S(1)}, u32[]{:S(2)}, u32[]{:S(2)}) collective-permute-start(bf16[64,896]{1,0:T(8,128)(2,1)S(1)} %get-tuple-element.39), channel_id=1, source_target_pairs={{0,64},{64,128},{128,192},{1,65},{65,129},{129,193},{2,66},{66,130... | collective-permute-start | bytes 344072 | tf_op jit(solution)/shard_map/ppermute | solution.py:25
  662.4 12.0 %collective-permute-start.7 = (bf16[64,896]{1,0:T(8,128)(2,1)S(1)}, bf16[64,896]{1,0:T(8,128)(2,1)S(1)}, u32[]{:S(2)}, u32[]{:S(2)}) collective-permute-start(bf16[64,896]{1,0:T(8,128)(2,1)S(1)} %get-tuple-element.41), channel_id=1, source_target_pairs={{0,64},{64,128},{128,192},{1,65},{65,129},{129,193},{2,66},{66,130... | collective-permute-start | bytes 344072 | tf_op jit(solution)/shard_map/ppermute | solution.py:25
  665.3 11.0 %collective-permute-start.4 = (bf16[64,896]{1,0:T(8,128)(2,1)S(1)}, bf16[64,896]{1,0:T(8,128)(2,1)S(1)}, u32[]{:S(2)}, u32[]{:S(2)}) collective-permute-start(bf16[64,896]{1,0:T(8,128)(2,1)S(1)} %get-tuple-element.35), channel_id=1, source_target_pairs={{0,64},{64,128},{128,192},{1,65},{65,129},{129,193},{2,66},{66,130... | collective-permute-start | bytes 344072 | tf_op jit(solution)/shard_map/ppermute | solution.py:25
  668.2 9.0 %collective-permute-start.1 = (bf16[64,896]{1,0:T(8,128)(2,1)S(1)}, bf16[64,896]{1,0:T(8,128)(2,1)S(1)}, u32[]{:S(2)}, u32[]{:S(2)}) collective-permute-start(bf16[64,896]{1,0:T(8,128)(2,1)S(1)} %get-tuple-element.38), channel_id=1, source_target_pairs={{64,0},{128,64},{192,128},{65,1},{129,65},{193,129},{66,2},{130,66... | collective-permute-start | bytes 344072 | tf_op jit(solution)/shard_map/ppermute | solution.py:25
  670.6 7.6 %collective-permute-start.2 = (bf16[64,896]{1,0:T(8,128)(2,1)S(1)}, bf16[64,896]{1,0:T(8,128)(2,1)S(1)}, u32[]{:S(2)}, u32[]{:S(2)}) collective-permute-start(bf16[64,896]{1,0:T(8,128)(2,1)S(1)} %get-tuple-element.40), channel_id=1, source_target_pairs={{64,0},{128,64},{192,128},{65,1},{129,65},{193,129},{66,2},{130,66... | collective-permute-start | bytes 344072 | tf_op jit(solution)/shard_map/ppermute | solution.py:25
  672.5 7.6 %collective-permute-start.3 = (bf16[64,896]{1,0:T(8,128)(2,1)S(1)}, bf16[64,896]{1,0:T(8,128)(2,1)S(1)}, u32[]{:S(2)}, u32[]{:S(2)}) collective-permute-start(bf16[64,896]{1,0:T(8,128)(2,1)S(1)} %get-tuple-element.42), channel_id=1, source_target_pairs={{64,0},{128,64},{192,128},{65,1},{129,65},{193,129},{66,2},{130,66... | collective-permute-start | bytes 344072 | tf_op jit(solution)/shard_map/ppermute | solution.py:25
  674.5 7.6 %collective-permute-start = (bf16[64,896]{1,0:T(8,128)(2,1)S(1)}, bf16[64,896]{1,0:T(8,128)(2,1)S(1)}, u32[]{:S(2)}, u32[]{:S(2)}) collective-permute-start(bf16[64,896]{1,0:T(8,128)(2,1)S(1)} %get-tuple-element.36), channel_id=1, source_target_pairs={{64,0},{128,64},{192,128},{65,1},{129,65},{193,129},{66,2},{130,66... | collective-permute-start | bytes 344072 | tf_op jit(solution)/shard_map/ppermute | solution.py:25
  (14 other events, 39.3 us)
Sparse Core Ops, SparseCore 0:
  9.8 40.9 all-gather.9
  53.1 38.5 all-gather.11
  159.0 63.6 all-gather.13
  224.9 39.0 all-gather.15
  354.3 40.2 reduce-scatter.6
  397.0 41.8 reduce-scatter.8
  441.4 40.6 reduce-scatter.10
  484.7 39.8 reduce-scatter.4

commit v2 on v1

v2 whole, which is shorter than its diff:
```python
import functools

import jax
import jax.numpy as jnp
from jax import lax
from jax.experimental import pallas as pl
from jax.experimental.pallas import tpu as pltpu
from jax.sharding import Mesh, PartitionSpec as P

SHARE = 4
DEPTH = 2 * SHARE
WIDTHS = (512, 1024, 1024, 1024)
EXTRA = 128
HALF = 64
LANES = 128
META = 16
VMEM_LIMIT = 48 * 1024 * 1024

f32 = jnp.float32
bf16 = jnp.bfloat16


def shifted(block, distance):
    devices = range(lax.axis_size("section"))
    route = [(i - distance, i) for i in devices if i - distance in devices]
    return lax.ppermute(block, "section", route)


def slot_hits(meta, first, stride, count, capacity):
    ids = (first + stride * lax.broadcasted_iota(jnp.int32, (count, LANES), 0)).astype(f32)
    named = (meta[0:1] == ids) | (meta[1:2] == ids)
    row = lax.broadcasted_iota(jnp.int32, (LANES, LANES), 0)
    col = lax.broadcasted_iota(jnp.int32, (LANES, LANES), 1)
    earlier = (row < col) & (row // HALF == col // HALF)
    before = lax.dot_general(
        named.astype(f32).astype(bf16),
        earlier.astype(f32).astype(bf16),
        (((1,), (0,)), ((), ())),
        preferred_element_type=f32,
    )
    stretch = lax.broadcasted_iota(jnp.int32, (count, LANES), 1) // HALF
    keys = jnp.where(named, before + (stretch * capacity).astype(f32), -1.0)
    slot = lax.broadcasted_iota(jnp.int32, (count, 2 * capacity, LANES), 1).astype(f32)
    return jnp.where(slot == keys[:, None, :], 1.0, 0.0), ids


def flat(hits):
    return hits.reshape(-1, LANES).astype(bf16)


def pack_kernel(capacity, width, place, meta_rows, rows, out):
    columns = out.shape[0]
    meta = meta_rows[0].astype(f32)
    hits, ids = slot_hits(meta, place[0], 2, columns, capacity)
    packed = jnp.dot(flat(hits), rows[0, :LANES], preferred_element_type=f32)
    out[:, 0, :, :width] = packed.astype(bf16).reshape(columns, 2 * capacity, width)
    if out.shape[3] > width:
        gates = jnp.where(meta[0:1] == ids, meta[2:3], 0.0) + jnp.where(meta[1:2] == ids, meta[3:4], 0.0)
        scale = jnp.sum(hits * gates[:, None, :], axis=2, keepdims=True)
        out[:, 0, :, width:] = jnp.broadcast_to(scale, (columns, 2 * capacity, EXTRA)).astype(bf16)


def pack(place, tagged, rows, columns, capacity, extra):
    depth, tokens, width = rows.shape
    span = 2 * capacity
    return pl.pallas_call(
        functools.partial(pack_kernel, capacity, width),
        out_shape=jax.ShapeDtypeStruct((columns, depth, span, width + extra), bf16),
        grid_spec=pltpu.PrefetchScalarGridSpec(
            num_scalar_prefetch=1,
            grid=(depth,),
            in_specs=[
                pl.BlockSpec((1, META, LANES), lambda z, place: (z, LANES // META, 0)),
                pl.BlockSpec((1, tokens, width), lambda z, place: (z, 0, 0)),
            ],
            out_specs=pl.BlockSpec((columns, 1, span, width + extra), lambda z, place: (0, z, 0, 0)),
        ),
        compiler_params=pltpu.CompilerParams(vmem_limit_bytes=VMEM_LIMIT),
        name="pack_rows",
    )(place, tagged, rows)


def fold_kernel(capacity, width, place, meta_rows, rows, *rest):
    out = rest[-1]
    columns = rows.shape[0]
    meta = meta_rows[0].astype(f32)
    hits, ids = slot_hits(meta, place[0], 2, columns, capacity)
    table = rows[:, 0].reshape(columns * 2 * capacity, rows.shape[3])
    contract = (((0,), (0,)), ((), ()))
    total = lax.dot_general(flat(hits), table[:, :width], contract, preferred_element_type=f32)
    out[0, :, :width] = total.astype(bf16)
    if out.shape[2] > width:
        first = flat(hits * jnp.where(meta[0:1] == ids, 1.0, 0.0)[:, None, :])
        second = flat(hits * jnp.where(meta[1:2] == ids, 1.0, 0.0)[:, None, :])
        parts = table[:, width:]
        low = lax.dot_general(first, parts, contract, preferred_element_type=f32)
        high = lax.dot_general(second, parts, contract, preferred_element_type=f32)
        lane = lax.broadcasted_iota(jnp.int32, (LANES, EXTRA), 1)
        out[0, :, width:] = jnp.where(lane < HALF, low, high).astype(bf16)


def fold(place, tagged, rows, capacity, extra, earlier=()):
    columns, depth, span, width = rows.shape
    return pl.pallas_call(
        functools.partial(fold_kernel, capacity, width - extra),
        out_shape=jax.ShapeDtypeStruct((depth, LANES, width), bf16),
        grid_spec=pltpu.PrefetchScalarGridSpec(
            num_scalar_prefetch=1,
            grid=(depth,),
            in_specs=[
                pl.BlockSpec((1, META, LANES), lambda z, place: (z, LANES // META, 0)),
                pl.BlockSpec((columns, 1, span, width), lambda z, place: (0, z, 0, 0)),
            ]
            + [pl.BlockSpec(memory_space=pl.ANY)] * len(earlier),
            out_specs=pl.BlockSpec((1, LANES, width), lambda z, place: (z, 0, 0)),
        ),
        compiler_params=pltpu.CompilerParams(vmem_limit_bytes=VMEM_LIMIT),
        name="fold_rows",
    )(place, tagged, rows, *earlier)


def weights_kernel(scales, preacts, scaled, gate_fac, up_fac, hidden):
    width = hidden.shape[1]
    scale = scales[:, 0:1].astype(f32)
    gate_pre = preacts[:, :width].astype(f32)
    up_pre = preacts[:, width:].astype(f32)
    sig = 1.0 / (1.0 + jnp.exp(-gate_pre))
    act = gate_pre * sig
    both = act * up_pre
    hidden[...] = both
    scaled[...] = (scale * both).astype(bf16)
    gate_fac[...] = scale * (up_pre * sig * (1.0 + gate_pre * (1.0 - sig)))
    up_fac[...] = scale * act


def slot_weights(received, preacts, steps):
    total, both = preacts.shape
    width = both // 2
    rows = total // steps
    last = received.shape[1] // EXTRA - 1
    block = pl.BlockSpec((rows, width), lambda i: (i, 0))
    shape = functools.partial(jax.ShapeDtypeStruct, (total, width))
    return pl.pallas_call(
        weights_kernel,
        out_shape=[shape(bf16), shape(f32), shape(f32), shape(f32)],
        grid=(steps,),
        in_specs=[
            pl.BlockSpec((rows, EXTRA), lambda i: (i, last)),
            pl.BlockSpec((rows, both), lambda i: (i, 0)),
        ],
        out_specs=[block] * 4,
        compiler_params=pltpu.CompilerParams(vmem_limit_bytes=VMEM_LIMIT),
        name="slot_weights",
    )(received, preacts)


NT = (((1,), (1,)), ((), ()))


def slice_grad(both, gate_up, out):
    grad = lax.dot_general(both, gate_up, NT, preferred_element_type=f32)
    out[0, :, :, : gate_up.shape[0]] = grad.astype(bf16).reshape(out.shape[1], out.shape[2], gate_up.shape[0])


def middle_kernel(last, down_proj, back, gate_fac, up_fac, hidden, gate_up, both, probs, out):
    total = back[...] + lax.dot_general(last[...], down_proj[...], NT, preferred_element_type=f32)
    part = jnp.sum(hidden[...] * total, axis=1, keepdims=True)
    probs[...] = jnp.broadcast_to(part, probs.shape).astype(bf16)
    half = total.shape[1]
    both[:, :half] = (total * gate_fac[...]).astype(bf16)
    both[:, half:] = (total * up_fac[...]).astype(bf16)
    slice_grad(both[...], gate_up[...], out)


def middle(last, down_proj, piece, back, gate_fac, up_fac, hidden, gate_up, block, width, grid_shape):
    columns, depth, span = grid_shape
    rows = depth * span
    total, half = back.shape
    full = gate_up.shape[1]
    wide = pl.BlockSpec((rows, half), lambda i: (i, 0))
    return pl.pallas_call(
        middle_kernel,
        out_shape=[
            jax.ShapeDtypeStruct((total, full), bf16),
            jax.ShapeDtypeStruct((total, EXTRA), bf16),
            jax.ShapeDtypeStruct((columns, depth, span, width), bf16),
        ],
        grid=(columns,),
        in_specs=[
            pl.BlockSpec((rows, last.shape[1]), lambda i: (i, 0)),
            pl.BlockSpec((half, last.shape[1]), lambda i: (0, piece)),
            wide,
            wide,
            wide,
            wide,
            pl.BlockSpec((width, full), lambda i: (block, 0)),
        ],
        out_specs=[
            pl.BlockSpec((rows, full), lambda i: (i, 0)),
            pl.BlockSpec((rows, EXTRA), lambda i: (i, 0)),
            pl.BlockSpec((1, depth, span, width), lambda i: (i, 0, 0, 0)),
        ],
        compiler_params=pltpu.CompilerParams(vmem_limit_bytes=VMEM_LIMIT),
        name="middle",
    )(last, down_proj, back, gate_fac, up_fac, hidden, gate_up)


def grad_kernel(both, gate_up, probs, *rest):
    out = rest[-1]
    slice_grad(both[...], gate_up[...], out)
    width = gate_up.shape[0]
    if out.shape[3] > width:
        out[0, :, :, width:] = probs[...].reshape(out.shape[1], out.shape[2], EXTRA)


def back_part(both, gate_up, probs, block, width, extra, grid_shape, earlier):
    columns, depth, span = grid_shape
    rows = depth * span
    full = gate_up.shape[1]
    return pl.pallas_call(
        grad_kernel,
        out_shape=jax.ShapeDtypeStruct((columns, depth, span, width + extra), bf16),
        grid=(columns,),
        in_specs=[
            pl.BlockSpec((rows, full), lambda i: (i, 0)),
            pl.BlockSpec((width, full), lambda i: (block, 0)),
            pl.BlockSpec((rows, EXTRA), lambda i: (i, 0)),
        ]
        + [pl.BlockSpec(memory_space=pl.ANY)] * len(earlier),
        out_specs=pl.BlockSpec((1, depth, span, width + extra), lambda i: (i, 0, 0, 0)),
        compiler_params=pltpu.CompilerParams(vmem_limit_bytes=VMEM_LIMIT),
        name="slice_grad",
    )(both, gate_up, probs, *earlier)


def exchange(block):
    return lax.all_to_all(block, "column", split_axis=0, concat_axis=0, tiled=True)


def shards(grad_out, gate_probs, routes, saved_preacts, w_gate_up, w_down):
    columns = lax.axis_size("column")
    depth = lax.axis_size("depth")
    capacity = saved_preacts.shape[4]
    span = 2 * capacity
    slots = columns * depth * span
    grid_shape = (columns, depth, span)
    width = grad_out.shape[3]
    tokens = grad_out.shape[2]
    starts = [sum(WIDTHS[1:])] + [sum(WIDTHS[1:c]) for c in range(1, len(WIDTHS))]
    bounds = [(low, low + size) for low, size in zip(starts, WIDTHS)]
    half = lax.axis_index("depth") // SHARE
    place = half.astype(jnp.int32).reshape(1)
    gate_up = w_gate_up[0, 0]
    down_proj = w_down[0, 0]

    picks = jnp.moveaxis(routes[0], 2, 0).reshape(2, 2 * tokens).astype(bf16)
    gates = jnp.moveaxis(gate_probs[0], 2, 0).reshape(2, 2 * tokens)
    tags = jnp.pad(jnp.concatenate([picks, gates]), ((0, META - 4), (0, WIDTHS[0] - 2 * tokens)))

    rows_in = grad_out[0].reshape(2 * tokens, width)
    got = []
    tagged = None
    for c, (low, high) in enumerate(bounds):
        part = rows_in[:, low:high]
        if c == 0:
            part = jnp.concatenate([part, tags])
        gathered = lax.all_gather(part, "depth", axis=0, tiled=False)
        tagged = gathered if c == 0 else tagged
        sent = pack(place, tagged, gathered, columns, capacity, EXTRA if c == 0 else 0)
        got.append(exchange(sent).reshape(slots, -1))
    preacts = jnp.concatenate([saved_preacts[0, 0, 0], saved_preacts[0, 1, 0]], axis=1)
    scaled, gate_fac, up_fac, hidden = slot_weights(got[0], preacts.reshape(slots, -1), columns)
    back = None
    for c in range(len(bounds) - 1):
        low, high = bounds[c]
        piece = lax.dot_general(
            got[c][:, : high - low], down_proj[:, low:high], NT, preferred_element_type=f32
        )
        back = piece if back is None else back + piece

    def down_slice(c):
        low, high = bounds[c]
        return lax.dot_general(
            scaled, got[c][:, : high - low], (((0,), (0,)), ((), ())), preferred_element_type=f32
        ).astype(bf16)

    order = list(range(1, len(bounds))) + [0]
    last = len(bounds) - 1
    both, probs, sending = middle(
        got[last],
        down_proj,
        bounds[last][0] // WIDTHS[last],
        back,
        gate_fac,
        up_fac,
        hidden,
        gate_up,
        bounds[order[0]][0] // WIDTHS[order[0]],
        WIDTHS[order[0]],
        grid_shape,
    )
    downs, moved, folded = {}, {}, {}
    for n, c in enumerate(order):
        returned = exchange(sending)
        if n + 1 < len(order):
            following = order[n + 1]
            earlier = []
            if n >= 1:
                downs[order[n - 1]] = down_slice(order[n - 1])
                earlier = [folded[order[n - 1]], downs[order[n - 1]]]
            following_rows = back_part(
                both,
                gate_up,
                probs,
                bounds[following][0] // WIDTHS[following],
                WIDTHS[following],
                EXTRA if following == 0 else 0,
                grid_shape,
                earlier,
            )
            earlier = [following_rows]
            sending = following_rows
        else:
            downs[order[n - 1]] = down_slice(order[n - 1])
            downs[c] = down_slice(c)
            down_grad = jnp.concatenate([downs[k] for k in order], axis=1)
            earlier = [down_grad, folded[order[n - 1]]] + [piece for k in order[: n - 1] for piece in moved[k]]
        folded[c] = fold(place, tagged, returned, capacity, EXTRA if c == 0 else 0, earlier)
        reduced = lax.psum_scatter(folded[c], "depth", scatter_dimension=0, tiled=False)
        moved[c] = (
            shifted(reduced[:tokens, : WIDTHS[c]], -1),
            shifted(reduced[tokens:, : WIDTHS[c]], 1),
        )
    prob_grad = reduced[:, WIDTHS[0] :].reshape(2, tokens, 2, HALF)[:, :, :, 0].astype(f32)
    return (
        jnp.concatenate([moved[c][0] for c in order], axis=1)[None],
        jnp.concatenate([moved[c][1] for c in order], axis=1)[None],
        prob_grad[None],
        down_grad[None, None],
    )


def solution(mesh):
    sections, slices = mesh.devices.shape
    grid = Mesh(mesh.devices.reshape(sections, slices // DEPTH, DEPTH), ("section", "column", "depth"))
    spread = ("column", "depth")
    in_specs = (
        P("section", None, spread, None),
        P("section", None, spread, None),
        P("section", None, spread, None),
        P("section", None, spread, None, None, None),
        P("section", spread, None, None),
        P("section", spread, None, None),
    )
    out_specs = (
        P("section", spread, None),
        P("section", spread, None),
        P("section", None, spread, None),
        P("section", spread, None, None),
    )
    return jax.shard_map(shards, mesh=grid, in_specs=in_specs, out_specs=out_specs, check_vma=False)
```

time: 691 us -> 550 us (0.80)
  blocking collectives: 391 us -> 0 us
  waiting for transfers between devices: 107 us -> 312 us
  Pallas kernels: 50 us -> 81.3 us
  starting transfers between devices: 70.8 us -> 83.2 us
  matrix products: 32.6 us -> 21.6 us
  local copies, waits for them, and re-layouts: 18.6 us -> 26.6 us
    all_gather x2 -> x0, blocking collectives: 273 us -> none  [the longest x1 140 us: shards(): lax.all_gather(jnp.pad(prob_part, (0, 2048 - sources * span)).reshape(16,...]
    all_to_all x4 -> x0, blocking collectives: 118 us -> none  [shards(): lax.all_to_all(part.reshape(columns, depth, span, step), 'column', split_...]
    all_to_all x4 -> x8, waiting for transfers between devices: 30.2 us -> 116 us  [exchange(): lax.all_to_all(block, 'column', split_axis=0, concat_axis=0, tiled=True)]
    reduce_scatter x4, waiting for transfers between devices: 0.06 us -> 66 us  [shards(): lax.psum_scatter(folded[c], 'depth', scatter_dimension=0, tiled=False)]
    all_gather x4, waiting for transfers between devices: 70.1 us -> 125 us  [shards(): gathered = lax.all_gather(part, 'depth', axis=0, tiled=False)]
    pallas_call x9 -> x13, Pallas kernels: 50 us -> 81.3 us  [the longest x4 28.1 us: fold(): pl.pallas_call(functools.partial(fold_kernel, capacity, width - extra), o...]
    all_to_all x4 -> x8, starting transfers between devices: 18 us -> 44.3 us  [exchange(): lax.all_to_all(block, 'column', split_axis=0, concat_axis=0, tiled=True)]
    ppermute x8, starting transfers between devices: 52.4 us -> 38.6 us  [shifted(): return lax.ppermute(block, 'section', route)]
  transfers between devices with their start and end apart: 20 -> 24, of which waited for: 7 -> 14; matrix products, arithmetic and copies ran while one was open for 5% -> 7% of each run, Pallas kernels for 6% -> 10%
where the time goes in v2:
time: 550 us; the launch traced here: 548 us
  waiting for transfers between devices  312 us (57%)
  starting transfers between devices  83.2 us (15%)
  Pallas kernels  81.3 us (15%)
  local copies, waits for them, and re-layouts  26.6 us (5%)
  matrix products  21.6 us (4%)
  between operations  14.5 us (3%)
  other arithmetic  8.4 us (2%)
    all_gather x4, waiting for transfers between devices, shards(): gathered = lax.all_gather(part, 'depth', axis=0, tiled=False)  125 us
    all_to_all x8, waiting for transfers between devices, exchange(): lax.all_to_all(block, 'column', split_axis=0, concat_axis=0, tiled=True)  116 us
    reduce_scatter x4, waiting for transfers between devices, shards(): lax.psum_scatter(folded[c], 'depth', scatter_dimension=0, tiled=False)  66 us
    all_to_all x8, starting transfers between devices, exchange(): lax.all_to_all(block, 'column', split_axis=0, concat_axis=0, tiled=True)  44.3 us
    ppermute x8, starting transfers between devices, shifted(): return lax.ppermute(block, 'section', route)  38.6 us
    pallas_call x4, Pallas kernels, fold(): pl.pallas_call(functools.partial(fold_kernel, capacity, width - extra), o...  28.1 us
    pallas_call x4, Pallas kernels, pack(): pl.pallas_call(functools.partial(pack_kernel, capacity, width), out_shape...  19.5 us
    pallas_call x3, Pallas kernels, back_part(): pl.pallas_call(grad_kernel, out_shape=jax.ShapeDtypeStruct((columns, dept...  17.7 us
  transfers between devices with their start and end apart: 24, of which 14 were waited for; matrix products, arithmetic and copies ran while one was open for 7% of the time, Pallas kernels for 10%

profile of v2, /device:TPU:1, one launch (start us, length us, event | category | flops | bytes accessed | tf_op | source)
XLA Modules:
  0.0 548.0 jit_solution(1059736622244423137)
XLA Ops:
  13.2 36.2 %all-gather.9.cloned.1.call-done = bf16[1152,512]{1,0:T(8,128)(2,1)} async-done(((bf16[144,512]{1,0:T(8,128)(2,1)}), bf16[1152,512]{1,0:T(8,128)(2,1)}) %all-gather.9.cloned.1.call-update) | async-done | bytes 1179664 | tf_op jit(solution)/shard_map/all_gather | solution.py:267
  60.2 31.3 %all-gather.13.cloned.1.call-done = bf16[1024,1024]{1,0:T(8,128)(2,1)} async-done(((bf16[128,1024]{1,0:T(8,128)(2,1)}), bf16[1024,1024]{1,0:T(8,128)(2,1)}) %all-gather.13.cloned.1.call-update) | async-done | bytes 2097168 | tf_op jit(solution)/shard_map/all_gather | solution.py:267
  104.9 28.7 %all-gather.15.cloned.1.call-done = bf16[1024,1024]{1,0:T(8,128)(2,1)} async-done(((bf16[128,1024]{1,0:T(8,128)(2,1)}), bf16[1024,1024]{1,0:T(8,128)(2,1)}) %all-gather.15.cloned.1.call-update) | async-done | bytes 2097168 | tf_op jit(solution)/shard_map/all_gather | solution.py:267
  147.1 28.5 %all-gather.11.cloned.1.call-done = bf16[1024,1024]{1,0:T(8,128)(2,1)} async-done(((bf16[128,1024]{1,0:T(8,128)(2,1)}), bf16[1024,1024]{1,0:T(8,128)(2,1)}) %all-gather.11.cloned.1.call-update) | async-done | bytes 2097168 | tf_op jit(solution)/shard_map/all_gather | solution.py:267
  205.9 22.2 %all-to-all-done = bf16[8,8,24,1024]{3,2,1,0:T(8,128)(2,1)} async-done(((bf16[8,8,24,1024]{3,2,1,0:T(8,128)(2,1)}), bf16[8,8,24,1024]{3,2,1,0:T(8,128)(2,1)}, u32[]{:S(2)}, u32[]{:S(2)}) %all-to-all-start) | async-done | bytes 3145760 | tf_op jit(solution)/shard_map/all_to_all | solution.py:237
  231.0 11.3 %middle.1 = (bf16[1536,512]{1,0:T(8,128)(2,1)S(1)}, bf16[1536,128]{1,0:T(8,128)(2,1)S(1)}, bf16[8,8,24,1024]{3,2,1,0:T(8,128)(2,1)}) custom-call(bf16[1536,1024]{1,0:T(8,128)(2,1)} %bitcast.8.last, bf16[256,3584]{1,0:T(8,128)(2,1)} %bitcast.76, f32[1536,256]{1,0:T(8,128)S(1)} %copy-done.3, f32[1536,256]{1,0:T(8,128)S(1)} %copy-done.12, ...), custom_call_target="tpu_custom_call" | custom-call | tf_op jit(solution)/shard_map/middle/pallas_call | solution.py:181
  246.8 5.3 slice_grad.3.rest_0_
  253.7 31.3 %all-to-all-done.4.rows = bf16[8,8,24,1024]{3,2,1,0:T(8,128)(2,1)} async-done(((bf16[8,8,24,1024]{3,2,1,0:T(8,128)(2,1)}), bf16[8,8,24,1024]{3,2,1,0:T(8,128)(2,1)}, u32[]{:S(2)}, u32[]{:S(2)}) %all-to-all-start.4) | async-done | bytes 3145760 | tf_op jit(solution)/shard_map/all_to_all | solution.py:237
  285.0 7.3 %fold_rows.4.rest_0_ = bf16[8,128,1024]{2,1,0:T(8,128)(2,1)} custom-call(s32[1]{0:T(128)} %bitcast.place, bf16[8,144,512]{2,1,0:T(8,128)(2,1)S(1)} %bitcast.61, bf16[8,8,24,1024]{3,2,1,0:T(8,128)(2,1)} %all-to-all-done.4.rows, bf16[8,8,24,1024]{3,2,1,0:T(8,128)(2,1)} %copy-done.2), custom_call_target="tpu_custom_call" | custom-call | tf_op jit(solution)/shard_map/fold_rows/pallas_call | solution.py:104
  300.0 6.8 %slice_grad.4.rest_0_ = bf16[8,8,24,1024]{3,2,1,0:T(8,128)(2,1)} custom-call(bf16[1536,512]{1,0:T(8,128)(2,1)S(1)} %get-tuple-element.15.both, bf16[3584,512]{1,0:T(8,128)(2,1)} %bitcast.70, bf16[1536,128]{1,0:T(8,128)(2,1)S(1)} %get-tuple-element.16.probs, bf16[8,128,1024]{2,1,0:T(8,128)(2,1)} %fold_rows.4.rest_0_, ...), custom_call_target="tpu_custom_call" | custom-call | tf_op jit(solution)/shard_map/slice_grad/pallas_call | solution.py:220
  307.7 27.5 %all-to-all-done.5.rows = bf16[8,8,24,1024]{3,2,1,0:T(8,128)(2,1)} async-done(((bf16[8,8,24,1024]{3,2,1,0:T(8,128)(2,1)}), bf16[8,8,24,1024]{3,2,1,0:T(8,128)(2,1)}, u32[]{:S(2)}, u32[]{:S(2)}) %all-to-all-start.5) | async-done | bytes 3145760 | tf_op jit(solution)/shard_map/all_to_all | solution.py:237
  335.2 7.4 %fold_rows.5.rest_0_ = bf16[8,128,1024]{2,1,0:T(8,128)(2,1)} custom-call(s32[1]{0:T(128)} %bitcast.place, bf16[8,144,512]{2,1,0:T(8,128)(2,1)S(1)} %bitcast.62, bf16[8,8,24,1024]{3,2,1,0:T(8,128)(2,1)} %all-to-all-done.5.rows, bf16[8,8,24,1024]{3,2,1,0:T(8,128)(2,1)} %slice_grad.4.rest_0_), custom_call_target="tpu_custom_call" | custom-call | tf_op jit(solution)/shard_map/fold_rows/pallas_call | solution.py:104
  342.5 11.2 %all-to-all-start.6 = ((bf16[8,8,24,1024]{3,2,1,0:T(8,128)(2,1)}), bf16[8,8,24,1024]{3,2,1,0:T(8,128)(2,1)}, u32[]{:S(2)}, u32[]{:S(2)}) async-start(bf16[8,8,24,1024]{3,2,1,0:T(8,128)(2,1)} %slice_grad.4.rest_0_), calls=%async_computation.8 | async-start | bytes 6291456 | tf_op jit(solution)/shard_map/all_to_all | solution.py:237
  356.9 5.5 %slice_grad.5.rest_0_ = bf16[8,8,24,640]{3,2,1,0:T(8,128)(2,1)} custom-call(bf16[1536,512]{1,0:T(8,128)(2,1)S(1)} %get-tuple-element.15.both, bf16[3584,512]{1,0:T(8,128)(2,1)} %bitcast.71, bf16[1536,128]{1,0:T(8,128)(2,1)S(1)} %get-tuple-element.16.probs, bf16[8,128,1024]{2,1,0:T(8,128)(2,1)} %fold_rows.5.rest_0_, ...), custom_call_target="tpu_custom_call" | custom-call | tf_op jit(solution)/shard_map/slice_grad/pallas_call | solution.py:220
  363.2 28.9 %all-to-all-done.6.rows = bf16[8,8,24,1024]{3,2,1,0:T(8,128)(2,1)} async-done(((bf16[8,8,24,1024]{3,2,1,0:T(8,128)(2,1)}), bf16[8,8,24,1024]{3,2,1,0:T(8,128)(2,1)}, u32[]{:S(2)}, u32[]{:S(2)}) %all-to-all-start.6) | async-done | bytes 3145760 | tf_op jit(solution)/shard_map/all_to_all | solution.py:237
  392.1 5.4 all-to-all-start.7
  405.7 7.4 %collective-permute-start.3 = (bf16[64,1024]{1,0:T(8,128)(2,1)}, bf16[64,1024]{1,0:T(8,128)(2,1)}, u32[]{:S(2)}, u32[]{:S(2)}) collective-permute-start(bf16[64,1024]{1,0:T(8,128)(2,1)} %get-tuple-element.29), channel_id=1, source_target_pairs={{0,64},{64,128},{128,192},{1,65},{65,129},{129,193},{2,66},{66,130... | collective-permute-start | bytes 393224 | tf_op jit(solution)/shard_map/ppermute | solution.py:26
  416.7 5.1 collective-permute-start.4
  426.6 7.4 %fold_rows.6.rest_1_ = bf16[8,128,1024]{2,1,0:T(8,128)(2,1)} custom-call(s32[1]{0:T(128)} %bitcast.place, bf16[8,144,512]{2,1,0:T(8,128)(2,1)S(1)} %bitcast.63, bf16[8,8,24,1024]{3,2,1,0:T(8,128)(2,1)} %all-to-all-done.6.rows, bf16[8,8,24,640]{3,2,1,0:T(8,128)(2,1)} %slice_grad.5.rest_0_), custom_call_target="tpu_custom_call" | custom-call | tf_op jit(solution)/shard_map/fold_rows/pallas_call | solution.py:104
  434.0 6.0 %fold_rows.7 = bf16[8,128,640]{2,1,0:T(8,128)(2,1)S(1)} custom-call(s32[1]{0:T(128)} %bitcast.place, bf16[8,144,512]{2,1,0:T(8,128)(2,1)S(1)} %bitcast.64, bf16[8,8,24,640]{3,2,1,0:T(8,128)(2,1)} %all-to-all-done.7.rows, bf16[256,3584]{1,0:T(8,128)(2,1)S(1)} %get-tuple-element.19.rest_0_, bf16[8,128,1024]{2,1,0:T(8,128)(2,1)} %fold_rows.6.rest_1_, ...), custom_call_target="tpu_custom_call" | custom-call | tf_op jit(solution)/shard_map/fold_rows/pallas_call | solution.py:104
  441.9 33.9 %reduce-scatter.11.cloned.1.call-done = bf16[1,128,640]{2,1,0:T(8,128)(2,1)} async-done(((bf16[8,128,640]{2,1,0:T(8,128)(2,1)}), bf16[1,128,640]{2,1,0:T(8,128)(2,1)}) %reduce-scatter.11.cloned.1.call-update) | async-done | bytes 163856 | tf_op jit(solution)/shard_map/reduce_scatter | solution.py:329
  477.6 9.2 %collective-permute-start.7 = (bf16[64,512]{1,0:T(8,128)(2,1)S(1)}, bf16[64,512]{1,0:T(8,128)(2,1)S(1)}, u32[]{:S(2)}, u32[]{:S(2)}) collective-permute-start(bf16[64,512]{1,0:T(8,128)(2,1)S(1)} %get-tuple-element.31), channel_id=1, source_target_pairs={{0,64},{64,128},{128,192},{1,65},{65,129},{129,193},{2,66},{66,130... | collective-permute-start | bytes 196616 | tf_op jit(solution)/shard_map/ppermute | solution.py:26
  486.8 32.0 %reduce-scatter.9.cloned.1.call-done = bf16[1,128,1024]{2,1,0:T(8,128)(2,1)} async-done(((bf16[8,128,1024]{2,1,0:T(8,128)(2,1)}), bf16[1,128,1024]{2,1,0:T(8,128)(2,1)}) %reduce-scatter.9.cloned.1.call-update) | async-done | bytes 262160 | tf_op jit(solution)/shard_map/reduce_scatter | solution.py:329
  519.9 9.2 %collective-permute-start.6 = (bf16[64,1024]{1,0:T(8,128)(2,1)S(1)}, bf16[64,1024]{1,0:T(8,128)(2,1)S(1)}, u32[]{:S(2)}, u32[]{:S(2)}) collective-permute-start(bf16[64,1024]{1,0:T(8,128)(2,1)S(1)} %get-tuple-element.25), channel_id=1, source_target_pairs={{0,64},{64,128},{128,192},{1,65},{65,129},{129,193},{2,66},{66,130... | collective-permute-start | bytes 393224 | tf_op jit(solution)/shard_map/ppermute | solution.py:26
  (117 shorter events, 128.4 us)
Async XLA Ops:
  7.2 42.2 %all-gather.9.cloned.1.call-start = ((), (), s32[]{:S(2)}) async-start(), calls=%async_computation.16 | async-start | bytes 1327104 | tf_op jit(solution)/shard_map/all_gather | solution.py:267
  10.4 81.1 %all-gather.13.cloned.1.call-start = ((), (), s32[]{:S(2)}) async-start(), calls=%async_computation.18 | async-start | bytes 2359296 | tf_op jit(solution)/shard_map/all_gather | solution.py:267
  12.5 121.1 %all-gather.15.cloned.1.call-start = ((), (), s32[]{:S(2)}) async-start(), calls=%async_computation.19 | async-start | bytes 2359296 | tf_op jit(solution)/shard_map/all_gather | solution.py:267
  55.2 42.9 %all-to-all-start.1 = ((bf16[8,8,24,640]{3,2,1,0:T(8,128)(2,1)}), bf16[8,8,24,640]{3,2,1,0:T(8,128)(2,1)S(1)}, u32[]{:S(2)}, u32[]{:S(2)}) async-start(bf16[8,8,24,640]{3,2,1,0:T(8,128)(2,1)} %pack_rows.5), calls=%async_computation.1 | async-start | bytes 3932160 | tf_op jit(solution)/shard_map/all_to_all | solution.py:237
  99.4 43.3 %all-to-all-start.2 = ((bf16[8,8,24,1024]{3,2,1,0:T(8,128)(2,1)}), bf16[8,8,24,1024]{3,2,1,0:T(8,128)(2,1)}, u32[]{:S(2)}, u32[]{:S(2)}) async-start(bf16[8,8,24,1024]{3,2,1,0:T(8,128)(2,1)} %pack_rows.6), calls=%async_computation.2 | async-start | bytes 6291456 | tf_op jit(solution)/shard_map/all_to_all | solution.py:237
  104.3 71.4 %all-gather.11.cloned.1.call-start = ((), (), s32[]{:S(2)}) async-start(), calls=%async_computation.17 | async-start | bytes 2359296 | tf_op jit(solution)/shard_map/all_gather | solution.py:267
  142.7 42.7 %all-to-all-start.3 = ((bf16[8,8,24,1024]{3,2,1,0:T(8,128)(2,1)}), bf16[8,8,24,1024]{3,2,1,0:T(8,128)(2,1)}, u32[]{:S(2)}, u32[]{:S(2)}) async-start(bf16[8,8,24,1024]{3,2,1,0:T(8,128)(2,1)} %pack_rows.7), calls=%async_computation.3 | async-start | bytes 6291456 | tf_op jit(solution)/shard_map/all_to_all | solution.py:237
  185.4 42.8 %all-to-all-start = ((bf16[8,8,24,1024]{3,2,1,0:T(8,128)(2,1)}), bf16[8,8,24,1024]{3,2,1,0:T(8,128)(2,1)}, u32[]{:S(2)}, u32[]{:S(2)}) async-start(bf16[8,8,24,1024]{3,2,1,0:T(8,128)(2,1)} %pack_rows.4), calls=%async_computation | async-start | bytes 6291456 | tf_op jit(solution)/shard_map/all_to_all | solution.py:237
  242.2 42.8 %all-to-all-start.4 = ((bf16[8,8,24,1024]{3,2,1,0:T(8,128)(2,1)}), bf16[8,8,24,1024]{3,2,1,0:T(8,128)(2,1)}, u32[]{:S(2)}, u32[]{:S(2)}) async-start(bf16[8,8,24,1024]{3,2,1,0:T(8,128)(2,1)} %get-tuple-element.14), calls=%async_computation.4 | async-start | bytes 6291456 | tf_op jit(solution)/shard_map/all_to_all | solution.py:237
  246.7 157.3 %reduce-scatter.5.cloned.1.call-start = ((), (), s32[]{:S(2)}) async-start(), calls=%async_computation.12 | async-start | bytes 2359296 | tf_op jit(solution)/shard_map/reduce_scatter | solution.py:329
  292.4 42.8 %all-to-all-start.5 = ((bf16[8,8,24,1024]{3,2,1,0:T(8,128)(2,1)}), bf16[8,8,24,1024]{3,2,1,0:T(8,128)(2,1)}, u32[]{:S(2)}, u32[]{:S(2)}) async-start(bf16[8,8,24,1024]{3,2,1,0:T(8,128)(2,1)} %copy-done.2), calls=%async_computation.6 | async-start | bytes 6291456 | tf_op jit(solution)/shard_map/all_to_all | solution.py:237
  296.8 118.2 %reduce-scatter.7.cloned.1.call-start = ((), (), s32[]{:S(2)}) async-start(), calls=%async_computation.13 | async-start | bytes 2359296 | tf_op jit(solution)/shard_map/reduce_scatter | solution.py:329
  342.5 49.6 %all-to-all-start.6 = ((bf16[8,8,24,1024]{3,2,1,0:T(8,128)(2,1)}), bf16[8,8,24,1024]{3,2,1,0:T(8,128)(2,1)}, u32[]{:S(2)}, u32[]{:S(2)}) async-start(bf16[8,8,24,1024]{3,2,1,0:T(8,128)(2,1)} %slice_grad.4.rest_0_), calls=%async_computation.8 | async-start | bytes 6291456 | tf_op jit(solution)/shard_map/all_to_all | solution.py:237
  392.1 41.8 %all-to-all-start.7 = ((bf16[8,8,24,640]{3,2,1,0:T(8,128)(2,1)}), bf16[8,8,24,640]{3,2,1,0:T(8,128)(2,1)}, u32[]{:S(2)}, u32[]{:S(2)}) async-start(bf16[8,8,24,640]{3,2,1,0:T(8,128)(2,1)} %slice_grad.5.rest_0_), calls=%async_computation.10 | async-start | bytes 3932160 | tf_op jit(solution)/shard_map/all_to_all | solution.py:237
  397.5 78.3 %reduce-scatter.11.cloned.1.call-start = ((), (), s32[]{:S(2)}) async-start(), calls=%async_computation.15 | async-start | bytes 1474560 | tf_op jit(solution)/shard_map/reduce_scatter | solution.py:329
  405.7 28.3 %collective-permute-start.3 = (bf16[64,1024]{1,0:T(8,128)(2,1)}, bf16[64,1024]{1,0:T(8,128)(2,1)}, u32[]{:S(2)}, u32[]{:S(2)}) collective-permute-start(bf16[64,1024]{1,0:T(8,128)(2,1)} %get-tuple-element.29), channel_id=1, source_target_pairs={{0,64},{64,128},{128,192},{1,65},{65,129},{129,193},{2,66},{66,130... | collective-permute-start | bytes 393224 | tf_op jit(solution)/shard_map/ppermute | solution.py:26
  413.1 20.9 %collective-permute-start = (bf16[64,1024]{1,0:T(8,128)(2,1)}, bf16[64,1024]{1,0:T(8,128)(2,1)}, u32[]{:S(2)}, u32[]{:S(2)}) collective-permute-start(bf16[64,1024]{1,0:T(8,128)(2,1)} %get-tuple-element.30), channel_id=1, source_target_pairs={{64,0},{128,64},{192,128},{65,1},{129,65},{193,129},{66,2},{130,66... | collective-permute-start | bytes 393224 | tf_op jit(solution)/shard_map/ppermute | solution.py:26
  416.7 17.2 %collective-permute-start.4 = (bf16[64,1024]{1,0:T(8,128)(2,1)}, bf16[64,1024]{1,0:T(8,128)(2,1)}, u32[]{:S(2)}, u32[]{:S(2)}) collective-permute-start(bf16[64,1024]{1,0:T(8,128)(2,1)} %get-tuple-element.27), channel_id=1, source_target_pairs={{0,64},{64,128},{128,192},{1,65},{65,129},{129,193},{2,66},{66,130... | collective-permute-start | bytes 393224 | tf_op jit(solution)/shard_map/ppermute | solution.py:26
  421.9 12.1 %collective-permute-start.1 = (bf16[64,1024]{1,0:T(8,128)(2,1)}, bf16[64,1024]{1,0:T(8,128)(2,1)}, u32[]{:S(2)}, u32[]{:S(2)}) collective-permute-start(bf16[64,1024]{1,0:T(8,128)(2,1)} %get-tuple-element.28), channel_id=1, source_target_pairs={{64,0},{128,64},{192,128},{65,1},{129,65},{193,129},{66,2},{130,66... | collective-permute-start | bytes 393224 | tf_op jit(solution)/shard_map/ppermute | solution.py:26
  441.1 77.7 %reduce-scatter.9.cloned.1.call-start = ((), (), s32[]{:S(2)}) async-start(), calls=%async_computation.14 | async-start | bytes 2359296 | tf_op jit(solution)/shard_map/reduce_scatter | solution.py:329
  477.6 55.9 %collective-permute-start.7 = (bf16[64,512]{1,0:T(8,128)(2,1)S(1)}, bf16[64,512]{1,0:T(8,128)(2,1)S(1)}, u32[]{:S(2)}, u32[]{:S(2)}) collective-permute-start(bf16[64,512]{1,0:T(8,128)(2,1)S(1)} %get-tuple-element.31), channel_id=1, source_target_pairs={{0,64},{64,128},{128,192},{1,65},{65,129},{129,193},{2,66},{66,130... | collective-permute-start | bytes 196616 | tf_op jit(solution)/shard_map/ppermute | solution.py:26
  519.9 13.7 %collective-permute-start.6 = (bf16[64,1024]{1,0:T(8,128)(2,1)S(1)}, bf16[64,1024]{1,0:T(8,128)(2,1)S(1)}, u32[]{:S(2)}, u32[]{:S(2)}) collective-permute-start(bf16[64,1024]{1,0:T(8,128)(2,1)S(1)} %get-tuple-element.25), channel_id=1, source_target_pairs={{0,64},{64,128},{128,192},{1,65},{65,129},{129,193},{2,66},{66,130... | collective-permute-start | bytes 393224 | tf_op jit(solution)/shard_map/ppermute | solution.py:26
  529.7 7.1 %collective-permute-start.5 = (bf16[64,512]{1,0:T(8,128)(2,1)S(1)}, bf16[64,512]{1,0:T(8,128)(2,1)S(1)}, u32[]{:S(2)}, u32[]{:S(2)}) collective-permute-start(bf16[64,512]{1,0:T(8,128)(2,1)S(1)} %get-tuple-element.32), channel_id=1, source_target_pairs={{64,0},{128,64},{192,128},{65,1},{129,65},{193,129},{66,2},{130,66... | collective-permute-start | bytes 196616 | tf_op jit(solution)/shard_map/ppermute | solution.py:26
  531.6 7.8 %collective-permute-start.2 = (bf16[64,1024]{1,0:T(8,128)(2,1)S(1)}, bf16[64,1024]{1,0:T(8,128)(2,1)S(1)}, u32[]{:S(2)}, u32[]{:S(2)}) collective-permute-start(bf16[64,1024]{1,0:T(8,128)(2,1)S(1)} %get-tuple-element.26), channel_id=1, source_target_pairs={{64,0},{128,64},{192,128},{65,1},{129,65},{193,129},{66,2},{130,66... | collective-permute-start | bytes 393224 | tf_op jit(solution)/shard_map/ppermute | solution.py:26
  (21 other events, 147.4 us)
Sparse Core Ops, SparseCore 0:
  10.5 38.8 all-gather.8
  51.8 39.7 all-gather.12
  93.9 39.6 all-gather.14
  135.8 39.8 all-gather.10
  292.5 44.2 reduce-scatter.4
  342.7 46.2 reduce-scatter.6
  441.2 34.4 reduce-scatter.10
  478.3 40.4 reduce-scatter.8

commit v3 on v0

v3 whole, which is shorter than its diff:
```python
import functools

import jax
import jax.numpy as jnp
from jax import lax
from jax.experimental import pallas as pl
from jax.experimental.pallas import tpu as pltpu
from jax.sharding import Mesh, PartitionSpec as P

SHARE = 4
DEPTH = 2 * SHARE
GROUPS = ((0,), (-1, 1), (-2, 2), (-3, 3), (-4,))
EXTRA = 128
HALF = 64
LANES = 128
META = 8
TILE = 512
VMEM_LIMIT = 56 * 1024 * 1024

f32 = jnp.float32
bf16 = jnp.bfloat16
NT = (((1,), (1,)), ((), ()))
TN = (((0,), (0,)), ((), ()))


def tags(rows):
    meta = rows[LANES : LANES + META, : 4 * LANES].astype(f32)
    return [meta[0:1, k * LANES : (k + 1) * LANES] for k in range(4)]


def slot_hits(picks, half, count, capacity):
    ids = (half + 2 * lax.broadcasted_iota(jnp.int32, (count, LANES), 0)).astype(f32)
    named = (picks[0] == ids) | (picks[1] == ids)
    row = lax.broadcasted_iota(jnp.int32, (LANES, LANES), 0)
    col = lax.broadcasted_iota(jnp.int32, (LANES, LANES), 1)
    earlier = (row < col) & (row // HALF == col // HALF)
    before = jnp.dot(
        named.astype(f32).astype(bf16), earlier.astype(f32).astype(bf16), preferred_element_type=f32
    )
    stretch = lax.broadcasted_iota(jnp.int32, (count, LANES), 1) // HALF
    keys = jnp.where(named, before + (stretch * capacity).astype(f32), -1.0)
    slot = lax.broadcasted_iota(jnp.int32, (count, 2 * capacity, LANES), 1).astype(f32)
    return jnp.where(slot == keys[:, None, :], 1.0, 0.0), ids


def flat(hits):
    return hits.reshape(-1, LANES).astype(bf16)


def tiles(width):
    return [slice(low, low + TILE) for low in range(0, width, TILE)]


def params():
    return pltpu.CompilerParams(vmem_limit_bytes=VMEM_LIMIT)


SMEM = pl.BlockSpec(memory_space=pltpu.SMEM)
VMEM = pl.BlockSpec(memory_space=pltpu.VMEM)
ANY = pl.BlockSpec(memory_space=pl.ANY)


def pack_kernel(capacity, count, tagged, width, place, *refs):
    out = refs[-1]
    columns = out.shape[0]
    for m in range(count):
        rows = refs[m]
        hits, _ = slot_hits(tags(rows), place[0], columns, capacity)
        ones = flat(hits)
        for tile in tiles(width):
            packed = jnp.dot(ones, rows[:LANES, tile], preferred_element_type=f32)
            out[:, m, :, tile] = packed.astype(bf16).reshape(columns, 2 * capacity, TILE)
    if out.shape[3] > width:
        lane = lax.broadcasted_iota(jnp.int32, (columns, 2 * capacity, EXTRA), 2)
        scales = jnp.zeros((columns, 2 * capacity, EXTRA), f32)
        for k, rows in enumerate(refs[count : count + tagged]):
            meta = rows[:, :].astype(f32)
            picks = [meta[0:1, i * LANES : (i + 1) * LANES] for i in range(4)]
            hits, ids = slot_hits(picks, place[0], columns, capacity)
            gates = jnp.where(picks[0] == ids, picks[2], 0.0) + jnp.where(picks[1] == ids, picks[3], 0.0)
            scale = jnp.sum(hits * gates[:, None, :], axis=2, keepdims=True)
            scales = jnp.where(lane == k, scale, scales)
        out[:, 0, :, width:] = scales.astype(bf16)


def pack(place, arrivals, columns, capacity, tagged=(), earlier=()):
    width = arrivals[0].shape[1]
    extra = EXTRA if tagged else 0
    only_tags = pl.BlockSpec((META, 4 * LANES), lambda i: (LANES // META, 0))
    return pl.pallas_call(
        functools.partial(pack_kernel, capacity, len(arrivals), len(tagged), width),
        out_shape=jax.ShapeDtypeStruct((columns, len(arrivals), 2 * capacity, width + extra), bf16),
        grid=(1,),
        in_specs=[SMEM] + [VMEM] * len(arrivals) + [only_tags] * len(tagged) + [ANY] * len(earlier),
        out_specs=VMEM,
        compiler_params=params(),
        name="pack_rows",
    )(place, *arrivals, *tagged, *earlier)


def expert_parts(rows, preacts, down_proj):
    width = down_proj.shape[1]
    half = down_proj.shape[0]
    back = lax.dot_general(rows, down_proj, NT, preferred_element_type=f32)
    gate_pre = preacts[:, :half].astype(f32)
    up_pre = preacts[:, half:].astype(f32)
    sig = 1.0 / (1.0 + jnp.exp(-gate_pre))
    act = gate_pre * sig
    hidden = act * up_pre
    part = jnp.sum(hidden * back, axis=1, keepdims=True)
    gate_side = back * up_pre * sig * (1.0 + gate_pre * (1.0 - sig))
    return gate_side, back * act, hidden, part


def prepare_kernel(width, place, rows, preacts, down_proj, sides, hidden, parts):
    slots = sides.shape[1]
    half = hidden.shape[2]
    table = rows[:, 0, :, :width].reshape(slots, width)
    pre = preacts[:, 0].reshape(slots, 2 * half)
    gate_side, up_side, hid, part = expert_parts(table, pre, down_proj[...])
    sides[0, :, :half] = gate_side
    sides[0, :, half:] = up_side
    hidden[0] = hid
    parts[0] = jnp.broadcast_to(part, (slots, EXTRA))


def prepare(place, received, preacts, down_proj):
    columns, count, span = received.shape[:3]
    half, width = down_proj.shape
    slots = columns * span
    block = lambda m, place: (m, 0, 0)
    return pl.pallas_call(
        functools.partial(prepare_kernel, width),
        out_shape=[
            jax.ShapeDtypeStruct((count, slots, 2 * half), f32),
            jax.ShapeDtypeStruct((count, slots, half), f32),
            jax.ShapeDtypeStruct((count, slots, EXTRA), f32),
        ],
        grid_spec=pltpu.PrefetchScalarGridSpec(
            num_scalar_prefetch=1,
            grid=(count,),
            in_specs=[
                pl.BlockSpec((columns, 1, span, width), lambda m, place: (0, m, 0, 0)),
                pl.BlockSpec((columns, 1, span, 2 * half), lambda m, place: (0, place[1 + m], 0, 0)),
                pl.BlockSpec((half, width), lambda m, place: (0, 0)),
            ],
            out_specs=[
                pl.BlockSpec((1, slots, 2 * half), block),
                pl.BlockSpec((1, slots, half), block),
                pl.BlockSpec((1, slots, EXTRA), block),
            ],
        ),
        compiler_params=params(),
        name="prepare",
    )(place, received, preacts, down_proj)


def turn_kernel(count, place, received, preacts, down_proj, gate_up, *refs):
    others, hidden, out = refs[:-2], refs[-2], refs[-1]
    half, width = down_proj.shape
    columns, _, span, _ = received.shape
    slots = columns * span
    table = received[:, 0, :, :width].reshape(slots, width)
    scales = received[:, 0, :, width:].astype(f32).reshape(slots, EXTRA)
    gate_side, up_side, hid, part = expert_parts(table, preacts[:, 0].reshape(slots, 2 * half), down_proj[...])
    hidden[0] = hid
    scale = scales[:, count - 1 : count]
    both = jnp.concatenate([scale * gate_side, scale * up_side], axis=1).astype(bf16)
    for tile in tiles(width):
        grad = lax.dot_general(both, gate_up[tile, :], NT, preferred_element_type=f32)
        out[:, 0, :, tile] = grad.astype(bf16).reshape(columns, span, TILE)
    lane = lax.broadcasted_iota(jnp.int32, (slots, EXTRA), 1)
    parts = jnp.where(lane == count - 1, part, 0.0)
    k = 0
    for group in others:
        for m in range(group.shape[0]):
            parts = jnp.where(lane == k, group[m], parts)
            k += 1
    out[:, 0, :, width:] = parts.astype(bf16).reshape(columns, span, EXTRA)


def turn(place, received, preacts, down_proj, gate_up, parts):
    columns, _, span, wide = received.shape
    half, width = down_proj.shape
    slots = columns * span
    count = 1 + sum(p.shape[0] for p in parts)
    return pl.pallas_call(
        functools.partial(turn_kernel, count),
        out_shape=[
            jax.ShapeDtypeStruct((1, slots, half), f32),
            jax.ShapeDtypeStruct((columns, 1, span, wide), bf16),
        ],
        grid_spec=pltpu.PrefetchScalarGridSpec(
            num_scalar_prefetch=1,
            grid=(1,),
            in_specs=[
                VMEM,
                pl.BlockSpec((columns, 1, span, 2 * half), lambda m, place: (0, place[1], 0, 0)),
                VMEM,
                VMEM,
            ]
            + [VMEM] * len(parts),
            out_specs=[VMEM, VMEM],
        ),
        compiler_params=params(),
        name="turn",
    )(place, received, preacts, down_proj, gate_up, *parts)


def grad_kernel(first, sides, last, gate_up, *rest):
    out = rest[-1]
    width = gate_up.shape[0]
    columns, _, span, _ = out.shape
    slots = columns * span
    scales = last[:, 0].reshape(slots, EXTRA).astype(f32)
    lane = lax.broadcasted_iota(jnp.int32, (slots, EXTRA), 1)
    index = first + pl.program_id(0)
    scale = jnp.sum(jnp.where(lane == index, scales, 0.0), axis=1, keepdims=True)
    both = (scale * sides[0]).astype(bf16)
    for tile in tiles(width):
        grad = lax.dot_general(both, gate_up[tile, :], NT, preferred_element_type=f32)
        out[:, 0, :, tile] = grad.astype(bf16).reshape(columns, span, TILE)


def slice_grad(first, sides, last, gate_up, earlier):
    count, slots, full = sides.shape
    columns, _, span, wide = last.shape
    width = gate_up.shape[0]
    return pl.pallas_call(
        functools.partial(grad_kernel, first),
        out_shape=jax.ShapeDtypeStruct((columns, count, span, width), bf16),
        grid=(count,),
        in_specs=[
            pl.BlockSpec((1, slots, full), lambda m: (m, 0, 0)),
            pl.BlockSpec((columns, 1, span, EXTRA), lambda m: (0, 0, 0, width // EXTRA)),
            pl.BlockSpec((width, full), lambda m: (0, 0)),
        ]
        + [ANY] * len(earlier),
        out_specs=pl.BlockSpec((columns, 1, span, width), lambda m: (0, m, 0, 0)),
        compiler_params=params(),
        name="slice_grad",
    )(sides, last, gate_up, *earlier)


def down_kernel(groups, last, *refs):
    rows, hidden, out, scaled = refs[:groups], refs[groups : 2 * groups], refs[-2], refs[-1]
    slots = hidden[0].shape[1]

    @pl.when(pl.program_id(0) == 0)
    def _():
        scales = last[:, 0].reshape(slots, EXTRA).astype(f32)
        k = 0
        for group in hidden:
            for m in range(group.shape[0]):
                scaled[k * slots : (k + 1) * slots] = (scales[:, k : k + 1] * group[m]).astype(bf16)
                k += 1

    total = jnp.zeros(out.shape, f32)
    k = 0
    for group in rows:
        for m in range(group.shape[1]):
            table = group[:, m].reshape(slots, out.shape[1])
            part = scaled[k * slots : (k + 1) * slots]
            total += lax.dot_general(part, table, TN, preferred_element_type=f32)
            k += 1
    out[...] = total.astype(bf16)


def down_grads(received, hidden, width):
    last = received[-1]
    columns, _, span, _ = last.shape
    count = sum(h.shape[0] for h in hidden)
    slots, half = hidden[0].shape[1:]
    return pl.pallas_call(
        functools.partial(down_kernel, len(received)),
        out_shape=jax.ShapeDtypeStruct((half, width), bf16),
        grid=(width // TILE,),
        in_specs=[pl.BlockSpec((columns, 1, span, EXTRA), lambda i: (0, 0, 0, width // EXTRA))]
        + [pl.BlockSpec((columns, g.shape[1], span, TILE), lambda i: (0, 0, 0, i)) for g in received]
        + [pl.BlockSpec(h.shape, lambda i: (0, 0, 0)) for h in hidden],
        out_specs=pl.BlockSpec((half, TILE), lambda i: (0, i)),
        scratch_shapes=[pltpu.VMEM((count * slots, half), bf16)],
        compiler_params=params(),
        name="down_grads",
    )(last, *received, *hidden)


def fold_kernel(capacity, first, count, coming, final, place, parts, *refs):
    returned = refs[0]
    metas = refs[1 : 1 + count]
    incoming = refs[1 + count : 1 + count + coming]
    outs = refs[-3:] if final else refs[-count:]
    columns, _, span, _ = returned.shape
    slots = columns * span
    table = parts[:, 0].astype(f32)
    for m in range(count):
        meta = metas[m][:, :].astype(f32)
        picks = [meta[0:1, i * LANES : (i + 1) * LANES] for i in range(4)]
        hits, ids = slot_hits(picks, place[0], columns, capacity)
        ones = flat(hits)
        added = list(incoming) if final else list(incoming[m : m + 1])
        for tile in tiles(returned.shape[3] // TILE * TILE):
            rows = returned[:, m, :, tile].reshape(slots, TILE)
            total = lax.dot_general(ones, rows, TN, preferred_element_type=f32)
            for other in added:
                total = total + other[:LANES, tile].astype(f32)
            total = total.astype(bf16)
            if final:
                outs[0][:, tile] = total[:HALF]
                outs[1][:, tile] = total[HALF:]
            else:
                outs[m][:LANES, tile] = total
        values = hits * table[:, :, first + m : first + m + 1]
        for k in range(2):
            named = jnp.where(picks[k] == ids, 1.0, 0.0)[:, None, :]
            line = jnp.sum(jnp.sum(values * named, axis=1), axis=0, keepdims=True)
            lanes = slice(k * LANES, (k + 1) * LANES)
            for other in added:
                line = line + other[LANES : LANES + META, lanes].astype(f32)[0:1]
            if final:
                outs[2][:, lanes] = jnp.broadcast_to(line, (META, LANES))
            else:
                outs[m][LANES : LANES + META, lanes] = jnp.broadcast_to(line, (META, LANES)).astype(bf16)


def fold(place, first, parts, returned, arrivals, incoming, capacity, final, earlier=()):
    columns, count, span, _ = returned.shape
    width = arrivals[0].shape[1]
    only_tags = pl.BlockSpec((META, 4 * LANES), lambda i: (LANES // META, 0))
    if final:
        shapes = [jax.ShapeDtypeStruct((HALF, width), bf16)] * 2
        shapes.append(jax.ShapeDtypeStruct((META, 2 * LANES), f32))
    else:
        shapes = [jax.ShapeDtypeStruct((LANES + META, width), bf16)] * count
    return pl.pallas_call(
        functools.partial(fold_kernel, capacity, first, count, len(incoming), final),
        out_shape=shapes,
        grid=(1,),
        in_specs=[SMEM, pl.BlockSpec((columns, 1, span, EXTRA), lambda i: (0, 0, 0, width // EXTRA)), VMEM]
        + [only_tags] * count
        + [VMEM] * len(incoming)
        + [ANY] * len(earlier),
        out_specs=[VMEM] * len(shapes),
        compiler_params=params(),
        name="fold_rows",
    )(place, parts, returned, *arrivals, *incoming, *earlier)


def exchange(block):
    return lax.all_to_all(block, "column", split_axis=0, concat_axis=0, tiled=True)


def hop(block, distance):
    return lax.ppermute(block, "depth", [(i, (i + distance) % DEPTH) for i in range(DEPTH)])


def shifted(block, distance):
    devices = range(lax.axis_size("section"))
    route = [(i - distance, i) for i in devices if i - distance in devices]
    return lax.ppermute(block, "section", route)


def shards(grad_out, gate_probs, routes, saved_preacts, w_gate_up, w_down):
    columns = lax.axis_size("column")
    capacity = saved_preacts.shape[4]
    span = 2 * capacity
    width = grad_out.shape[3]
    tokens = grad_out.shape[2]
    level = lax.axis_index("depth")
    half = level // SHARE
    gate_up = w_gate_up[0, 0]
    down_proj = w_down[0, 0]

    def place(group):
        where = [half] + [(level + DEPTH + offset) % DEPTH for offset in group]
        return jnp.stack(where).astype(jnp.int32)

    picks = jnp.moveaxis(routes[0], 2, 0).reshape(1, 4 * tokens).astype(bf16)
    gates = jnp.moveaxis(gate_probs[0], 2, 0).reshape(1, 4 * tokens)
    line = jnp.concatenate([picks, gates], axis=1)
    own = jnp.concatenate(
        [
            grad_out[0].reshape(2 * tokens, width),
            jnp.pad(line, ((0, META - 1), (0, width - line.shape[1]))),
        ]
    )
    arrivals = {0: own}
    for group in GROUPS[1:]:
        for offset in group:
            toward = 1 if offset < 0 else -1
            arrivals[offset] = hop(arrivals[offset + toward], toward)
    everyone = [arrivals[offset] for group in GROUPS for offset in group]

    preacts = jnp.concatenate([saved_preacts[0, 0, 0], saved_preacts[0, 1, 0]], axis=1)
    preacts = preacts.reshape(columns, DEPTH, span, -1)
    received, sides, hidden, parts = [], [], [], []
    for n, group in enumerate(GROUPS):
        last = group == GROUPS[-1]
        earlier = sides[n - 2 : n - 1] if n >= 2 else [preacts] * n
        sent = pack(
            place(group),
            [arrivals[offset] for offset in group],
            columns,
            capacity,
            everyone if last else (),
            earlier,
        )
        got = exchange(sent)
        received.append(got)
        if not last:
            pieces = prepare(place(group), got, preacts, down_proj)
            sides.append(pieces[0])
            hidden.append(pieces[1])
            parts.append(pieces[2])
    last = received[-1]
    final_hidden, sending = turn(place(GROUPS[-1]), last, preacts, down_proj, gate_up, parts)
    hidden.append(final_hidden)

    first = [sum(len(group) for group in GROUPS[:n]) for n in range(len(GROUPS))]
    part_rows = None
    coming = []
    folded = []
    down_grad = None
    for n in reversed(range(len(GROUPS))):
        group = GROUPS[n]
        returned = exchange(sending)
        if part_rows is None:
            part_rows = returned
        earlier = []
        if n > 0:
            if n == len(GROUPS) - 3:
                down_grad = down_grads(received, hidden, width)
                folded = list(folded) + [down_grad]
            sending = slice_grad(first[n - 1], sides[n - 1], last, gate_up, folded)
            earlier = [sending]
        folded = fold(
            place(group),
            first[n],
            part_rows,
            returned,
            [arrivals[offset] for offset in group],
            coming,
            capacity,
            n == 0,
            earlier,
        )
        if n > 0:
            coming = [hop(block, -1 if offset < 0 else 1) for block, offset in zip(folded, group)]
    above, below, probs = folded
    prob_grad = jnp.moveaxis(probs[0].reshape(2, 2, tokens), 0, 2)
    return (shifted(above, -1)[None], shifted(below, 1)[None], prob_grad[None], down_grad[None, None])


def solution(mesh):
    sections, slices = mesh.devices.shape
    grid = Mesh(mesh.devices.reshape(sections, slices // DEPTH, DEPTH), ("section", "column", "depth"))
    spread = ("column", "depth")
    in_specs = (
        P("section", None, spread, None),
        P("section", None, spread, None),
        P("section", None, spread, None),
        P("section", None, spread, None, None, None),
        P("section", spread, None, None),
        P("section", spread, None, None),
    )
    out_specs = (
        P("section", spread, None),
        P("section", spread, None),
        P("section", None, spread, None),
        P("section", spread, None, None),
    )
    return jax.shard_map(shards, mesh=grid, in_specs=in_specs, out_specs=out_specs, check_vma=False)
```

time: 698 us -> 416 us (0.60); the launches traced: 686 us -> 414 us
  waiting for transfers between devices: 468 us -> 205 us
  Pallas kernels: 0 us -> 98.5 us
  local copies, waits for them, and re-layouts: 90.1 us -> 21.2 us
  other arithmetic: 40.4 us -> 9.08 us
  matrix products: 27.7 us -> 0 us
  starting transfers between devices: 59.1 us -> 80.1 us
    all_to_all x4 -> x10, waiting for transfers between devices: 468 us -> 74.9 us  [exchange(): lax.all_to_all(block, 'column', split_axis=0, concat_axis=0, tiled=True)]
    ppermute x2 -> x16, waiting for transfers between devices: 0.01 us -> 130 us  [the longest x14 125 us: hop(): lax.ppermute(block, 'depth', [(i, (i + distance) % DEPTH) for i in range(...]
    pallas_call x0 -> x20, Pallas kernels: none -> 98.5 us  [the longest x4 23 us: slice_grad(): pl.pallas_call(functools.partial(grad_kernel, first), out_shape=jax.Shape...]
    reshape x10 -> x1, local copies, waits for them, and re-layouts: 28.7 us -> 0.09 us  [shards(): gates = jnp.moveaxis(gate_probs[0], 2, 0).reshape(1, 4 * tokens)]
    dot_general x3 -> x0, matrix products: 27.7 us -> none  [the longest x1 10.4 us: expert_slice(): lax.dot_general(d_both, gate_up, (((1,), (1,)), ((), ())), preferred_elem...]
    reduce_sum x10 -> x0, other arithmetic: 19.7 us -> none  [the longest x1 12.5 us: unpack(): grad_back.astype(jnp.float32).reshape(-1, SHARE, grad_back.shape[1], width)]
    broadcast_in_dim x14 -> x0, local copies, waits for them, and re-layouts: 19 us -> none  [the longest x10 18.6 us: spread(): jnp.broadcast_to(values[:, None], (values.shape[0], SHARE) + shape_rest)]
    concatenate x1 -> x0, local copies, waits for them, and re-layouts: 17.5 us -> none  [share_out(): rows = jnp.concatenate([spread(item[0]) for item in stretch_packs], axis=1)]
  transfers between devices with their start and end apart: 6 -> 26, of which waited for: 2 -> 24; matrix products, arithmetic and copies ran while one was open for 16% -> 3% of each run, Pallas kernels for 0% -> 20%
where the time goes in v3:
time: 416 us; the launch traced here: 414 us
  waiting for transfers between devices  205 us (49%)
  Pallas kernels  98.5 us (24%)
  starting transfers between devices  80.1 us (19%)
  local copies, waits for them, and re-layouts  21.2 us (5%)
  other arithmetic  9.08 us (2%)
    ppermute x14, waiting for transfers between devices, hop(): lax.ppermute(block, 'depth', [(i, (i + distance) % DEPTH) for i in range(...  125 us
    all_to_all x10, waiting for transfers between devices, exchange(): lax.all_to_all(block, 'column', split_axis=0, concat_axis=0, tiled=True)  74.9 us
    all_to_all x10, starting transfers between devices, exchange(): lax.all_to_all(block, 'column', split_axis=0, concat_axis=0, tiled=True)  53.2 us
    pallas_call x4, Pallas kernels, slice_grad(): pl.pallas_call(functools.partial(grad_kernel, first), out_shape=jax.Shape...  23 us
    pallas_call x5, Pallas kernels, fold(): pl.pallas_call(functools.partial(fold_kernel, capacity, first, count, len...  19.4 us
    pallas_call x4, Pallas kernels, prepare(): pl.pallas_call(functools.partial(prepare_kernel, width), out_shape=[jax.S...  19.4 us
    pallas_call x5, Pallas kernels, pack(): pl.pallas_call(functools.partial(pack_kernel, capacity, len(arrivals), le...  18.8 us
    unnamed x38, local copies, waits for them, and re-layouts  14.5 us
  transfers between devices with their start and end apart: 26, of which 24 were waited for; matrix products, arithmetic and copies ran while one was open for 3% of the time, Pallas kernels for 20%

profile of v3, /device:TPU:1, one launch (start us, length us, event | category | flops | bytes accessed | tf_op | source)
XLA Modules:
  0.0 414.3 jit_solution(3926392579663906814)
XLA Ops:
  7.9 6.0 %all-to-all-start = ((bf16[8,1,24,3584]{3,2,1,0:T(8,128)(2,1)}), bf16[8,1,24,3584]{3,2,1,0:T(8,128)(2,1)S(1)}, u32[]{:S(2)}, u32[]{:S(2)}) async-start(bf16[8,1,24,3584]{3,2,1,0:T(8,128)(2,1)} %pack_rows.5), calls=%async_computation | async-start | bytes 2752512 | tf_op jit(solution)/shard_map/all_to_all | solution.py:350
  13.9 5.7 %collective-permute-start.4 = (bf16[136,3584]{1,0:T(8,128)(2,1)S(1)}, bf16[136,3584]{1,0:T(8,128)(2,1)S(1)}, u32[]{:S(2)}, u32[]{:S(2)}) collective-permute-start(bf16[136,3584]{1,0:T(8,128)(2,1)S(1)} %copy-done.4), channel_id=1, source_target_pairs={{0,7},{1,0},{2,1},{3,2},{4,3},{5,4},{6,5},{7,6},{8,15},{9,8},{10,9... | collective-permute-start | bytes 2924552 | tf_op jit(solution)/shard_map/ppermute | solution.py:354
  27.7 11.7 %collective-permute-done.4.refs_3_.refs_1_.refs_2_ = bf16[136,3584]{1,0:T(8,128)(2,1)S(1)} collective-permute-done((bf16[136,3584]{1,0:T(8,128)(2,1)S(1)}, bf16[136,3584]{1,0:T(8,128)(2,1)S(1)}, u32[]{:S(2)}, u32[]{:S(2)}) %collective-permute-start.4) | collective-permute-done | bytes 974880 | tf_op jit(solution)/shard_map/ppermute | solution.py:354
  58.9 14.4 %collective-permute-done.5.refs_1_.refs_5_.refs_2_ = bf16[136,3584]{1,0:T(8,128)(2,1)} collective-permute-done((bf16[136,3584]{1,0:T(8,128)(2,1)}, bf16[136,3584]{1,0:T(8,128)(2,1)}, u32[]{:S(2)}, u32[]{:S(2)}) %collective-permute-start.5) | collective-permute-done | bytes 974880 | tf_op jit(solution)/shard_map/ppermute | solution.py:354
  79.9 6.9 %all-to-all-done.3.rows.refs_1_ = bf16[8,2,24,3584]{3,2,1,0:T(8,128)(2,1)S(1)} async-done(((bf16[8,2,24,3584]{3,2,1,0:T(8,128)(2,1)}), bf16[8,2,24,3584]{3,2,1,0:T(8,128)(2,1)S(1)}, u32[]{:S(2)}, u32[]{:S(2)}) %all-to-all-start.3) | async-done | bytes 2752544 | tf_op jit(solution)/shard_map/all_to_all | solution.py:350
  100.0 15.4 %collective-permute-done.6.refs_7_.refs_1_.refs_2_ = bf16[136,3584]{1,0:T(8,128)(2,1)S(1)} collective-permute-done((bf16[136,3584]{1,0:T(8,128)(2,1)}, bf16[136,3584]{1,0:T(8,128)(2,1)S(1)}, u32[]{:S(2)}, u32[]{:S(2)}) %collective-permute-start.6) | collective-permute-done | bytes 974880 | tf_op jit(solution)/shard_map/ppermute | solution.py:354
  126.8 8.9 %all-to-all-start.4 = ((bf16[8,2,24,3584]{3,2,1,0:T(8,128)(2,1)}), bf16[8,2,24,3584]{3,2,1,0:T(8,128)(2,1)S(1)}, u32[]{:S(2)}, u32[]{:S(2)}) async-start(bf16[8,2,24,3584]{3,2,1,0:T(8,128)(2,1)} %pack_rows.9), calls=%async_computation.4 | async-start | bytes 5505024 | tf_op jit(solution)/shard_map/all_to_all | solution.py:350
  141.5 16.8 %collective-permute-done.3.refs_0_.refs_8_.refs_1_ = bf16[136,3584]{1,0:T(8,128)(2,1)} collective-permute-done((bf16[136,3584]{1,0:T(8,128)(2,1)}, bf16[136,3584]{1,0:T(8,128)(2,1)}, u32[]{:S(2)}, u32[]{:S(2)}) %collective-permute-start.3) | collective-permute-done | bytes 974880 | tf_op jit(solution)/shard_map/ppermute | solution.py:354
  161.6 8.2 %all-to-all-done.4.rows.refs_3_ = bf16[8,2,24,3584]{3,2,1,0:T(8,128)(2,1)S(1)} async-done(((bf16[8,2,24,3584]{3,2,1,0:T(8,128)(2,1)}), bf16[8,2,24,3584]{3,2,1,0:T(8,128)(2,1)S(1)}, u32[]{:S(2)}, u32[]{:S(2)}) %all-to-all-start.4) | async-done | bytes 2752544 | tf_op jit(solution)/shard_map/all_to_all | solution.py:350
  174.9 5.1 %prepare.7 = (f32[2,192,512]{2,1,0:T(8,128)}, f32[2,192,256]{2,1,0:T(8,128)}, f32[2,192,128]{2,1,0:T(8,128)}) custom-call(s32[3]{0:T(128)} %pad_add_fusion.4.place, bf16[8,2,24,3584]{3,2,1,0:T(8,128)(2,1)} %copy-done.3, bf16[8,8,24,512]{3,2,1,0:T(8,128)(2,1)} %pad_maximum_fusion.preacts.refs_2_, bf16[256,3584]{1,0:T(8,128)(2,1)} %bitcast.37), custom_call_target="tpu_custom_call" | custom-call | tf_op jit(solution)/shard_map/prepare/pallas_call | solution.py:132
  180.0 14.7 %all-to-all-done.2.received.last.refs_4_ = bf16[8,1,24,3712]{3,2,1,0:T(8,128)(2,1)S(1)} async-done(((bf16[8,1,24,3712]{3,2,1,0:T(8,128)(2,1)}), bf16[8,1,24,3712]{3,2,1,0:T(8,128)(2,1)S(1)}, u32[]{:S(2)}, u32[]{:S(2)}) %all-to-all-start.2) | async-done | bytes 1425440 | tf_op jit(solution)/shard_map/all_to_all | solution.py:350
  195.8 7.6 %turn.1 = (f32[1,192,256]{2,1,0:T(8,128)}, bf16[8,1,24,3712]{3,2,1,0:T(8,128)(2,1)}) custom-call(s32[2]{0:T(128)} %pad_add_fusion.1.place, bf16[8,1,24,3712]{3,2,1,0:T(8,128)(2,1)} %copy-done, bf16[8,8,24,512]{3,2,1,0:T(8,128)(2,1)} %pad_maximum_fusion.preacts.refs_2_, bf16[256,3584]{1,0:T(8,128)(2,1)} %bitcast.38, bf16[3584,512]{1,0:T(8,128)(2,1)} %bitcast.29, ...), custom_call_target="tpu_custom_call" | custom-call | tf_op jit(solution)/shard_map/turn/pallas_call | solution.py:187
  207.0 6.1 %slice_grad.4.refs_2_ = bf16[8,2,24,3584]{3,2,1,0:T(8,128)(2,1)} custom-call(f32[2,192,512]{2,1,0:T(8,128)} %get-tuple-element.35.sides, bf16[8,1,24,3712]{3,2,1,0:T(8,128)(2,1)} %copy-done, bf16[3584,512]{1,0:T(8,128)(2,1)} %bitcast.30), custom_call_target="tpu_custom_call" | custom-call | tf_op jit(solution)/shard_map/slice_grad/pallas_call | solution.py:229
  213.1 13.7 %all-to-all-done.5.parts.refs_0_ = bf16[8,1,24,3712]{3,2,1,0:T(8,128)(2,1)S(1)} async-done(((bf16[8,1,24,3712]{3,2,1,0:T(8,128)(2,1)}), bf16[8,1,24,3712]{3,2,1,0:T(8,128)(2,1)S(1)}, u32[]{:S(2)}, u32[]{:S(2)}) %all-to-all-start.5) | async-done | bytes 1425440 | tf_op jit(solution)/shard_map/all_to_all | solution.py:350
  235.3 6.1 %slice_grad.5.refs_4_ = bf16[8,2,24,3584]{3,2,1,0:T(8,128)(2,1)} custom-call(f32[2,192,512]{2,1,0:T(8,128)} %get-tuple-element.28.refs_9_.sides, bf16[8,1,24,3712]{3,2,1,0:T(8,128)(2,1)} %copy-done, bf16[3584,512]{1,0:T(8,128)(2,1)} %bitcast.31, bf16[136,3584]{1,0:T(8,128)(2,1)} %fold_rows.5.rest_0_), custom_call_target="tpu_custom_call" | custom-call | tf_op jit(solution)/shard_map/slice_grad/pallas_call | solution.py:229
  241.5 25.0 %all-to-all-done.7.refs_0_ = bf16[8,2,24,3584]{3,2,1,0:T(8,128)(2,1)} async-done(((bf16[8,2,24,3584]{3,2,1,0:T(8,128)(2,1)}), bf16[8,2,24,3584]{3,2,1,0:T(8,128)(2,1)}, u32[]{:S(2)}, u32[]{:S(2)}) %all-to-all-start.7) | async-done | bytes 2752544 | tf_op jit(solution)/shard_map/all_to_all | solution.py:350
  266.5 9.0 %all-to-all-start.6 = ((bf16[8,2,24,3584]{3,2,1,0:T(8,128)(2,1)}), bf16[8,2,24,3584]{3,2,1,0:T(8,128)(2,1)S(1)}, u32[]{:S(2)}, u32[]{:S(2)}) async-start(bf16[8,2,24,3584]{3,2,1,0:T(8,128)(2,1)} %slice_grad.5.refs_4_), calls=%async_computation.6 | async-start | bytes 5505024 | tf_op jit(solution)/shard_map/all_to_all | solution.py:350
  276.6 10.3 %down_grads.1.rest_2_ = bf16[256,3584]{1,0:T(8,128)(2,1)} custom-call(bf16[8,1,24,3712]{3,2,1,0:T(8,128)(2,1)} %copy-done, bf16[8,1,24,3584]{3,2,1,0:T(8,128)(2,1)} %copy-done.5, bf16[8,2,24,3584]{3,2,1,0:T(8,128)(2,1)} %copy-done.2, bf16[8,2,24,3584]{3,2,1,0:T(8,128)(2,1)} %all-to-all-done.1.rows.refs_2_, bf16[8,2,24,3584]{3,2,1,0:T(8,128)(2,1)} %copy-done.3, ...), custom_call_target="tpu_custom_call" | custom-call | tf_op jit(solution)/shard_map/down_grads/pallas_call | solution.py:274
  286.9 9.9 %collective-permute-done.7.refs_3_ = bf16[136,3584]{1,0:T(8,128)(2,1)S(1)} collective-permute-done((bf16[136,3584]{1,0:T(8,128)(2,1)}, bf16[136,3584]{1,0:T(8,128)(2,1)S(1)}, u32[]{:S(2)}, u32[]{:S(2)}) %collective-permute-start.7) | collective-permute-done | bytes 974880 | tf_op jit(solution)/shard_map/ppermute | solution.py:354
  301.9 6.1 %slice_grad.6.refs_5_ = bf16[8,2,24,3584]{3,2,1,0:T(8,128)(2,1)} custom-call(f32[2,192,512]{2,1,0:T(8,128)} %get-tuple-element.32.refs_2_.sides, bf16[8,1,24,3712]{3,2,1,0:T(8,128)(2,1)} %copy-done, bf16[3584,512]{1,0:T(8,128)(2,1)} %bitcast.32, bf16[136,3584]{1,0:T(8,128)(2,1)} %get-tuple-element.36.rest_0_, bf16[136,3584]{1,0:T(8,128)(2,1)} %get-tuple-element.37.rest_1_, ...), custom_call_target="tpu_custom_call" | custom-call | tf_op jit(solution)/shard_map/slice_grad/pallas_call | solution.py:229
  317.2 19.7 %collective-permute-done.8.refs_3_ = bf16[136,3584]{1,0:T(8,128)(2,1)S(1)} collective-permute-done((bf16[136,3584]{1,0:T(8,128)(2,1)}, bf16[136,3584]{1,0:T(8,128)(2,1)S(1)}, u32[]{:S(2)}, u32[]{:S(2)}) %collective-permute-start.8) | collective-permute-done | bytes 974880 | tf_op jit(solution)/shard_map/ppermute | solution.py:354
  353.8 8.2 %collective-permute-done.10.refs_3_ = bf16[136,3584]{1,0:T(8,128)(2,1)S(1)} collective-permute-done((bf16[136,3584]{1,0:T(8,128)(2,1)}, bf16[136,3584]{1,0:T(8,128)(2,1)S(1)}, u32[]{:S(2)}, u32[]{:S(2)}) %collective-permute-start.10) | collective-permute-done | bytes 974880 | tf_op jit(solution)/shard_map/ppermute | solution.py:354
  371.1 16.3 %collective-permute-done.12.refs_2_ = bf16[136,3584]{1,0:T(8,128)(2,1)S(1)} collective-permute-done((bf16[136,3584]{1,0:T(8,128)(2,1)}, bf16[136,3584]{1,0:T(8,128)(2,1)S(1)}, u32[]{:S(2)}, u32[]{:S(2)}) %collective-permute-start.12) | collective-permute-done | bytes 974880 | tf_op jit(solution)/shard_map/ppermute | solution.py:354
  394.3 8.3 %collective-permute-start.14 = (bf16[64,3584]{1,0:T(8,128)(2,1)}, bf16[64,3584]{1,0:T(8,128)(2,1)S(1)}, u32[]{:S(2)}, u32[]{:S(2)}) collective-permute-start(bf16[64,3584]{1,0:T(8,128)(2,1)} %get-tuple-element.47), channel_id=1, source_target_pairs={{64,0},{128,64},{192,128},{65,1},{129,65},{193,129},{66,2},{130,66... | collective-permute-start | bytes 1376264 | tf_op jit(solution)/shard_map/ppermute | solution.py:360
  (105 shorter events, 153.4 us)
Async XLA Ops:
  7.9 38.9 %all-to-all-start = ((bf16[8,1,24,3584]{3,2,1,0:T(8,128)(2,1)}), bf16[8,1,24,3584]{3,2,1,0:T(8,128)(2,1)S(1)}, u32[]{:S(2)}, u32[]{:S(2)}) async-start(bf16[8,1,24,3584]{3,2,1,0:T(8,128)(2,1)} %pack_rows.5), calls=%async_computation | async-start | bytes 2752512 | tf_op jit(solution)/shard_map/all_to_all | solution.py:350
  13.9 25.6 %collective-permute-start.4 = (bf16[136,3584]{1,0:T(8,128)(2,1)S(1)}, bf16[136,3584]{1,0:T(8,128)(2,1)S(1)}, u32[]{:S(2)}, u32[]{:S(2)}) collective-permute-start(bf16[136,3584]{1,0:T(8,128)(2,1)S(1)} %copy-done.4), channel_id=1, source_target_pairs={{0,7},{1,0},{2,1},{3,2},{4,3},{5,4},{6,5},{7,6},{8,15},{9,8},{10,9... | collective-permute-start | bytes 2924552 | tf_op jit(solution)/shard_map/ppermute | solution.py:354
  19.6 23.1 %collective-permute-start = (bf16[136,3584]{1,0:T(8,128)(2,1)S(1)}, bf16[136,3584]{1,0:T(8,128)(2,1)}, u32[]{:S(2)}, u32[]{:S(2)}) collective-permute-start(bf16[136,3584]{1,0:T(8,128)(2,1)S(1)} %copy-done.4), channel_id=1, source_target_pairs={{0,1},{1,2},{2,3},{3,4},{4,5},{5,6},{6,7},{7,0},{8,9},{9,10},{10,1... | collective-permute-start | bytes 2924552 | tf_op jit(solution)/shard_map/ppermute | solution.py:354
  47.9 38.8 %all-to-all-start.3 = ((bf16[8,2,24,3584]{3,2,1,0:T(8,128)(2,1)}), bf16[8,2,24,3584]{3,2,1,0:T(8,128)(2,1)S(1)}, u32[]{:S(2)}, u32[]{:S(2)}) async-start(bf16[8,2,24,3584]{3,2,1,0:T(8,128)(2,1)} %pack_rows.8), calls=%async_computation.3 | async-start | bytes 5505024 | tf_op jit(solution)/shard_map/all_to_all | solution.py:350
  52.7 20.7 %collective-permute-start.5 = (bf16[136,3584]{1,0:T(8,128)(2,1)}, bf16[136,3584]{1,0:T(8,128)(2,1)}, u32[]{:S(2)}, u32[]{:S(2)}) collective-permute-start(bf16[136,3584]{1,0:T(8,128)(2,1)} %copy-done.7), channel_id=1, source_target_pairs={{0,7},{1,0},{2,1},{3,2},{4,3},{5,4},{6,5},{7,6},{8,15},{9,8},{10,9... | collective-permute-start | bytes 2924552 | tf_op jit(solution)/shard_map/ppermute | solution.py:354
  53.8 21.9 %collective-permute-start.1 = (bf16[136,3584]{1,0:T(8,128)(2,1)}, bf16[136,3584]{1,0:T(8,128)(2,1)}, u32[]{:S(2)}, u32[]{:S(2)}) collective-permute-start(bf16[136,3584]{1,0:T(8,128)(2,1)} %collective-permute-done.refs_2_.refs_0_.refs_1_), channel_id=1, source_target_pairs={{0,1},{1,2},{2,3},{3,4},{4,5},{5,6},{6,7},{7,0},{8,9},{9,10},{10,1... | collective-permute-start | bytes 2924552 | tf_op jit(solution)/shard_map/ppermute | solution.py:354
  88.3 38.5 %all-to-all-start.1 = ((bf16[8,2,24,3584]{3,2,1,0:T(8,128)(2,1)}), bf16[8,2,24,3584]{3,2,1,0:T(8,128)(2,1)}, u32[]{:S(2)}, u32[]{:S(2)}) async-start(bf16[8,2,24,3584]{3,2,1,0:T(8,128)(2,1)} %pack_rows.6), calls=%async_computation.1 | async-start | bytes 5505024 | tf_op jit(solution)/shard_map/all_to_all | solution.py:350
  92.7 22.6 %collective-permute-start.6 = (bf16[136,3584]{1,0:T(8,128)(2,1)}, bf16[136,3584]{1,0:T(8,128)(2,1)S(1)}, u32[]{:S(2)}, u32[]{:S(2)}) collective-permute-start(bf16[136,3584]{1,0:T(8,128)(2,1)} %collective-permute-done.5.refs_1_.refs_5_.refs_2_), channel_id=1, source_target_pairs={{0,7},{1,0},{2,1},{3,2},{4,3},{5,4},{6,5},{7,6},{8,15},{9,8},{10,9... | collective-permute-start | bytes 2924552 | tf_op jit(solution)/shard_map/ppermute | solution.py:354
  93.9 23.5 %collective-permute-start.2 = (bf16[136,3584]{1,0:T(8,128)(2,1)}, bf16[136,3584]{1,0:T(8,128)(2,1)S(1)}, u32[]{:S(2)}, u32[]{:S(2)}) collective-permute-start(bf16[136,3584]{1,0:T(8,128)(2,1)} %collective-permute-done.1.refs_0_.refs_4_.refs_1_), channel_id=1, source_target_pairs={{0,1},{1,2},{2,3},{3,4},{4,5},{5,6},{6,7},{7,0},{8,9},{9,10},{10,1... | collective-permute-start | bytes 2924552 | tf_op jit(solution)/shard_map/ppermute | solution.py:354
  126.8 42.9 %all-to-all-start.4 = ((bf16[8,2,24,3584]{3,2,1,0:T(8,128)(2,1)}), bf16[8,2,24,3584]{3,2,1,0:T(8,128)(2,1)S(1)}, u32[]{:S(2)}, u32[]{:S(2)}) async-start(bf16[8,2,24,3584]{3,2,1,0:T(8,128)(2,1)} %pack_rows.9), calls=%async_computation.4 | async-start | bytes 5505024 | tf_op jit(solution)/shard_map/all_to_all | solution.py:350
  135.7 22.5 %collective-permute-start.3 = (bf16[136,3584]{1,0:T(8,128)(2,1)}, bf16[136,3584]{1,0:T(8,128)(2,1)}, u32[]{:S(2)}, u32[]{:S(2)}) collective-permute-start(bf16[136,3584]{1,0:T(8,128)(2,1)} %copy-done.9), channel_id=1, source_target_pairs={{0,1},{1,2},{2,3},{3,4},{4,5},{5,6},{6,7},{7,0},{8,9},{9,10},{10,1... | collective-permute-start | bytes 2924552 | tf_op jit(solution)/shard_map/ppermute | solution.py:354
  171.4 23.4 %all-to-all-start.2 = ((bf16[8,1,24,3712]{3,2,1,0:T(8,128)(2,1)}), bf16[8,1,24,3712]{3,2,1,0:T(8,128)(2,1)S(1)}, u32[]{:S(2)}, u32[]{:S(2)}) async-start(bf16[8,1,24,3712]{3,2,1,0:T(8,128)(2,1)} %pack_rows.7), calls=%async_computation.2 | async-start | bytes 2850816 | tf_op jit(solution)/shard_map/all_to_all | solution.py:350
  203.4 23.4 %all-to-all-start.5 = ((bf16[8,1,24,3712]{3,2,1,0:T(8,128)(2,1)}), bf16[8,1,24,3712]{3,2,1,0:T(8,128)(2,1)S(1)}, u32[]{:S(2)}, u32[]{:S(2)}) async-start(bf16[8,1,24,3712]{3,2,1,0:T(8,128)(2,1)} %get-tuple-element.34), calls=%async_computation.5 | async-start | bytes 2850816 | tf_op jit(solution)/shard_map/all_to_all | solution.py:350
  228.0 38.5 %all-to-all-start.7 = ((bf16[8,2,24,3584]{3,2,1,0:T(8,128)(2,1)}), bf16[8,2,24,3584]{3,2,1,0:T(8,128)(2,1)}, u32[]{:S(2)}, u32[]{:S(2)}) async-start(bf16[8,2,24,3584]{3,2,1,0:T(8,128)(2,1)} %slice_grad.4.refs_2_), calls=%async_computation.7 | async-start | bytes 5505024 | tf_op jit(solution)/shard_map/all_to_all | solution.py:350
  266.5 43.1 %all-to-all-start.6 = ((bf16[8,2,24,3584]{3,2,1,0:T(8,128)(2,1)}), bf16[8,2,24,3584]{3,2,1,0:T(8,128)(2,1)S(1)}, u32[]{:S(2)}, u32[]{:S(2)}) async-start(bf16[8,2,24,3584]{3,2,1,0:T(8,128)(2,1)} %slice_grad.5.refs_4_), calls=%async_computation.6 | async-start | bytes 5505024 | tf_op jit(solution)/shard_map/all_to_all | solution.py:350
  275.5 21.2 %collective-permute-start.7 = (bf16[136,3584]{1,0:T(8,128)(2,1)}, bf16[136,3584]{1,0:T(8,128)(2,1)S(1)}, u32[]{:S(2)}, u32[]{:S(2)}) collective-permute-start(bf16[136,3584]{1,0:T(8,128)(2,1)} %fold_rows.5.rest_0_), channel_id=1, source_target_pairs={{0,7},{1,0},{2,1},{3,2},{4,3},{5,4},{6,5},{7,6},{8,15},{9,8},{10,9... | collective-permute-start | bytes 2924552 | tf_op jit(solution)/shard_map/ppermute | solution.py:354
  311.2 38.5 %all-to-all-start.9 = ((bf16[8,2,24,3584]{3,2,1,0:T(8,128)(2,1)}), bf16[8,2,24,3584]{3,2,1,0:T(8,128)(2,1)}, u32[]{:S(2)}, u32[]{:S(2)}) async-start(bf16[8,2,24,3584]{3,2,1,0:T(8,128)(2,1)} %slice_grad.6.refs_5_), calls=%async_computation.9 | async-start | bytes 5505024 | tf_op jit(solution)/shard_map/all_to_all | solution.py:350
  315.6 21.2 %collective-permute-start.8 = (bf16[136,3584]{1,0:T(8,128)(2,1)}, bf16[136,3584]{1,0:T(8,128)(2,1)S(1)}, u32[]{:S(2)}, u32[]{:S(2)}) collective-permute-start(bf16[136,3584]{1,0:T(8,128)(2,1)} %get-tuple-element.36.rest_0_), channel_id=1, source_target_pairs={{0,7},{1,0},{2,1},{3,2},{4,3},{5,4},{6,5},{7,6},{8,15},{9,8},{10,9... | collective-permute-start | bytes 2924552 | tf_op jit(solution)/shard_map/ppermute | solution.py:354
  316.8 20.8 %collective-permute-start.9 = (bf16[136,3584]{1,0:T(8,128)(2,1)}, bf16[136,3584]{1,0:T(8,128)(2,1)S(1)}, u32[]{:S(2)}, u32[]{:S(2)}) collective-permute-start(bf16[136,3584]{1,0:T(8,128)(2,1)} %get-tuple-element.37.rest_1_), channel_id=1, source_target_pairs={{0,1},{1,2},{2,3},{3,4},{4,5},{5,6},{6,7},{7,0},{8,9},{9,10},{10,1... | collective-permute-start | bytes 2924552 | tf_op jit(solution)/shard_map/ppermute | solution.py:354
  343.2 18.9 %collective-permute-start.10 = (bf16[136,3584]{1,0:T(8,128)(2,1)}, bf16[136,3584]{1,0:T(8,128)(2,1)S(1)}, u32[]{:S(2)}, u32[]{:S(2)}) collective-permute-start(bf16[136,3584]{1,0:T(8,128)(2,1)} %get-tuple-element.43.rest_0_), channel_id=1, source_target_pairs={{0,7},{1,0},{2,1},{3,2},{4,3},{5,4},{6,5},{7,6},{8,15},{9,8},{10,9... | collective-permute-start | bytes 2924552 | tf_op jit(solution)/shard_map/ppermute | solution.py:354
  344.2 19.9 %collective-permute-start.11 = (bf16[136,3584]{1,0:T(8,128)(2,1)}, bf16[136,3584]{1,0:T(8,128)(2,1)S(1)}, u32[]{:S(2)}, u32[]{:S(2)}) collective-permute-start(bf16[136,3584]{1,0:T(8,128)(2,1)} %get-tuple-element.44.rest_1_), channel_id=1, source_target_pairs={{0,1},{1,2},{2,3},{3,4},{4,5},{5,6},{6,7},{7,0},{8,9},{9,10},{10,1... | collective-permute-start | bytes 2924552 | tf_op jit(solution)/shard_map/ppermute | solution.py:354
  349.7 21.3 %all-to-all-start.8 = ((bf16[8,1,24,3584]{3,2,1,0:T(8,128)(2,1)}), bf16[8,1,24,3584]{3,2,1,0:T(8,128)(2,1)S(1)}, u32[]{:S(2)}, u32[]{:S(2)}) async-start(bf16[8,1,24,3584]{3,2,1,0:T(8,128)(2,1)} %slice_grad.7.refs_5_), calls=%async_computation.8 | async-start | bytes 2752512 | tf_op jit(solution)/shard_map/all_to_all | solution.py:350
  369.6 17.8 %collective-permute-start.12 = (bf16[136,3584]{1,0:T(8,128)(2,1)}, bf16[136,3584]{1,0:T(8,128)(2,1)S(1)}, u32[]{:S(2)}, u32[]{:S(2)}) collective-permute-start(bf16[136,3584]{1,0:T(8,128)(2,1)} %get-tuple-element.45), channel_id=1, source_target_pairs={{0,7},{1,0},{2,1},{3,2},{4,3},{5,4},{6,5},{7,6},{8,15},{9,8},{10,9... | collective-permute-start | bytes 2924552 | tf_op jit(solution)/shard_map/ppermute | solution.py:354
  370.8 19.0 %collective-permute-start.13 = (bf16[136,3584]{1,0:T(8,128)(2,1)}, bf16[136,3584]{1,0:T(8,128)(2,1)S(1)}, u32[]{:S(2)}, u32[]{:S(2)}) collective-permute-start(bf16[136,3584]{1,0:T(8,128)(2,1)} %get-tuple-element.46), channel_id=1, source_target_pairs={{0,1},{1,2},{2,3},{3,4},{4,5},{5,6},{6,7},{7,0},{8,9},{9,10},{10,1... | collective-permute-start | bytes 2924552 | tf_op jit(solution)/shard_map/ppermute | solution.py:354
  (20 other events, 75.6 us)

commit v4 on v3

--- a/solution.py
+++ b/solution.py
@@ -15,7 +15,7 @@
 LANES = 128
 META = 8
 TILE = 512
-VMEM_LIMIT = 56 * 1024 * 1024
+VMEM_LIMIT = 63 * 1024 * 1024
 
 f32 = jnp.float32
 bf16 = jnp.bfloat16
@@ -428,10 +428,11 @@
             part_rows = returned
         earlier = []
         if n > 0:
+            held = list(coming)
             if n == len(GROUPS) - 3:
                 down_grad = down_grads(received, hidden, width)
-                folded = list(folded) + [down_grad]
-            sending = slice_grad(first[n - 1], sides[n - 1], last, gate_up, folded)
+                held.append(down_grad)
+            sending = slice_grad(first[n - 1], sides[n - 1], last, gate_up, held)
             earlier = [sending]
         folded = fold(
             place(group),

time: 416 us -> 398 us (0.957)
  local copies, waits for them, and re-layouts: 21.2 us -> 7.65 us
    all_to_all x10, waiting for transfers between devices: 74.9 us -> 53.2 us  [exchange(): lax.all_to_all(block, 'column', split_axis=0, concat_axis=0, tiled=True)]
    ppermute x14, waiting for transfers between devices: 125 us -> 144 us  [hop(): lax.ppermute(block, 'depth', [(i, (i + distance) % DEPTH) for i in range(...]
    unnamed x38 -> x22, local copies, waits for them, and re-layouts: 14.5 us -> 3.44 us
  transfers between devices with their start and end apart: 26 -> 26, of which waited for: 24 -> 24; matrix products, arithmetic and copies ran while one was open for 3% -> 2% of each run, Pallas kernels for 20% -> 21%
where the time goes in v4:
time: 398 us; the launch traced here: 396 us
  waiting for transfers between devices  201 us (51%)
  Pallas kernels  98.6 us (25%)
  starting transfers between devices  79.2 us (20%)
  other arithmetic  8.9 us (2%)
  local copies, waits for them, and re-layouts  7.65 us (2%)
    ppermute x14, waiting for transfers between devices, hop(): lax.ppermute(block, 'depth', [(i, (i + distance) % DEPTH) for i in range(...  144 us
    all_to_all x10, starting transfers between devices, exchange(): lax.all_to_all(block, 'column', split_axis=0, concat_axis=0, tiled=True)  54.9 us
    all_to_all x10, waiting for transfers between devices, exchange(): lax.all_to_all(block, 'column', split_axis=0, concat_axis=0, tiled=True)  53.2 us
    pallas_call x4, Pallas kernels, slice_grad(): pl.pallas_call(functools.partial(grad_kernel, first), out_shape=jax.Shape...  22.9 us
    pallas_call x5, Pallas kernels, fold(): pl.pallas_call(functools.partial(fold_kernel, capacity, first, count, len...  19.5 us
    pallas_call x4, Pallas kernels, prepare(): pl.pallas_call(functools.partial(prepare_kernel, width), out_shape=[jax.S...  19.4 us
    pallas_call x5, Pallas kernels, pack(): pl.pallas_call(functools.partial(pack_kernel, capacity, len(arrivals), le...  18.8 us
    ppermute x14, starting transfers between devices, hop(): lax.ppermute(block, 'depth', [(i, (i + distance) % DEPTH) for i in range(...  14.3 us
  transfers between devices with their start and end apart: 26, of which 24 were waited for; matrix products, arithmetic and copies ran while one was open for 2% of the time, Pallas kernels for 21%

profile of v4, /device:TPU:1, one launch (start us, length us, event | category | flops | bytes accessed | tf_op | source)
XLA Modules:
  0.0 396.3 jit_solution(15218562462741091089)
XLA Ops:
  8.0 6.0 %all-to-all-start = ((bf16[8,1,24,3584]{3,2,1,0:T(8,128)(2,1)}), bf16[8,1,24,3584]{3,2,1,0:T(8,128)(2,1)}, u32[]{:S(2)}, u32[]{:S(2)}) async-start(bf16[8,1,24,3584]{3,2,1,0:T(8,128)(2,1)} %pack_rows.5), calls=%async_computation | async-start | bytes 2752512 | tf_op jit(solution)/shard_map/all_to_all | solution.py:350
  14.0 5.7 %collective-permute-start.4 = (bf16[136,3584]{1,0:T(8,128)(2,1)S(1)}, bf16[136,3584]{1,0:T(8,128)(2,1)S(1)}, u32[]{:S(2)}, u32[]{:S(2)}) collective-permute-start(bf16[136,3584]{1,0:T(8,128)(2,1)S(1)} %copy-done), channel_id=1, source_target_pairs={{0,7},{1,0},{2,1},{3,2},{4,3},{5,4},{6,5},{7,6},{8,15},{9,8},{10,9... | collective-permute-start | bytes 2924552 | tf_op jit(solution)/shard_map/ppermute | solution.py:354
  25.2 14.5 %collective-permute-done.4.refs_3_.refs_1_.refs_2_ = bf16[136,3584]{1,0:T(8,128)(2,1)S(1)} collective-permute-done((bf16[136,3584]{1,0:T(8,128)(2,1)S(1)}, bf16[136,3584]{1,0:T(8,128)(2,1)S(1)}, u32[]{:S(2)}, u32[]{:S(2)}) %collective-permute-start.4) | collective-permute-done | bytes 974880 | tf_op jit(solution)/shard_map/ppermute | solution.py:354
  58.3 14.2 %collective-permute-done.5.refs_1_.refs_5_.refs_2_ = bf16[136,3584]{1,0:T(8,128)(2,1)} collective-permute-done((bf16[136,3584]{1,0:T(8,128)(2,1)S(1)}, bf16[136,3584]{1,0:T(8,128)(2,1)}, u32[]{:S(2)}, u32[]{:S(2)}) %collective-permute-start.5) | collective-permute-done | bytes 974880 | tf_op jit(solution)/shard_map/ppermute | solution.py:354
  79.2 6.9 %all-to-all-done.3.rows.refs_1_ = bf16[8,2,24,3584]{3,2,1,0:T(8,128)(2,1)} async-done(((bf16[8,2,24,3584]{3,2,1,0:T(8,128)(2,1)}), bf16[8,2,24,3584]{3,2,1,0:T(8,128)(2,1)}, u32[]{:S(2)}, u32[]{:S(2)}) %all-to-all-start.3) | async-done | bytes 2752544 | tf_op jit(solution)/shard_map/all_to_all | solution.py:350
  97.8 15.4 %collective-permute-done.6.refs_7_.refs_1_.refs_2_ = bf16[136,3584]{1,0:T(8,128)(2,1)S(1)} collective-permute-done((bf16[136,3584]{1,0:T(8,128)(2,1)}, bf16[136,3584]{1,0:T(8,128)(2,1)S(1)}, u32[]{:S(2)}, u32[]{:S(2)}) %collective-permute-start.6) | collective-permute-done | bytes 974880 | tf_op jit(solution)/shard_map/ppermute | solution.py:354
  119.3 5.3 %all-to-all-done.1.rows.refs_2_ = bf16[8,2,24,3584]{3,2,1,0:T(8,128)(2,1)} async-done(((bf16[8,2,24,3584]{3,2,1,0:T(8,128)(2,1)}), bf16[8,2,24,3584]{3,2,1,0:T(8,128)(2,1)}, u32[]{:S(2)}, u32[]{:S(2)}) %all-to-all-start.1) | async-done | bytes 2752544 | tf_op jit(solution)/shard_map/all_to_all | solution.py:350
  124.6 8.9 %all-to-all-start.4 = ((bf16[8,2,24,3584]{3,2,1,0:T(8,128)(2,1)}), bf16[8,2,24,3584]{3,2,1,0:T(8,128)(2,1)}, u32[]{:S(2)}, u32[]{:S(2)}) async-start(bf16[8,2,24,3584]{3,2,1,0:T(8,128)(2,1)} %pack_rows.9), calls=%async_computation.4 | async-start | bytes 5505024 | tf_op jit(solution)/shard_map/all_to_all | solution.py:350
  139.2 16.8 %collective-permute-done.3.refs_0_.refs_8_.refs_1_ = bf16[136,3584]{1,0:T(8,128)(2,1)S(1)} collective-permute-done((bf16[136,3584]{1,0:T(8,128)(2,1)}, bf16[136,3584]{1,0:T(8,128)(2,1)S(1)}, u32[]{:S(2)}, u32[]{:S(2)}) %collective-permute-start.3) | collective-permute-done | bytes 974880 | tf_op jit(solution)/shard_map/ppermute | solution.py:354
  160.3 7.4 %all-to-all-done.4.rows.refs_3_ = bf16[8,2,24,3584]{3,2,1,0:T(8,128)(2,1)} async-done(((bf16[8,2,24,3584]{3,2,1,0:T(8,128)(2,1)}), bf16[8,2,24,3584]{3,2,1,0:T(8,128)(2,1)}, u32[]{:S(2)}, u32[]{:S(2)}) %all-to-all-start.4) | async-done | bytes 2752544 | tf_op jit(solution)/shard_map/all_to_all | solution.py:350
  171.9 5.1 %prepare.7 = (f32[2,192,512]{2,1,0:T(8,128)}, f32[2,192,256]{2,1,0:T(8,128)}, f32[2,192,128]{2,1,0:T(8,128)}) custom-call(s32[3]{0:T(128)} %pad_add_fusion.4.place, bf16[8,2,24,3584]{3,2,1,0:T(8,128)(2,1)} %all-to-all-done.4.rows.refs_3_, bf16[8,8,24,512]{3,2,1,0:T(8,128)(2,1)} %pad_maximum_fusion.preacts.refs_2_, bf16[256,3584]{1,0:T(8,128)(2,1)} %bitcast.37), custom_call_target="tpu_custom_call" | custom-call | tf_op jit(solution)/shard_map/prepare/pallas_call | solution.py:132
  177.1 14.8 %all-to-all-done.2.received.last.refs_4_ = bf16[8,1,24,3712]{3,2,1,0:T(8,128)(2,1)} async-done(((bf16[8,1,24,3712]{3,2,1,0:T(8,128)(2,1)}), bf16[8,1,24,3712]{3,2,1,0:T(8,128)(2,1)}, u32[]{:S(2)}, u32[]{:S(2)}) %all-to-all-start.2) | async-done | bytes 1425440 | tf_op jit(solution)/shard_map/all_to_all | solution.py:350
  191.8 7.6 %turn.1 = (f32[1,192,256]{2,1,0:T(8,128)}, bf16[8,1,24,3712]{3,2,1,0:T(8,128)(2,1)}) custom-call(s32[2]{0:T(128)} %pad_add_fusion.1.place, bf16[8,1,24,3712]{3,2,1,0:T(8,128)(2,1)} %all-to-all-done.2.received.last.refs_4_, bf16[8,8,24,512]{3,2,1,0:T(8,128)(2,1)} %pad_maximum_fusion.preacts.refs_2_, bf16[256,3584]{1,0:T(8,128)(2,1)} %bitcast.38, ...), custom_call_target="tpu_custom_call" | custom-call | tf_op jit(solution)/shard_map/turn/pallas_call | solution.py:187
  203.7 6.1 %slice_grad.4.refs_2_ = bf16[8,2,24,3584]{3,2,1,0:T(8,128)(2,1)} custom-call(f32[2,192,512]{2,1,0:T(8,128)} %get-tuple-element.35.sides, bf16[8,1,24,3712]{3,2,1,0:T(8,128)(2,1)} %all-to-all-done.2.received.last.refs_4_, bf16[3584,512]{1,0:T(8,128)(2,1)} %bitcast.30), custom_call_target="tpu_custom_call" | custom-call | tf_op jit(solution)/shard_map/slice_grad/pallas_call | solution.py:229
  209.8 13.8 %all-to-all-done.5.parts.refs_0_ = bf16[8,1,24,3712]{3,2,1,0:T(8,128)(2,1)} async-done(((bf16[8,1,24,3712]{3,2,1,0:T(8,128)(2,1)}), bf16[8,1,24,3712]{3,2,1,0:T(8,128)(2,1)}, u32[]{:S(2)}, u32[]{:S(2)}) %all-to-all-start.5) | async-done | bytes 1425440 | tf_op jit(solution)/shard_map/all_to_all | solution.py:350
  232.1 21.5 %collective-permute-done.7.rest_0_.refs_3_ = bf16[136,3584]{1,0:T(8,128)(2,1)S(1)} collective-permute-done((bf16[136,3584]{1,0:T(8,128)(2,1)}, bf16[136,3584]{1,0:T(8,128)(2,1)S(1)}, u32[]{:S(2)}, u32[]{:S(2)}) %collective-permute-start.7) | collective-permute-done | bytes 974880 | tf_op jit(solution)/shard_map/ppermute | solution.py:354
  254.5 6.1 %slice_grad.5.refs_4_ = bf16[8,2,24,3584]{3,2,1,0:T(8,128)(2,1)} custom-call(f32[2,192,512]{2,1,0:T(8,128)} %get-tuple-element.28.refs_9_.sides, bf16[8,1,24,3712]{3,2,1,0:T(8,128)(2,1)} %all-to-all-done.2.received.last.refs_4_, bf16[3584,512]{1,0:T(8,128)(2,1)} %bitcast.31, bf16[136,3584]{1,0:T(8,128)(2,1)} %copy-done.7), custom_call_target="tpu_custom_call" | custom-call | tf_op jit(solution)/shard_map/slice_grad/pallas_call | solution.py:229
  262.2 9.0 %all-to-all-start.6 = ((bf16[8,2,24,3584]{3,2,1,0:T(8,128)(2,1)}), bf16[8,2,24,3584]{3,2,1,0:T(8,128)(2,1)}, u32[]{:S(2)}, u32[]{:S(2)}) async-start(bf16[8,2,24,3584]{3,2,1,0:T(8,128)(2,1)} %slice_grad.5.refs_4_), calls=%async_computation.6 | async-start | bytes 5505024 | tf_op jit(solution)/shard_map/all_to_all | solution.py:350
  276.9 10.3 %down_grads.1.rest_2_ = bf16[256,3584]{1,0:T(8,128)(2,1)} custom-call(bf16[8,1,24,3712]{3,2,1,0:T(8,128)(2,1)} %all-to-all-done.2.received.last.refs_4_, bf16[8,1,24,3584]{3,2,1,0:T(8,128)(2,1)} %all-to-all-done.rows.refs_0_, bf16[8,2,24,3584]{3,2,1,0:T(8,128)(2,1)} %all-to-all-done.3.rows.refs_1_, bf16[8,2,24,3584]{3,2,1,0:T(8,128)(2,1)} %all-to-all-done.1.rows.refs_2_, ...), custom_call_target="tpu_custom_call" | custom-call | tf_op jit(solution)/shard_map/down_grads/pallas_call | solution.py:274
  287.1 9.6 %collective-permute-done.8.rest_0_.refs_3_ = bf16[136,3584]{1,0:T(8,128)(2,1)S(1)} collective-permute-done((bf16[136,3584]{1,0:T(8,128)(2,1)}, bf16[136,3584]{1,0:T(8,128)(2,1)S(1)}, u32[]{:S(2)}, u32[]{:S(2)}) %collective-permute-start.8) | collective-permute-done | bytes 974880 | tf_op jit(solution)/shard_map/ppermute | solution.py:354
  298.8 6.1 %slice_grad.6.refs_5_ = bf16[8,2,24,3584]{3,2,1,0:T(8,128)(2,1)} custom-call(f32[2,192,512]{2,1,0:T(8,128)} %get-tuple-element.32.refs_2_.sides, bf16[8,1,24,3712]{3,2,1,0:T(8,128)(2,1)} %all-to-all-done.2.received.last.refs_4_, bf16[3584,512]{1,0:T(8,128)(2,1)} %bitcast.32, bf16[136,3584]{1,0:T(8,128)(2,1)} %copy-done.5, ...), custom_call_target="tpu_custom_call" | custom-call | tf_op jit(solution)/shard_map/slice_grad/pallas_call | solution.py:229
  315.6 18.1 %collective-permute-done.10.rest_0_.refs_3_ = bf16[136,3584]{1,0:T(8,128)(2,1)S(1)} collective-permute-done((bf16[136,3584]{1,0:T(8,128)(2,1)}, bf16[136,3584]{1,0:T(8,128)(2,1)S(1)}, u32[]{:S(2)}, u32[]{:S(2)}) %collective-permute-start.10) | collective-permute-done | bytes 974880 | tf_op jit(solution)/shard_map/ppermute | solution.py:354
  354.1 19.2 %collective-permute-done.12.refs_2_ = bf16[136,3584]{1,0:T(8,128)(2,1)S(1)} collective-permute-done((bf16[136,3584]{1,0:T(8,128)(2,1)}, bf16[136,3584]{1,0:T(8,128)(2,1)S(1)}, u32[]{:S(2)}, u32[]{:S(2)}) %collective-permute-start.12) | collective-permute-done | bytes 974880 | tf_op jit(solution)/shard_map/ppermute | solution.py:354
  379.0 5.6 %collective-permute-start.14 = (bf16[64,3584]{1,0:T(8,128)(2,1)}, bf16[64,3584]{1,0:T(8,128)(2,1)S(1)}, u32[]{:S(2)}, u32[]{:S(2)}) collective-permute-start(bf16[64,3584]{1,0:T(8,128)(2,1)} %get-tuple-element.47), channel_id=1, source_target_pairs={{64,0},{128,64},{192,128},{65,1},{129,65},{193,129},{66,2},{130,66... | collective-permute-start | bytes 1376264 | tf_op jit(solution)/shard_map/ppermute | solution.py:360
  (89 shorter events, 141.8 us)
Async XLA Ops:
  8.0 39.0 %all-to-all-start = ((bf16[8,1,24,3584]{3,2,1,0:T(8,128)(2,1)}), bf16[8,1,24,3584]{3,2,1,0:T(8,128)(2,1)}, u32[]{:S(2)}, u32[]{:S(2)}) async-start(bf16[8,1,24,3584]{3,2,1,0:T(8,128)(2,1)} %pack_rows.5), calls=%async_computation | async-start | bytes 2752512 | tf_op jit(solution)/shard_map/all_to_all | solution.py:350
  14.0 25.6 %collective-permute-start.4 = (bf16[136,3584]{1,0:T(8,128)(2,1)S(1)}, bf16[136,3584]{1,0:T(8,128)(2,1)S(1)}, u32[]{:S(2)}, u32[]{:S(2)}) collective-permute-start(bf16[136,3584]{1,0:T(8,128)(2,1)S(1)} %copy-done), channel_id=1, source_target_pairs={{0,7},{1,0},{2,1},{3,2},{4,3},{5,4},{6,5},{7,6},{8,15},{9,8},{10,9... | collective-permute-start | bytes 2924552 | tf_op jit(solution)/shard_map/ppermute | solution.py:354
  19.7 23.2 %collective-permute-start = (bf16[136,3584]{1,0:T(8,128)(2,1)S(1)}, bf16[136,3584]{1,0:T(8,128)(2,1)}, u32[]{:S(2)}, u32[]{:S(2)}) collective-permute-start(bf16[136,3584]{1,0:T(8,128)(2,1)S(1)} %copy-done), channel_id=1, source_target_pairs={{0,1},{1,2},{2,3},{3,4},{4,5},{5,6},{6,7},{7,0},{8,9},{9,10},{10,1... | collective-permute-start | bytes 2924552 | tf_op jit(solution)/shard_map/ppermute | solution.py:354
  47.0 39.1 %all-to-all-start.3 = ((bf16[8,2,24,3584]{3,2,1,0:T(8,128)(2,1)}), bf16[8,2,24,3584]{3,2,1,0:T(8,128)(2,1)}, u32[]{:S(2)}, u32[]{:S(2)}) async-start(bf16[8,2,24,3584]{3,2,1,0:T(8,128)(2,1)} %pack_rows.8), calls=%async_computation.3 | async-start | bytes 5505024 | tf_op jit(solution)/shard_map/all_to_all | solution.py:350
  52.0 20.5 %collective-permute-start.5 = (bf16[136,3584]{1,0:T(8,128)(2,1)S(1)}, bf16[136,3584]{1,0:T(8,128)(2,1)}, u32[]{:S(2)}, u32[]{:S(2)}) collective-permute-start(bf16[136,3584]{1,0:T(8,128)(2,1)S(1)} %copy-done.2), channel_id=1, source_target_pairs={{0,7},{1,0},{2,1},{3,2},{4,3},{5,4},{6,5},{7,6},{8,15},{9,8},{10,9... | collective-permute-start | bytes 2924552 | tf_op jit(solution)/shard_map/ppermute | solution.py:354
  53.1 21.9 %collective-permute-start.1 = (bf16[136,3584]{1,0:T(8,128)(2,1)}, bf16[136,3584]{1,0:T(8,128)(2,1)}, u32[]{:S(2)}, u32[]{:S(2)}) collective-permute-start(bf16[136,3584]{1,0:T(8,128)(2,1)} %collective-permute-done.refs_2_.refs_0_.refs_1_), channel_id=1, source_target_pairs={{0,1},{1,2},{2,3},{3,4},{4,5},{5,6},{6,7},{7,0},{8,9},{9,10},{10,1... | collective-permute-start | bytes 2924552 | tf_op jit(solution)/shard_map/ppermute | solution.py:354
  86.1 38.5 %all-to-all-start.1 = ((bf16[8,2,24,3584]{3,2,1,0:T(8,128)(2,1)}), bf16[8,2,24,3584]{3,2,1,0:T(8,128)(2,1)}, u32[]{:S(2)}, u32[]{:S(2)}) async-start(bf16[8,2,24,3584]{3,2,1,0:T(8,128)(2,1)} %pack_rows.6), calls=%async_computation.1 | async-start | bytes 5505024 | tf_op jit(solution)/shard_map/all_to_all | solution.py:350
  90.5 22.6 %collective-permute-start.6 = (bf16[136,3584]{1,0:T(8,128)(2,1)}, bf16[136,3584]{1,0:T(8,128)(2,1)S(1)}, u32[]{:S(2)}, u32[]{:S(2)}) collective-permute-start(bf16[136,3584]{1,0:T(8,128)(2,1)} %collective-permute-done.5.refs_1_.refs_5_.refs_2_), channel_id=1, source_target_pairs={{0,7},{1,0},{2,1},{3,2},{4,3},{5,4},{6,5},{7,6},{8,15},{9,8},{10,9... | collective-permute-start | bytes 2924552 | tf_op jit(solution)/shard_map/ppermute | solution.py:354
  91.7 23.5 %collective-permute-start.2 = (bf16[136,3584]{1,0:T(8,128)(2,1)}, bf16[136,3584]{1,0:T(8,128)(2,1)}, u32[]{:S(2)}, u32[]{:S(2)}) collective-permute-start(bf16[136,3584]{1,0:T(8,128)(2,1)} %collective-permute-done.1.refs_0_.refs_4_.refs_1_), channel_id=1, source_target_pairs={{0,1},{1,2},{2,3},{3,4},{4,5},{5,6},{6,7},{7,0},{8,9},{9,10},{10,1... | collective-permute-start | bytes 2924552 | tf_op jit(solution)/shard_map/ppermute | solution.py:354
  124.6 43.0 %all-to-all-start.4 = ((bf16[8,2,24,3584]{3,2,1,0:T(8,128)(2,1)}), bf16[8,2,24,3584]{3,2,1,0:T(8,128)(2,1)}, u32[]{:S(2)}, u32[]{:S(2)}) async-start(bf16[8,2,24,3584]{3,2,1,0:T(8,128)(2,1)} %pack_rows.9), calls=%async_computation.4 | async-start | bytes 5505024 | tf_op jit(solution)/shard_map/all_to_all | solution.py:350
  133.5 22.5 %collective-permute-start.3 = (bf16[136,3584]{1,0:T(8,128)(2,1)}, bf16[136,3584]{1,0:T(8,128)(2,1)S(1)}, u32[]{:S(2)}, u32[]{:S(2)}) collective-permute-start(bf16[136,3584]{1,0:T(8,128)(2,1)} %collective-permute-done.2.refs_6_.refs_0_.refs_1_), channel_id=1, source_target_pairs={{0,1},{1,2},{2,3},{3,4},{4,5},{5,6},{6,7},{7,0},{8,9},{9,10},{10,1... | collective-permute-start | bytes 2924552 | tf_op jit(solution)/shard_map/ppermute | solution.py:354
  167.7 24.1 %all-to-all-start.2 = ((bf16[8,1,24,3712]{3,2,1,0:T(8,128)(2,1)}), bf16[8,1,24,3712]{3,2,1,0:T(8,128)(2,1)}, u32[]{:S(2)}, u32[]{:S(2)}) async-start(bf16[8,1,24,3712]{3,2,1,0:T(8,128)(2,1)} %pack_rows.7), calls=%async_computation.2 | async-start | bytes 2850816 | tf_op jit(solution)/shard_map/all_to_all | solution.py:350
  199.4 24.2 %all-to-all-start.5 = ((bf16[8,1,24,3712]{3,2,1,0:T(8,128)(2,1)}), bf16[8,1,24,3712]{3,2,1,0:T(8,128)(2,1)}, u32[]{:S(2)}, u32[]{:S(2)}) async-start(bf16[8,1,24,3712]{3,2,1,0:T(8,128)(2,1)} %get-tuple-element.34), calls=%async_computation.5 | async-start | bytes 2850816 | tf_op jit(solution)/shard_map/all_to_all | solution.py:350
  223.6 38.6 %all-to-all-start.7 = ((bf16[8,2,24,3584]{3,2,1,0:T(8,128)(2,1)}), bf16[8,2,24,3584]{3,2,1,0:T(8,128)(2,1)}, u32[]{:S(2)}, u32[]{:S(2)}) async-start(bf16[8,2,24,3584]{3,2,1,0:T(8,128)(2,1)} %slice_grad.4.refs_2_), calls=%async_computation.7 | async-start | bytes 5505024 | tf_op jit(solution)/shard_map/all_to_all | solution.py:350
  231.0 22.6 %collective-permute-start.7 = (bf16[136,3584]{1,0:T(8,128)(2,1)}, bf16[136,3584]{1,0:T(8,128)(2,1)S(1)}, u32[]{:S(2)}, u32[]{:S(2)}) collective-permute-start(bf16[136,3584]{1,0:T(8,128)(2,1)} %fold_rows.5), channel_id=1, source_target_pairs={{0,7},{1,0},{2,1},{3,2},{4,3},{5,4},{6,5},{7,6},{8,15},{9,8},{10,9... | collective-permute-start | bytes 2924552 | tf_op jit(solution)/shard_map/ppermute | solution.py:354
  262.2 43.2 %all-to-all-start.6 = ((bf16[8,2,24,3584]{3,2,1,0:T(8,128)(2,1)}), bf16[8,2,24,3584]{3,2,1,0:T(8,128)(2,1)}, u32[]{:S(2)}, u32[]{:S(2)}) async-start(bf16[8,2,24,3584]{3,2,1,0:T(8,128)(2,1)} %slice_grad.5.refs_4_), calls=%async_computation.6 | async-start | bytes 5505024 | tf_op jit(solution)/shard_map/all_to_all | solution.py:350
  275.4 21.3 %collective-permute-start.8 = (bf16[136,3584]{1,0:T(8,128)(2,1)}, bf16[136,3584]{1,0:T(8,128)(2,1)S(1)}, u32[]{:S(2)}, u32[]{:S(2)}) collective-permute-start(bf16[136,3584]{1,0:T(8,128)(2,1)} %get-tuple-element.36), channel_id=1, source_target_pairs={{0,7},{1,0},{2,1},{3,2},{4,3},{5,4},{6,5},{7,6},{8,15},{9,8},{10,9... | collective-permute-start | bytes 2924552 | tf_op jit(solution)/shard_map/ppermute | solution.py:354
  276.5 22.3 %collective-permute-start.9 = (bf16[136,3584]{1,0:T(8,128)(2,1)}, bf16[136,3584]{1,0:T(8,128)(2,1)}, u32[]{:S(2)}, u32[]{:S(2)}) collective-permute-start(bf16[136,3584]{1,0:T(8,128)(2,1)} %get-tuple-element.37), channel_id=1, source_target_pairs={{0,1},{1,2},{2,3},{3,4},{4,5},{5,6},{6,7},{7,0},{8,9},{9,10},{10,1... | collective-permute-start | bytes 2924552 | tf_op jit(solution)/shard_map/ppermute | solution.py:354
  305.3 38.5 %all-to-all-start.9 = ((bf16[8,2,24,3584]{3,2,1,0:T(8,128)(2,1)}), bf16[8,2,24,3584]{3,2,1,0:T(8,128)(2,1)}, u32[]{:S(2)}, u32[]{:S(2)}) async-start(bf16[8,2,24,3584]{3,2,1,0:T(8,128)(2,1)} %slice_grad.6.refs_5_), calls=%async_computation.9 | async-start | bytes 5505024 | tf_op jit(solution)/shard_map/all_to_all | solution.py:350
  314.2 19.6 %collective-permute-start.10 = (bf16[136,3584]{1,0:T(8,128)(2,1)}, bf16[136,3584]{1,0:T(8,128)(2,1)S(1)}, u32[]{:S(2)}, u32[]{:S(2)}) collective-permute-start(bf16[136,3584]{1,0:T(8,128)(2,1)} %get-tuple-element.43), channel_id=1, source_target_pairs={{0,7},{1,0},{2,1},{3,2},{4,3},{5,4},{6,5},{7,6},{8,15},{9,8},{10,9... | collective-permute-start | bytes 2924552 | tf_op jit(solution)/shard_map/ppermute | solution.py:354
  315.3 20.8 %collective-permute-start.11 = (bf16[136,3584]{1,0:T(8,128)(2,1)}, bf16[136,3584]{1,0:T(8,128)(2,1)}, u32[]{:S(2)}, u32[]{:S(2)}) collective-permute-start(bf16[136,3584]{1,0:T(8,128)(2,1)} %get-tuple-element.44), channel_id=1, source_target_pairs={{0,1},{1,2},{2,3},{3,4},{4,5},{5,6},{6,7},{7,0},{8,9},{9,10},{10,1... | collective-permute-start | bytes 2924552 | tf_op jit(solution)/shard_map/ppermute | solution.py:354
  343.9 31.6 %all-to-all-start.8 = ((bf16[8,1,24,3584]{3,2,1,0:T(8,128)(2,1)}), bf16[8,1,24,3584]{3,2,1,0:T(8,128)(2,1)}, u32[]{:S(2)}, u32[]{:S(2)}) async-start(bf16[8,1,24,3584]{3,2,1,0:T(8,128)(2,1)} %slice_grad.7.refs_5_), calls=%async_computation.8 | async-start | bytes 2752512 | tf_op jit(solution)/shard_map/all_to_all | solution.py:350
  352.6 20.7 %collective-permute-start.12 = (bf16[136,3584]{1,0:T(8,128)(2,1)}, bf16[136,3584]{1,0:T(8,128)(2,1)S(1)}, u32[]{:S(2)}, u32[]{:S(2)}) collective-permute-start(bf16[136,3584]{1,0:T(8,128)(2,1)} %get-tuple-element.45), channel_id=1, source_target_pairs={{0,7},{1,0},{2,1},{3,2},{4,3},{5,4},{6,5},{7,6},{8,15},{9,8},{10,9... | collective-permute-start | bytes 2924552 | tf_op jit(solution)/shard_map/ppermute | solution.py:354
  353.7 21.8 %collective-permute-start.13 = (bf16[136,3584]{1,0:T(8,128)(2,1)}, bf16[136,3584]{1,0:T(8,128)(2,1)}, u32[]{:S(2)}, u32[]{:S(2)}) collective-permute-start(bf16[136,3584]{1,0:T(8,128)(2,1)} %get-tuple-element.46), channel_id=1, source_target_pairs={{0,1},{1,2},{2,3},{3,4},{4,5},{5,6},{6,7},{7,0},{8,9},{9,10},{10,1... | collective-permute-start | bytes 2924552 | tf_op jit(solution)/shard_map/ppermute | solution.py:354
  (12 other events, 61.0 us)

commit v5 on v4

--- a/solution.py
+++ b/solution.py
@@ -224,22 +224,35 @@
 
 def slice_grad(first, sides, last, gate_up, earlier):
     count, slots, full = sides.shape
-    columns, _, span, wide = last.shape
+    columns, _, span, _ = last.shape
     width = gate_up.shape[0]
+    shape = jax.ShapeDtypeStruct((columns, count, span, width), bf16)
+    most = width - TILE
+    shared = [
+        pl.BlockSpec((1, slots, full), lambda m: (m, 0, 0)),
+        pl.BlockSpec((columns, 1, span, EXTRA), lambda m: (0, 0, 0, width // EXTRA)),
+    ]
+    sending = pl.pallas_call(
+        functools.partial(grad_kernel, first),
+        out_shape=shape,
+        grid=(count,),
+        in_specs=shared + [pl.BlockSpec((most, full), lambda m: (0, 0))],
+        out_specs=pl.BlockSpec((columns, 1, span, most), lambda m: (0, m, 0, 0)),
+        compiler_params=params(),
+        name="slice_grad",
+    )(sides, last, gate_up)
     return pl.pallas_call(
         functools.partial(grad_kernel, first),
-        out_shape=jax.ShapeDtypeStruct((columns, count, span, width), bf16),
+        out_shape=shape,
         grid=(count,),
-        in_specs=[
-            pl.BlockSpec((1, slots, full), lambda m: (m, 0, 0)),
-            pl.BlockSpec((columns, 1, span, EXTRA), lambda m: (0, 0, 0, width // EXTRA)),
-            pl.BlockSpec((width, full), lambda m: (0, 0)),
-        ]
+        in_specs=shared
+        + [pl.BlockSpec((TILE, full), lambda m: (most // TILE, 0)), ANY]
         + [ANY] * len(earlier),
-        out_specs=pl.BlockSpec((columns, 1, span, width), lambda m: (0, m, 0, 0)),
-        compiler_params=params(),
-        name="slice_grad",
-    )(sides, last, gate_up, *earlier)
+        out_specs=pl.BlockSpec((columns, 1, span, TILE), lambda m: (0, m, 0, most // TILE)),
+        input_output_aliases={3: 0},
+        compiler_params=params(),
+        name="slice_grad_end",
+    )(sides, last, gate_up, sending, *earlier)
 
 
 def down_kernel(groups, last, *refs):
@@ -285,11 +298,11 @@
     )(last, *received, *hidden)
 
 
-def fold_kernel(capacity, first, count, coming, final, place, parts, *refs):
+def fold_kernel(capacity, first, count, coming, split, place, parts, *refs):
     returned = refs[0]
     metas = refs[1 : 1 + count]
     incoming = refs[1 + count : 1 + count + coming]
-    outs = refs[-3:] if final else refs[-count:]
+    outs = refs[-3 * count :] if split else refs[-count:]
     columns, _, span, _ = returned.shape
     slots = columns * span
     table = parts[:, 0].astype(f32)
@@ -298,16 +311,17 @@
         picks = [meta[0:1, i * LANES : (i + 1) * LANES] for i in range(4)]
         hits, ids = slot_hits(picks, place[0], columns, capacity)
         ones = flat(hits)
-        added = list(incoming) if final else list(incoming[m : m + 1])
+        added = incoming[m::count] if coming >= count else incoming[m : m + 1]
+        sums = [other for other in added if other.shape[0] > META]
         for tile in tiles(returned.shape[3] // TILE * TILE):
             rows = returned[:, m, :, tile].reshape(slots, TILE)
             total = lax.dot_general(ones, rows, TN, preferred_element_type=f32)
-            for other in added:
+            for other in sums:
                 total = total + other[:LANES, tile].astype(f32)
             total = total.astype(bf16)
-            if final:
-                outs[0][:, tile] = total[:HALF]
-                outs[1][:, tile] = total[HALF:]
+            if split:
+                outs[3 * m][:, tile] = total[:HALF]
+                outs[3 * m + 1][:, tile] = total[HALF:]
             else:
                 outs[m][:LANES, tile] = total
         values = hits * table[:, :, first + m : first + m + 1]
@@ -316,24 +330,26 @@
             line = jnp.sum(jnp.sum(values * named, axis=1), axis=0, keepdims=True)
             lanes = slice(k * LANES, (k + 1) * LANES)
             for other in added:
-                line = line + other[LANES : LANES + META, lanes].astype(f32)[0:1]
-            if final:
-                outs[2][:, lanes] = jnp.broadcast_to(line, (META, LANES))
+                low = LANES if other.shape[0] > META else 0
+                line = line + other[low : low + META, lanes].astype(f32)[0:1]
+            line = jnp.broadcast_to(line, (META, LANES)).astype(bf16)
+            if split:
+                outs[3 * m + 2][:, lanes] = line
             else:
-                outs[m][LANES : LANES + META, lanes] = jnp.broadcast_to(line, (META, LANES)).astype(bf16)
-
-
-def fold(place, first, parts, returned, arrivals, incoming, capacity, final, earlier=()):
+                outs[m][LANES : LANES + META, lanes] = line
+
+
+def fold(place, first, parts, returned, arrivals, incoming, capacity, split, earlier=()):
     columns, count, span, _ = returned.shape
     width = arrivals[0].shape[1]
     only_tags = pl.BlockSpec((META, 4 * LANES), lambda i: (LANES // META, 0))
-    if final:
-        shapes = [jax.ShapeDtypeStruct((HALF, width), bf16)] * 2
-        shapes.append(jax.ShapeDtypeStruct((META, 2 * LANES), f32))
+    if split:
+        halves = [jax.ShapeDtypeStruct((HALF, width), bf16)] * 2
+        shapes = (halves + [jax.ShapeDtypeStruct((META, 2 * LANES), bf16)]) * count
     else:
         shapes = [jax.ShapeDtypeStruct((LANES + META, width), bf16)] * count
     return pl.pallas_call(
-        functools.partial(fold_kernel, capacity, first, count, len(incoming), final),
+        functools.partial(fold_kernel, capacity, first, count, len(incoming), split),
         out_shape=shapes,
         grid=(1,),
         in_specs=[SMEM, pl.BlockSpec((columns, 1, span, EXTRA), lambda i: (0, 0, 0, width // EXTRA)), VMEM]
@@ -354,10 +370,15 @@
     return lax.ppermute(block, "depth", [(i, (i + distance) % DEPTH) for i in range(DEPTH)])
 
 
-def shifted(block, distance):
-    devices = range(lax.axis_size("section"))
-    route = [(i - distance, i) for i in devices if i - distance in devices]
-    return lax.ppermute(block, "section", route)
+def shifted(block, distance, along=0):
+    sections = lax.axis_size("section")
+    route = [
+        (i * DEPTH + z, (i + distance) * DEPTH + (z + along) % DEPTH)
+        for i in range(sections)
+        for z in range(DEPTH)
+        if 0 <= i + distance < sections
+    ]
+    return lax.ppermute(block, ("section", "depth"), route)
 
 
 def shards(grad_out, gate_probs, routes, saved_preacts, w_gate_up, w_down):
@@ -442,14 +463,22 @@
             [arrivals[offset] for offset in group],
             coming,
             capacity,
-            n == 0,
+            n <= 1,
             earlier,
         )
-        if n > 0:
-            coming = [hop(block, -1 if offset < 0 else 1) for block, offset in zip(folded, group)]
-    above, below, probs = folded
-    prob_grad = jnp.moveaxis(probs[0].reshape(2, 2, tokens), 0, 2)
-    return (shifted(above, -1)[None], shifted(below, 1)[None], prob_grad[None], down_grad[None, None])
+        along = [-1 if offset < 0 else 1 for offset in group]
+        if n > 1:
+            coming = [hop(block, way) for block, way in zip(folded, along)]
+        elif n == 1:
+            coming = [hop(folded[3 * m + 2], way) for m, way in enumerate(along)]
+            above = [shifted(folded[3 * m], -1, way) for m, way in enumerate(along)]
+            below = [shifted(folded[3 * m + 1], 1, way) for m, way in enumerate(along)]
+    above.append(shifted(folded[0], -1))
+    below.append(shifted(folded[1], 1))
+    from_above = sum(part.astype(f32) for part in above).astype(bf16)
+    from_below = sum(part.astype(f32) for part in below).astype(bf16)
+    prob_grad = jnp.moveaxis(folded[2][0].astype(f32).reshape(2, 2, tokens), 0, 2)
+    return (from_above[None], from_below[None], prob_grad[None], down_grad[None, None])
 
 
 def solution(mesh):

time: 398 us -> 398 us (level)
  waiting for transfers between devices: 201 us -> 164 us
  starting transfers between devices: 79.2 us -> 107 us
  Pallas kernels: 98.6 us -> 106 us
    ppermute x14, waiting for transfers between devices: 144 us -> 102 us  [hop(): lax.ppermute(block, 'depth', [(i, (i + distance) % DEPTH) for i in range(...]
    ppermute x14, starting transfers between devices: 14.3 us -> 32.7 us  [hop(): lax.ppermute(block, 'depth', [(i, (i + distance) % DEPTH) for i in range(...]
    ppermute x2 -> x6, starting transfers between devices: 10 us -> 22.8 us  [shifted(): return lax.ppermute(block, ('section', 'depth'), route)]
    ppermute x2 -> x6, waiting for transfers between devices: 4.33 us -> 14 us  [shifted(): return lax.ppermute(block, ('section', 'depth'), route)]
    pallas_call x4 -> x8, Pallas kernels: 22.9 us -> 31 us  [slice_grad(): pl.pallas_call(functools.partial(grad_kernel, first), out_shape=shape, gr...]
    all_to_all x10, waiting for transfers between devices: 53.2 us -> 47.9 us  [exchange(): lax.all_to_all(block, 'column', split_axis=0, concat_axis=0, tiled=True)]
  transfers between devices with their start and end apart: 26 -> 30, of which waited for: 24 -> 19; matrix products, arithmetic and copies ran while one was open for 2% -> 2% of each run, Pallas kernels for 21% -> 24%
where the time goes in v5:
time: 398 us; the launch traced here: 396 us
  waiting for transfers between devices  164 us (41%)
  starting transfers between devices  107 us (27%)
  Pallas kernels  106 us (27%)
  other arithmetic  11.4 us (3%)
  local copies, waits for them, and re-layouts  6.91 us (2%)
    ppermute x14, waiting for transfers between devices, hop(): lax.ppermute(block, 'depth', [(i, (i + distance) % DEPTH) for i in range(...  102 us
    all_to_all x10, starting transfers between devices, exchange(): lax.all_to_all(block, 'column', split_axis=0, concat_axis=0, tiled=True)  51.7 us
    all_to_all x10, waiting for transfers between devices, exchange(): lax.all_to_all(block, 'column', split_axis=0, concat_axis=0, tiled=True)  47.9 us
    ppermute x14, starting transfers between devices, hop(): lax.ppermute(block, 'depth', [(i, (i + distance) % DEPTH) for i in range(...  32.7 us
    pallas_call x8, Pallas kernels, slice_grad(): pl.pallas_call(functools.partial(grad_kernel, first), out_shape=shape, gr...  31 us
    ppermute x6, starting transfers between devices, shifted(): return lax.ppermute(block, ('section', 'depth'), route)  22.8 us
    pallas_call x4, Pallas kernels, prepare(): pl.pallas_call(functools.partial(prepare_kernel, width), out_shape=[jax.S...  19.5 us
    pallas_call x5, Pallas kernels, pack(): pl.pallas_call(functools.partial(pack_kernel, capacity, len(arrivals), le...  18.9 us
  transfers between devices with their start and end apart: 30, of which 19 were waited for; matrix products, arithmetic and copies ran while one was open for 2% of the time, Pallas kernels for 24%

profile of v5, /device:TPU:1, one launch (start us, length us, event | category | flops | bytes accessed | tf_op | source)
XLA Modules:
  0.0 396.4 jit_solution(7772866975124710074)
XLA Ops:
  8.0 6.0 %all-to-all-start = ((bf16[8,1,24,3584]{3,2,1,0:T(8,128)(2,1)}), bf16[8,1,24,3584]{3,2,1,0:T(8,128)(2,1)}, u32[]{:S(2)}, u32[]{:S(2)}) async-start(bf16[8,1,24,3584]{3,2,1,0:T(8,128)(2,1)} %pack_rows.5), calls=%async_computation | async-start | bytes 2752512 | tf_op jit(solution)/shard_map/all_to_all | solution.py:366
  25.2 15.4 %collective-permute-done.refs_2_.refs_0_.refs_1_ = bf16[136,3584]{1,0:T(8,128)(2,1)S(1)} collective-permute-done((bf16[136,3584]{1,0:T(8,128)(2,1)S(1)}, bf16[136,3584]{1,0:T(8,128)(2,1)S(1)}, u32[]{:S(2)}, u32[]{:S(2)}) %collective-permute-start) | collective-permute-done | bytes 974880 | tf_op jit(solution)/shard_map/ppermute | solution.py:370
  58.1 14.8 %collective-permute-done.1.refs_0_.refs_4_.refs_1_ = bf16[136,3584]{1,0:T(8,128)(2,1)} collective-permute-done((bf16[136,3584]{1,0:T(8,128)(2,1)S(1)}, bf16[136,3584]{1,0:T(8,128)(2,1)}, u32[]{:S(2)}, u32[]{:S(2)}) %collective-permute-start.1) | collective-permute-done | bytes 974880 | tf_op jit(solution)/shard_map/ppermute | solution.py:370
  77.2 7.6 %all-to-all-done.3.rows.refs_1_ = bf16[8,2,24,3584]{3,2,1,0:T(8,128)(2,1)} async-done(((bf16[8,2,24,3584]{3,2,1,0:T(8,128)(2,1)}), bf16[8,2,24,3584]{3,2,1,0:T(8,128)(2,1)}, u32[]{:S(2)}, u32[]{:S(2)}) %all-to-all-start.3) | async-done | bytes 2752544 | tf_op jit(solution)/shard_map/all_to_all | solution.py:366
  97.7 14.8 %collective-permute-done.2.refs_6_.refs_0_.refs_1_ = bf16[136,3584]{1,0:T(8,128)(2,1)S(1)} collective-permute-done((bf16[136,3584]{1,0:T(8,128)(2,1)}, bf16[136,3584]{1,0:T(8,128)(2,1)S(1)}, u32[]{:S(2)}, u32[]{:S(2)}) %collective-permute-start.2) | collective-permute-done | bytes 974880 | tf_op jit(solution)/shard_map/ppermute | solution.py:370
  117.6 5.7 %all-to-all-done.1.rows.refs_2_ = bf16[8,2,24,3584]{3,2,1,0:T(8,128)(2,1)} async-done(((bf16[8,2,24,3584]{3,2,1,0:T(8,128)(2,1)}), bf16[8,2,24,3584]{3,2,1,0:T(8,128)(2,1)}, u32[]{:S(2)}, u32[]{:S(2)}) %all-to-all-start.1) | async-done | bytes 2752544 | tf_op jit(solution)/shard_map/all_to_all | solution.py:366
  123.3 5.3 %all-to-all-start.4 = ((bf16[8,2,24,3584]{3,2,1,0:T(8,128)(2,1)}), bf16[8,2,24,3584]{3,2,1,0:T(8,128)(2,1)}, u32[]{:S(2)}, u32[]{:S(2)}) async-start(bf16[8,2,24,3584]{3,2,1,0:T(8,128)(2,1)} %pack_rows.9), calls=%async_computation.4 | async-start | bytes 5505024 | tf_op jit(solution)/shard_map/all_to_all | solution.py:366
  136.2 17.8 %collective-permute-done.3.refs_0_.refs_8_.refs_1_ = bf16[136,3584]{1,0:T(8,128)(2,1)} collective-permute-done((bf16[136,3584]{1,0:T(8,128)(2,1)S(1)}, bf16[136,3584]{1,0:T(8,128)(2,1)}, u32[]{:S(2)}, u32[]{:S(2)}) %collective-permute-start.3) | collective-permute-done | bytes 974880 | tf_op jit(solution)/shard_map/ppermute | solution.py:370
  157.4 5.4 %all-to-all-done.4.rows.refs_3_ = bf16[8,2,24,3584]{3,2,1,0:T(8,128)(2,1)} async-done(((bf16[8,2,24,3584]{3,2,1,0:T(8,128)(2,1)}), bf16[8,2,24,3584]{3,2,1,0:T(8,128)(2,1)}, u32[]{:S(2)}, u32[]{:S(2)}) %all-to-all-start.4) | async-done | bytes 2752544 | tf_op jit(solution)/shard_map/all_to_all | solution.py:366
  167.1 5.2 %prepare.7 = (f32[2,192,512]{2,1,0:T(8,128)}, f32[2,192,256]{2,1,0:T(8,128)}, f32[2,192,128]{2,1,0:T(8,128)}) custom-call(s32[3]{0:T(128)} %pad_add_fusion.4.place, bf16[8,2,24,3584]{3,2,1,0:T(8,128)(2,1)} %all-to-all-done.4.rows.refs_3_, bf16[8,8,24,512]{3,2,1,0:T(8,128)(2,1)} %pad_maximum_fusion.preacts.refs_2_, bf16[256,3584]{1,0:T(8,128)(2,1)} %bitcast.43), custom_call_target="tpu_custom_call" | custom-call | tf_op jit(solution)/shard_map/prepare/pallas_call | solution.py:132
  172.3 14.7 %all-to-all-done.2.received.last.refs_4_ = bf16[8,1,24,3712]{3,2,1,0:T(8,128)(2,1)} async-done(((bf16[8,1,24,3712]{3,2,1,0:T(8,128)(2,1)}), bf16[8,1,24,3712]{3,2,1,0:T(8,128)(2,1)}, u32[]{:S(2)}, u32[]{:S(2)}) %all-to-all-start.2) | async-done | bytes 1425440 | tf_op jit(solution)/shard_map/all_to_all | solution.py:366
  187.0 7.6 %turn.1 = (f32[1,192,256]{2,1,0:T(8,128)}, bf16[8,1,24,3712]{3,2,1,0:T(8,128)(2,1)}) custom-call(s32[2]{0:T(128)} %pad_add_fusion.1.place, bf16[8,1,24,3712]{3,2,1,0:T(8,128)(2,1)} %all-to-all-done.2.received.last.refs_4_, bf16[8,8,24,512]{3,2,1,0:T(8,128)(2,1)} %pad_maximum_fusion.preacts.refs_2_, bf16[256,3584]{1,0:T(8,128)(2,1)} %bitcast.44, ...), custom_call_target="tpu_custom_call" | custom-call | tf_op jit(solution)/shard_map/turn/pallas_call | solution.py:187
  198.9 5.6 %slice_grad.5.rest_0_ = bf16[8,2,24,3584]{3,2,1,0:T(8,128)(2,1)} custom-call(f32[2,192,512]{2,1,0:T(8,128)} %get-tuple-element.39.sides, bf16[8,1,24,3712]{3,2,1,0:T(8,128)(2,1)} %all-to-all-done.2.received.last.refs_4_, bf16[3584,512]{1,0:T(8,128)(2,1)} %bitcast.32), custom_call_target="tpu_custom_call" | custom-call | tf_op jit(solution)/shard_map/slice_grad/pallas_call | solution.py:235
  207.1 11.7 %all-to-all-done.5.parts.refs_0_ = bf16[8,1,24,3712]{3,2,1,0:T(8,128)(2,1)} async-done(((bf16[8,1,24,3712]{3,2,1,0:T(8,128)(2,1)}), bf16[8,1,24,3712]{3,2,1,0:T(8,128)(2,1)}, u32[]{:S(2)}, u32[]{:S(2)}) %all-to-all-start.5) | async-done | bytes 1425440 | tf_op jit(solution)/shard_map/all_to_all | solution.py:366
  226.1 5.2 %collective-permute-start.7 = (bf16[136,3584]{1,0:T(8,128)(2,1)}, bf16[136,3584]{1,0:T(8,128)(2,1)S(1)}, u32[]{:S(2)}, u32[]{:S(2)}) collective-permute-start(bf16[136,3584]{1,0:T(8,128)(2,1)} %fold_rows.5), channel_id=1, source_target_pairs={{0,7},{1,0},{2,1},{3,2},{4,3},{5,4},{6,5},{7,6},{8,15},{9,8},{10,9... | collective-permute-start | bytes 2924552 | tf_op jit(solution)/shard_map/ppermute | solution.py:370
  231.3 5.6 %slice_grad.6.rest_0_ = bf16[8,2,24,3584]{3,2,1,0:T(8,128)(2,1)} custom-call(f32[2,192,512]{2,1,0:T(8,128)} %get-tuple-element.32.refs_9_.sides, bf16[8,1,24,3712]{3,2,1,0:T(8,128)(2,1)} %all-to-all-done.2.received.last.refs_4_, bf16[3584,512]{1,0:T(8,128)(2,1)} %bitcast.34), custom_call_target="tpu_custom_call" | custom-call | tf_op jit(solution)/shard_map/slice_grad/pallas_call | solution.py:235
  236.9 14.8 %collective-permute-done.7.rest_1_.refs_3_ = bf16[136,3584]{1,0:T(8,128)(2,1)S(1)} collective-permute-done((bf16[136,3584]{1,0:T(8,128)(2,1)}, bf16[136,3584]{1,0:T(8,128)(2,1)S(1)}, u32[]{:S(2)}, u32[]{:S(2)}) %collective-permute-start.7) | collective-permute-done | bytes 974880 | tf_op jit(solution)/shard_map/ppermute | solution.py:370
  257.3 9.0 %all-to-all-start.8 = ((bf16[8,2,24,3584]{3,2,1,0:T(8,128)(2,1)}), bf16[8,2,24,3584]{3,2,1,0:T(8,128)(2,1)}, u32[]{:S(2)}, u32[]{:S(2)}) async-start(bf16[8,2,24,3584]{3,2,1,0:T(8,128)(2,1)} %slice_grad_end.5.refs_4_), calls=%async_computation.8 | async-start | bytes 5505024 | tf_op jit(solution)/shard_map/all_to_all | solution.py:366
  270.6 5.1 %collective-permute-start.8 = (bf16[136,3584]{1,0:T(8,128)(2,1)}, bf16[136,3584]{1,0:T(8,128)(2,1)S(1)}, u32[]{:S(2)}, u32[]{:S(2)}) collective-permute-start(bf16[136,3584]{1,0:T(8,128)(2,1)} %get-tuple-element.40), channel_id=1, source_target_pairs={{0,7},{1,0},{2,1},{3,2},{4,3},{5,4},{6,5},{7,6},{8,15},{9,8},{10,9... | collective-permute-start | bytes 2924552 | tf_op jit(solution)/shard_map/ppermute | solution.py:370
  275.8 5.5 %slice_grad.4.rest_0_ = bf16[8,2,24,3584]{3,2,1,0:T(8,128)(2,1)} custom-call(f32[2,192,512]{2,1,0:T(8,128)} %get-tuple-element.36.refs_2_.sides, bf16[8,1,24,3712]{3,2,1,0:T(8,128)(2,1)} %all-to-all-done.2.received.last.refs_4_, bf16[3584,512]{1,0:T(8,128)(2,1)} %bitcast.36), custom_call_target="tpu_custom_call" | custom-call | tf_op jit(solution)/shard_map/slice_grad/pallas_call | solution.py:235
  281.3 10.3 %down_grads.1.rest_3_ = bf16[256,3584]{1,0:T(8,128)(2,1)} custom-call(bf16[8,1,24,3712]{3,2,1,0:T(8,128)(2,1)} %all-to-all-done.2.received.last.refs_4_, bf16[8,1,24,3584]{3,2,1,0:T(8,128)(2,1)} %all-to-all-done.rows.refs_0_, bf16[8,2,24,3584]{3,2,1,0:T(8,128)(2,1)} %all-to-all-done.3.rows.refs_1_, bf16[8,2,24,3584]{3,2,1,0:T(8,128)(2,1)} %all-to-all-done.1.rows.refs_2_, ...), custom_call_target="tpu_custom_call" | custom-call | tf_op jit(solution)/shard_map/down_grads/pallas_call | solution.py:287
  318.9 14.8 %collective-permute-done.10.rest_1_.refs_3_ = bf16[136,3584]{1,0:T(8,128)(2,1)S(1)} collective-permute-done((bf16[136,3584]{1,0:T(8,128)(2,1)}, bf16[136,3584]{1,0:T(8,128)(2,1)S(1)}, u32[]{:S(2)}, u32[]{:S(2)}) %collective-permute-start.10) | collective-permute-done | bytes 974880 | tf_op jit(solution)/shard_map/ppermute | solution.py:370
  352.9 9.2 %collective-permute-start.17 = (bf16[64,3584]{1,0:T(8,128)(2,1)}, bf16[64,3584]{1,0:T(8,128)(2,1)S(1)}, u32[]{:S(2)}, u32[]{:S(2)}) collective-permute-start(bf16[64,3584]{1,0:T(8,128)(2,1)} %get-tuple-element.54), channel_id=1, source_target_pairs={{0,71},{1,64},{2,65},{3,66},{4,67},{5,68},{6,69},{7,70},{64,135},{... | collective-permute-start | bytes 1376264 | tf_op jit(solution)/shard_map/ppermute | solution.py:381
  381.5 6.0 %collective-permute-done.12 = bf16[64,3584]{1,0:T(8,128)(2,1)S(1)} collective-permute-done((bf16[64,3584]{1,0:T(8,128)(2,1)}, bf16[64,3584]{1,0:T(8,128)(2,1)S(1)}, u32[]{:S(2)}, u32[]{:S(2)}) %collective-permute-start.12) | collective-permute-done | bytes 458784 | tf_op jit(solution)/shard_map/ppermute | solution.py:381
  (103 shorter events, 172.3 us)
Async XLA Ops:
  8.0 37.8 %all-to-all-start = ((bf16[8,1,24,3584]{3,2,1,0:T(8,128)(2,1)}), bf16[8,1,24,3584]{3,2,1,0:T(8,128)(2,1)}, u32[]{:S(2)}, u32[]{:S(2)}) async-start(bf16[8,1,24,3584]{3,2,1,0:T(8,128)(2,1)} %pack_rows.5), calls=%async_computation | async-start | bytes 2752512 | tf_op jit(solution)/shard_map/all_to_all | solution.py:366
  14.0 26.6 %collective-permute-start = (bf16[136,3584]{1,0:T(8,128)(2,1)S(1)}, bf16[136,3584]{1,0:T(8,128)(2,1)S(1)}, u32[]{:S(2)}, u32[]{:S(2)}) collective-permute-start(bf16[136,3584]{1,0:T(8,128)(2,1)S(1)} %copy-done), channel_id=1, source_target_pairs={{0,1},{1,2},{2,3},{3,4},{4,5},{5,6},{6,7},{7,0},{8,9},{9,10},{10,1... | collective-permute-start | bytes 2924552 | tf_op jit(solution)/shard_map/ppermute | solution.py:370
  15.7 25.9 %collective-permute-start.4 = (bf16[136,3584]{1,0:T(8,128)(2,1)S(1)}, bf16[136,3584]{1,0:T(8,128)(2,1)}, u32[]{:S(2)}, u32[]{:S(2)}) collective-permute-start(bf16[136,3584]{1,0:T(8,128)(2,1)S(1)} %copy-done), channel_id=1, source_target_pairs={{0,7},{1,0},{2,1},{3,2},{4,3},{5,4},{6,5},{7,6},{8,15},{9,8},{10,9... | collective-permute-start | bytes 2924552 | tf_op jit(solution)/shard_map/ppermute | solution.py:370
  45.8 39.0 %all-to-all-start.3 = ((bf16[8,2,24,3584]{3,2,1,0:T(8,128)(2,1)}), bf16[8,2,24,3584]{3,2,1,0:T(8,128)(2,1)}, u32[]{:S(2)}, u32[]{:S(2)}) async-start(bf16[8,2,24,3584]{3,2,1,0:T(8,128)(2,1)} %pack_rows.8), calls=%async_computation.3 | async-start | bytes 5505024 | tf_op jit(solution)/shard_map/all_to_all | solution.py:366
  50.7 22.3 %collective-permute-start.1 = (bf16[136,3584]{1,0:T(8,128)(2,1)S(1)}, bf16[136,3584]{1,0:T(8,128)(2,1)}, u32[]{:S(2)}, u32[]{:S(2)}) collective-permute-start(bf16[136,3584]{1,0:T(8,128)(2,1)S(1)} %copy-done.2), channel_id=1, source_target_pairs={{0,1},{1,2},{2,3},{3,4},{4,5},{5,6},{6,7},{7,0},{8,9},{9,10},{10,1... | collective-permute-start | bytes 2924552 | tf_op jit(solution)/shard_map/ppermute | solution.py:370
  50.7 22.2 %collective-permute-start.5 = (bf16[136,3584]{1,0:T(8,128)(2,1)}, bf16[136,3584]{1,0:T(8,128)(2,1)}, u32[]{:S(2)}, u32[]{:S(2)}) collective-permute-start(bf16[136,3584]{1,0:T(8,128)(2,1)} %collective-permute-done.4.refs_3_.refs_1_.refs_2_), channel_id=1, source_target_pairs={{0,7},{1,0},{2,1},{3,2},{4,3},{5,4},{6,5},{7,6},{8,15},{9,8},{10,9... | collective-permute-start | bytes 2924552 | tf_op jit(solution)/shard_map/ppermute | solution.py:370
  84.8 38.5 %all-to-all-start.1 = ((bf16[8,2,24,3584]{3,2,1,0:T(8,128)(2,1)}), bf16[8,2,24,3584]{3,2,1,0:T(8,128)(2,1)}, u32[]{:S(2)}, u32[]{:S(2)}) async-start(bf16[8,2,24,3584]{3,2,1,0:T(8,128)(2,1)} %pack_rows.6), calls=%async_computation.1 | async-start | bytes 5505024 | tf_op jit(solution)/shard_map/all_to_all | solution.py:366
  89.2 23.3 %collective-permute-start.2 = (bf16[136,3584]{1,0:T(8,128)(2,1)}, bf16[136,3584]{1,0:T(8,128)(2,1)S(1)}, u32[]{:S(2)}, u32[]{:S(2)}) collective-permute-start(bf16[136,3584]{1,0:T(8,128)(2,1)} %collective-permute-done.1.refs_0_.refs_4_.refs_1_), channel_id=1, source_target_pairs={{0,1},{1,2},{2,3},{3,4},{4,5},{5,6},{6,7},{7,0},{8,9},{9,10},{10,1... | collective-permute-start | bytes 2924552 | tf_op jit(solution)/shard_map/ppermute | solution.py:370
  89.3 23.2 %collective-permute-start.6 = (bf16[136,3584]{1,0:T(8,128)(2,1)}, bf16[136,3584]{1,0:T(8,128)(2,1)}, u32[]{:S(2)}, u32[]{:S(2)}) collective-permute-start(bf16[136,3584]{1,0:T(8,128)(2,1)} %collective-permute-done.5.refs_1_.refs_5_.refs_2_), channel_id=1, source_target_pairs={{0,7},{1,0},{2,1},{3,2},{4,3},{5,4},{6,5},{7,6},{8,15},{9,8},{10,9... | collective-permute-start | bytes 2924552 | tf_op jit(solution)/shard_map/ppermute | solution.py:370
  123.3 39.5 %all-to-all-start.4 = ((bf16[8,2,24,3584]{3,2,1,0:T(8,128)(2,1)}), bf16[8,2,24,3584]{3,2,1,0:T(8,128)(2,1)}, u32[]{:S(2)}, u32[]{:S(2)}) async-start(bf16[8,2,24,3584]{3,2,1,0:T(8,128)(2,1)} %pack_rows.9), calls=%async_computation.4 | async-start | bytes 5505024 | tf_op jit(solution)/shard_map/all_to_all | solution.py:366
  128.7 25.3 %collective-permute-start.3 = (bf16[136,3584]{1,0:T(8,128)(2,1)S(1)}, bf16[136,3584]{1,0:T(8,128)(2,1)}, u32[]{:S(2)}, u32[]{:S(2)}) collective-permute-start(bf16[136,3584]{1,0:T(8,128)(2,1)S(1)} %copy-done.4), channel_id=1, source_target_pairs={{0,1},{1,2},{2,3},{3,4},{4,5},{5,6},{6,7},{7,0},{8,9},{9,10},{10,1... | collective-permute-start | bytes 2924552 | tf_op jit(solution)/shard_map/ppermute | solution.py:370
  162.8 24.2 %all-to-all-start.2 = ((bf16[8,1,24,3712]{3,2,1,0:T(8,128)(2,1)}), bf16[8,1,24,3712]{3,2,1,0:T(8,128)(2,1)}, u32[]{:S(2)}, u32[]{:S(2)}) async-start(bf16[8,1,24,3712]{3,2,1,0:T(8,128)(2,1)} %pack_rows.7), calls=%async_computation.2 | async-start | bytes 2850816 | tf_op jit(solution)/shard_map/all_to_all | solution.py:366
  194.7 24.2 %all-to-all-start.5 = ((bf16[8,1,24,3712]{3,2,1,0:T(8,128)(2,1)}), bf16[8,1,24,3712]{3,2,1,0:T(8,128)(2,1)}, u32[]{:S(2)}, u32[]{:S(2)}) async-start(bf16[8,1,24,3712]{3,2,1,0:T(8,128)(2,1)} %get-tuple-element.38), calls=%async_computation.5 | async-start | bytes 2850816 | tf_op jit(solution)/shard_map/all_to_all | solution.py:366
  218.8 38.5 %all-to-all-start.6 = ((bf16[8,2,24,3584]{3,2,1,0:T(8,128)(2,1)}), bf16[8,2,24,3584]{3,2,1,0:T(8,128)(2,1)}, u32[]{:S(2)}, u32[]{:S(2)}) async-start(bf16[8,2,24,3584]{3,2,1,0:T(8,128)(2,1)} %slice_grad_end.4.refs_2_), calls=%async_computation.6 | async-start | bytes 5505024 | tf_op jit(solution)/shard_map/all_to_all | solution.py:366
  226.1 25.5 %collective-permute-start.7 = (bf16[136,3584]{1,0:T(8,128)(2,1)}, bf16[136,3584]{1,0:T(8,128)(2,1)S(1)}, u32[]{:S(2)}, u32[]{:S(2)}) collective-permute-start(bf16[136,3584]{1,0:T(8,128)(2,1)} %fold_rows.5), channel_id=1, source_target_pairs={{0,7},{1,0},{2,1},{3,2},{4,3},{5,4},{6,5},{7,6},{8,15},{9,8},{10,9... | collective-permute-start | bytes 2924552 | tf_op jit(solution)/shard_map/ppermute | solution.py:370
  257.3 43.3 %all-to-all-start.8 = ((bf16[8,2,24,3584]{3,2,1,0:T(8,128)(2,1)}), bf16[8,2,24,3584]{3,2,1,0:T(8,128)(2,1)}, u32[]{:S(2)}, u32[]{:S(2)}) async-start(bf16[8,2,24,3584]{3,2,1,0:T(8,128)(2,1)} %slice_grad_end.5.refs_4_), calls=%async_computation.8 | async-start | bytes 5505024 | tf_op jit(solution)/shard_map/all_to_all | solution.py:366
  270.6 24.3 %collective-permute-start.8 = (bf16[136,3584]{1,0:T(8,128)(2,1)}, bf16[136,3584]{1,0:T(8,128)(2,1)S(1)}, u32[]{:S(2)}, u32[]{:S(2)}) collective-permute-start(bf16[136,3584]{1,0:T(8,128)(2,1)} %get-tuple-element.40), channel_id=1, source_target_pairs={{0,7},{1,0},{2,1},{3,2},{4,3},{5,4},{6,5},{7,6},{8,15},{9,8},{10,9... | collective-permute-start | bytes 2924552 | tf_op jit(solution)/shard_map/ppermute | solution.py:370
  275.8 22.3 %collective-permute-start.9 = (bf16[136,3584]{1,0:T(8,128)(2,1)}, bf16[136,3584]{1,0:T(8,128)(2,1)}, u32[]{:S(2)}, u32[]{:S(2)}) collective-permute-start(bf16[136,3584]{1,0:T(8,128)(2,1)} %get-tuple-element.41), channel_id=1, source_target_pairs={{0,1},{1,2},{2,3},{3,4},{4,5},{5,6},{6,7},{7,0},{8,9},{9,10},{10,1... | collective-permute-start | bytes 2924552 | tf_op jit(solution)/shard_map/ppermute | solution.py:370
  300.7 39.0 %all-to-all-start.7 = ((bf16[8,2,24,3584]{3,2,1,0:T(8,128)(2,1)}), bf16[8,2,24,3584]{3,2,1,0:T(8,128)(2,1)}, u32[]{:S(2)}, u32[]{:S(2)}) async-start(bf16[8,2,24,3584]{3,2,1,0:T(8,128)(2,1)} %slice_grad_end.6.refs_5_), calls=%async_computation.7 | async-start | bytes 5505024 | tf_op jit(solution)/shard_map/all_to_all | solution.py:366
  309.9 23.9 %collective-permute-start.10 = (bf16[136,3584]{1,0:T(8,128)(2,1)}, bf16[136,3584]{1,0:T(8,128)(2,1)S(1)}, u32[]{:S(2)}, u32[]{:S(2)}) collective-permute-start(bf16[136,3584]{1,0:T(8,128)(2,1)} %get-tuple-element.47), channel_id=1, source_target_pairs={{0,7},{1,0},{2,1},{3,2},{4,3},{5,4},{6,5},{7,6},{8,15},{9,8},{10,9... | collective-permute-start | bytes 2924552 | tf_op jit(solution)/shard_map/ppermute | solution.py:370
  314.6 22.3 %collective-permute-start.11 = (bf16[136,3584]{1,0:T(8,128)(2,1)}, bf16[136,3584]{1,0:T(8,128)(2,1)}, u32[]{:S(2)}, u32[]{:S(2)}) collective-permute-start(bf16[136,3584]{1,0:T(8,128)(2,1)} %get-tuple-element.48), channel_id=1, source_target_pairs={{0,1},{1,2},{2,3},{3,4},{4,5},{5,6},{6,7},{7,0},{8,9},{9,10},{10,1... | collective-permute-start | bytes 2924552 | tf_op jit(solution)/shard_map/ppermute | solution.py:370
  339.6 24.4 %all-to-all-start.9 = ((bf16[8,1,24,3584]{3,2,1,0:T(8,128)(2,1)}), bf16[8,1,24,3584]{3,2,1,0:T(8,128)(2,1)}, u32[]{:S(2)}, u32[]{:S(2)}) async-start(bf16[8,1,24,3584]{3,2,1,0:T(8,128)(2,1)} %slice_grad_end.7.refs_5_), calls=%async_computation.9 | async-start | bytes 2752512 | tf_op jit(solution)/shard_map/all_to_all | solution.py:366
  352.9 25.8 %collective-permute-start.17 = (bf16[64,3584]{1,0:T(8,128)(2,1)}, bf16[64,3584]{1,0:T(8,128)(2,1)S(1)}, u32[]{:S(2)}, u32[]{:S(2)}) collective-permute-start(bf16[64,3584]{1,0:T(8,128)(2,1)} %get-tuple-element.54), channel_id=1, source_target_pairs={{0,71},{1,64},{2,65},{3,66},{4,67},{5,68},{6,69},{7,70},{64,135},{... | collective-permute-start | bytes 1376264 | tf_op jit(solution)/shard_map/ppermute | solution.py:381
  362.0 18.5 %collective-permute-start.18 = (bf16[64,3584]{1,0:T(8,128)(2,1)}, bf16[64,3584]{1,0:T(8,128)(2,1)S(1)}, u32[]{:S(2)}, u32[]{:S(2)}) collective-permute-start(bf16[64,3584]{1,0:T(8,128)(2,1)} %get-tuple-element.55), channel_id=1, source_target_pairs={{0,65},{1,66},{2,67},{3,68},{4,69},{5,70},{6,71},{7,64},{64,129},{... | collective-permute-start | bytes 1376264 | tf_op jit(solution)/shard_map/ppermute | solution.py:381
  (17 other events, 133.4 us)

commit v6 on v5

--- a/solution.py
+++ b/solution.py
@@ -51,6 +51,21 @@
     return [slice(low, low + TILE) for low in range(0, width, TILE)]
 
 
+def read_tile(ref, source, tile):
+    share = TILE // ref.shape[4]
+    parts = [ref[:, source, tile * share + i] for i in range(share)]
+    block = parts[0] if share == 1 else jnp.concatenate(parts, axis=2)
+    return block.reshape(block.shape[0] * block.shape[1], TILE)
+
+
+def write_tile(ref, source, tile, values):
+    narrow = ref.shape[4]
+    share = TILE // narrow
+    block = values.reshape(ref.shape[0], ref.shape[3], TILE)
+    for i in range(share):
+        ref[:, source, tile * share + i] = block[:, :, i * narrow : (i + 1) * narrow]
+
+
 def params():
     return pltpu.CompilerParams(vmem_limit_bytes=VMEM_LIMIT)
 
@@ -67,10 +82,10 @@
         rows = refs[m]
         hits, _ = slot_hits(tags(rows), place[0], columns, capacity)
         ones = flat(hits)
-        for tile in tiles(width):
+        for k, tile in enumerate(tiles(width)):
             packed = jnp.dot(ones, rows[:LANES, tile], preferred_element_type=f32)
-            out[:, m, :, tile] = packed.astype(bf16).reshape(columns, 2 * capacity, TILE)
-    if out.shape[3] > width:
+            write_tile(out, m, k, packed.astype(bf16))
+    if tagged:
         lane = lax.broadcasted_iota(jnp.int32, (columns, 2 * capacity, EXTRA), 2)
         scales = jnp.zeros((columns, 2 * capacity, EXTRA), f32)
         for k, rows in enumerate(refs[count : count + tagged]):
@@ -80,16 +95,17 @@
             gates = jnp.where(picks[0] == ids, picks[2], 0.0) + jnp.where(picks[1] == ids, picks[3], 0.0)
             scale = jnp.sum(hits * gates[:, None, :], axis=2, keepdims=True)
             scales = jnp.where(lane == k, scale, scales)
-        out[:, 0, :, width:] = scales.astype(bf16)
+        out[:, 0, out.shape[2] - 1] = scales.astype(bf16)
 
 
 def pack(place, arrivals, columns, capacity, tagged=(), earlier=()):
     width = arrivals[0].shape[1]
-    extra = EXTRA if tagged else 0
+    narrow = EXTRA if tagged else TILE
+    pieces = width // narrow + (1 if tagged else 0)
     only_tags = pl.BlockSpec((META, 4 * LANES), lambda i: (LANES // META, 0))
     return pl.pallas_call(
         functools.partial(pack_kernel, capacity, len(arrivals), len(tagged), width),
-        out_shape=jax.ShapeDtypeStruct((columns, len(arrivals), 2 * capacity, width + extra), bf16),
+        out_shape=jax.ShapeDtypeStruct((columns, len(arrivals), pieces, 2 * capacity, narrow), bf16),
         grid=(1,),
         in_specs=[SMEM] + [VMEM] * len(arrivals) + [only_tags] * len(tagged) + [ANY] * len(earlier),
         out_specs=VMEM,
@@ -98,10 +114,12 @@
     )(place, *arrivals, *tagged, *earlier)
 
 
-def expert_parts(rows, preacts, down_proj):
+def expert_parts(received, preacts, down_proj):
     width = down_proj.shape[1]
     half = down_proj.shape[0]
-    back = lax.dot_general(rows, down_proj, NT, preferred_element_type=f32)
+    back = 0.0
+    for k, tile in enumerate(tiles(width)):
+        back += lax.dot_general(read_tile(received, 0, k), down_proj[:, tile], NT, preferred_element_type=f32)
     gate_pre = preacts[:, :half].astype(f32)
     up_pre = preacts[:, half:].astype(f32)
     sig = 1.0 / (1.0 + jnp.exp(-gate_pre))
@@ -112,12 +130,11 @@
     return gate_side, back * act, hidden, part
 
 
-def prepare_kernel(width, place, rows, preacts, down_proj, sides, hidden, parts):
+def prepare_kernel(place, rows, preacts, down_proj, sides, hidden, parts):
     slots = sides.shape[1]
     half = hidden.shape[2]
-    table = rows[:, 0, :, :width].reshape(slots, width)
     pre = preacts[:, 0].reshape(slots, 2 * half)
-    gate_side, up_side, hid, part = expert_parts(table, pre, down_proj[...])
+    gate_side, up_side, hid, part = expert_parts(rows, pre, down_proj)
     sides[0, :, :half] = gate_side
     sides[0, :, half:] = up_side
     hidden[0] = hid
@@ -125,12 +142,12 @@
 
 
 def prepare(place, received, preacts, down_proj):
-    columns, count, span = received.shape[:3]
+    columns, count, pieces, span, narrow = received.shape
     half, width = down_proj.shape
     slots = columns * span
     block = lambda m, place: (m, 0, 0)
     return pl.pallas_call(
-        functools.partial(prepare_kernel, width),
+        prepare_kernel,
         out_shape=[
             jax.ShapeDtypeStruct((count, slots, 2 * half), f32),
             jax.ShapeDtypeStruct((count, slots, half), f32),
@@ -140,7 +157,7 @@
             num_scalar_prefetch=1,
             grid=(count,),
             in_specs=[
-                pl.BlockSpec((columns, 1, span, width), lambda m, place: (0, m, 0, 0)),
+                pl.BlockSpec((columns, 1, pieces, span, narrow), lambda m, place: (0, m, 0, 0, 0)),
                 pl.BlockSpec((columns, 1, span, 2 * half), lambda m, place: (0, place[1 + m], 0, 0)),
                 pl.BlockSpec((half, width), lambda m, place: (0, 0)),
             ],
@@ -158,17 +175,16 @@
 def turn_kernel(count, place, received, preacts, down_proj, gate_up, *refs):
     others, hidden, out = refs[:-2], refs[-2], refs[-1]
     half, width = down_proj.shape
-    columns, _, span, _ = received.shape
+    columns, _, pieces, span, _ = received.shape
     slots = columns * span
-    table = received[:, 0, :, :width].reshape(slots, width)
-    scales = received[:, 0, :, width:].astype(f32).reshape(slots, EXTRA)
-    gate_side, up_side, hid, part = expert_parts(table, preacts[:, 0].reshape(slots, 2 * half), down_proj[...])
+    scales = received[:, 0, pieces - 1].astype(f32).reshape(slots, EXTRA)
+    gate_side, up_side, hid, part = expert_parts(received, preacts[:, 0].reshape(slots, 2 * half), down_proj)
     hidden[0] = hid
     scale = scales[:, count - 1 : count]
     both = jnp.concatenate([scale * gate_side, scale * up_side], axis=1).astype(bf16)
-    for tile in tiles(width):
+    for k, tile in enumerate(tiles(width)):
         grad = lax.dot_general(both, gate_up[tile, :], NT, preferred_element_type=f32)
-        out[:, 0, :, tile] = grad.astype(bf16).reshape(columns, span, TILE)
+        write_tile(out, 0, k, grad.astype(bf16))
     lane = lax.broadcasted_iota(jnp.int32, (slots, EXTRA), 1)
     parts = jnp.where(lane == count - 1, part, 0.0)
     k = 0
@@ -176,11 +192,11 @@
         for m in range(group.shape[0]):
             parts = jnp.where(lane == k, group[m], parts)
             k += 1
-    out[:, 0, :, width:] = parts.astype(bf16).reshape(columns, span, EXTRA)
+    out[:, 0, pieces - 1] = parts.astype(bf16).reshape(columns, span, EXTRA)
 
 
 def turn(place, received, preacts, down_proj, gate_up, parts):
-    columns, _, span, wide = received.shape
+    columns, _, pieces, span, narrow = received.shape
     half, width = down_proj.shape
     slots = columns * span
     count = 1 + sum(p.shape[0] for p in parts)
@@ -188,7 +204,7 @@
         functools.partial(turn_kernel, count),
         out_shape=[
             jax.ShapeDtypeStruct((1, slots, half), f32),
-            jax.ShapeDtypeStruct((columns, 1, span, wide), bf16),
+            jax.ShapeDtypeStruct((columns, 1, pieces, span, narrow), bf16),
         ],
         grid_spec=pltpu.PrefetchScalarGridSpec(
             num_scalar_prefetch=1,
@@ -210,34 +226,35 @@
 def grad_kernel(first, sides, last, gate_up, *rest):
     out = rest[-1]
     width = gate_up.shape[0]
-    columns, _, span, _ = out.shape
+    columns, _, _, span, _ = out.shape
     slots = columns * span
-    scales = last[:, 0].reshape(slots, EXTRA).astype(f32)
+    scales = last[:, 0, 0].reshape(slots, EXTRA).astype(f32)
     lane = lax.broadcasted_iota(jnp.int32, (slots, EXTRA), 1)
     index = first + pl.program_id(0)
     scale = jnp.sum(jnp.where(lane == index, scales, 0.0), axis=1, keepdims=True)
     both = (scale * sides[0]).astype(bf16)
-    for tile in tiles(width):
+    for k, tile in enumerate(tiles(width)):
         grad = lax.dot_general(both, gate_up[tile, :], NT, preferred_element_type=f32)
-        out[:, 0, :, tile] = grad.astype(bf16).reshape(columns, span, TILE)
+        write_tile(out, 0, k, grad.astype(bf16))
 
 
 def slice_grad(first, sides, last, gate_up, earlier):
     count, slots, full = sides.shape
-    columns, _, span, _ = last.shape
+    columns, _, _, span, _ = last.shape
     width = gate_up.shape[0]
-    shape = jax.ShapeDtypeStruct((columns, count, span, width), bf16)
+    pieces = width // TILE
+    shape = jax.ShapeDtypeStruct((columns, count, pieces, span, TILE), bf16)
     most = width - TILE
     shared = [
         pl.BlockSpec((1, slots, full), lambda m: (m, 0, 0)),
-        pl.BlockSpec((columns, 1, span, EXTRA), lambda m: (0, 0, 0, width // EXTRA)),
+        pl.BlockSpec((columns, 1, 1, span, EXTRA), lambda m: (0, 0, width // EXTRA, 0, 0)),
     ]
     sending = pl.pallas_call(
         functools.partial(grad_kernel, first),
         out_shape=shape,
         grid=(count,),
         in_specs=shared + [pl.BlockSpec((most, full), lambda m: (0, 0))],
-        out_specs=pl.BlockSpec((columns, 1, span, most), lambda m: (0, m, 0, 0)),
+        out_specs=pl.BlockSpec((columns, 1, pieces - 1, span, TILE), lambda m: (0, m, 0, 0, 0)),
         compiler_params=params(),
         name="slice_grad",
     )(sides, last, gate_up)
@@ -248,7 +265,7 @@
         in_specs=shared
         + [pl.BlockSpec((TILE, full), lambda m: (most // TILE, 0)), ANY]
         + [ANY] * len(earlier),
-        out_specs=pl.BlockSpec((columns, 1, span, TILE), lambda m: (0, m, 0, most // TILE)),
+        out_specs=pl.BlockSpec((columns, 1, 1, span, TILE), lambda m: (0, m, pieces - 1, 0, 0)),
         input_output_aliases={3: 0},
         compiler_params=params(),
         name="slice_grad_end",
@@ -261,7 +278,7 @@
 
     @pl.when(pl.program_id(0) == 0)
     def _():
-        scales = last[:, 0].reshape(slots, EXTRA).astype(f32)
+        scales = last[:, 0, 0].reshape(slots, EXTRA).astype(f32)
         k = 0
         for group in hidden:
             for m in range(group.shape[0]):
@@ -272,7 +289,7 @@
     k = 0
     for group in rows:
         for m in range(group.shape[1]):
-            table = group[:, m].reshape(slots, out.shape[1])
+            table = read_tile(group, m, 0)
             part = scaled[k * slots : (k + 1) * slots]
             total += lax.dot_general(part, table, TN, preferred_element_type=f32)
             k += 1
@@ -281,15 +298,18 @@
 
 def down_grads(received, hidden, width):
     last = received[-1]
-    columns, _, span, _ = last.shape
+    columns, _, _, span, _ = last.shape
     count = sum(h.shape[0] for h in hidden)
     slots, half = hidden[0].shape[1:]
     return pl.pallas_call(
         functools.partial(down_kernel, len(received)),
         out_shape=jax.ShapeDtypeStruct((half, width), bf16),
         grid=(width // TILE,),
-        in_specs=[pl.BlockSpec((columns, 1, span, EXTRA), lambda i: (0, 0, 0, width // EXTRA))]
-        + [pl.BlockSpec((columns, g.shape[1], span, TILE), lambda i: (0, 0, 0, i)) for g in received]
+        in_specs=[pl.BlockSpec((columns, 1, 1, span, EXTRA), lambda i: (0, 0, width // EXTRA, 0, 0))]
+        + [
+            pl.BlockSpec((columns, g.shape[1], TILE // g.shape[4], span, g.shape[4]), lambda i: (0, 0, i, 0, 0))
+            for g in received
+        ]
         + [pl.BlockSpec(h.shape, lambda i: (0, 0, 0)) for h in hidden],
         out_specs=pl.BlockSpec((half, TILE), lambda i: (0, i)),
         scratch_shapes=[pltpu.VMEM((count * slots, half), bf16)],
@@ -303,9 +323,8 @@
     metas = refs[1 : 1 + count]
     incoming = refs[1 + count : 1 + count + coming]
     outs = refs[-3 * count :] if split else refs[-count:]
-    columns, _, span, _ = returned.shape
-    slots = columns * span
-    table = parts[:, 0].astype(f32)
+    columns, _, pieces, span, narrow = returned.shape
+    table = parts[:, 0, 0].astype(f32)
     for m in range(count):
         meta = metas[m][:, :].astype(f32)
         picks = [meta[0:1, i * LANES : (i + 1) * LANES] for i in range(4)]
@@ -313,9 +332,8 @@
         ones = flat(hits)
         added = incoming[m::count] if coming >= count else incoming[m : m + 1]
         sums = [other for other in added if other.shape[0] > META]
-        for tile in tiles(returned.shape[3] // TILE * TILE):
-            rows = returned[:, m, :, tile].reshape(slots, TILE)
-            total = lax.dot_general(ones, rows, TN, preferred_element_type=f32)
+        for n, tile in enumerate(tiles(pieces * narrow // TILE * TILE)):
+            total = lax.dot_general(ones, read_tile(returned, m, n), TN, preferred_element_type=f32)
             for other in sums:
                 total = total + other[:LANES, tile].astype(f32)
             total = total.astype(bf16)
@@ -340,7 +358,7 @@
 
 
 def fold(place, first, parts, returned, arrivals, incoming, capacity, split, earlier=()):
-    columns, count, span, _ = returned.shape
+    columns, count, _, span, _ = returned.shape
     width = arrivals[0].shape[1]
     only_tags = pl.BlockSpec((META, 4 * LANES), lambda i: (LANES // META, 0))
     if split:
@@ -352,7 +370,7 @@
         functools.partial(fold_kernel, capacity, first, count, len(incoming), split),
         out_shape=shapes,
         grid=(1,),
-        in_specs=[SMEM, pl.BlockSpec((columns, 1, span, EXTRA), lambda i: (0, 0, 0, width // EXTRA)), VMEM]
+        in_specs=[SMEM, pl.BlockSpec((columns, 1, 1, span, EXTRA), lambda i: (0, 0, width // EXTRA, 0, 0)), VMEM]
         + [only_tags] * count
         + [VMEM] * len(incoming)
         + [ANY] * len(earlier),
@@ -363,7 +381,10 @@
 
 
 def exchange(block):
-    return lax.all_to_all(block, "column", split_axis=0, concat_axis=0, tiled=True)
+    columns, count, pieces, span, narrow = block.shape
+    merged = block.reshape(columns, count * pieces, span, narrow)
+    moved = lax.all_to_all(merged, "column", split_axis=0, concat_axis=0, tiled=True)
+    return moved.reshape(block.shape)
 
 
 def hop(block, distance):

time: 398 us -> 399 us (level)
  no operation moved by 1% of the time
where the time goes in v6:
time: 399 us; the launch traced here: 397 us
  waiting for transfers between devices  164 us (41%)
  starting transfers between devices  107 us (27%)
  Pallas kernels  106 us (27%)
  other arithmetic  11.4 us (3%)
  local copies, waits for them, and re-layouts  6.91 us (2%)
    ppermute x14, waiting for transfers between devices, hop(): lax.ppermute(block, 'depth', [(i, (i + distance) % DEPTH) for i in range(...  102 us
    all_to_all x10, starting transfers between devices, exchange(): lax.all_to_all(merged, 'column', split_axis=0, concat_axis=0, tiled=True)  52 us
    all_to_all x10, waiting for transfers between devices, exchange(): lax.all_to_all(merged, 'column', split_axis=0, concat_axis=0, tiled=True)  47.4 us
    ppermute x14, starting transfers between devices, hop(): lax.ppermute(block, 'depth', [(i, (i + distance) % DEPTH) for i in range(...  32.8 us
    pallas_call x8, Pallas kernels, slice_grad(): pl.pallas_call(functools.partial(grad_kernel, first), out_shape=shape, gr...  30.9 us
    ppermute x6, starting transfers between devices, shifted(): return lax.ppermute(block, ('section', 'depth'), route)  22.7 us
    pallas_call x4, Pallas kernels, prepare(): pl.pallas_call(prepare_kernel, out_shape=[jax.ShapeDtypeStruct((count, sl...  19.5 us
    pallas_call x5, Pallas kernels, fold(): pl.pallas_call(functools.partial(fold_kernel, capacity, first, count, len...  19 us
  transfers between devices with their start and end apart: 30, of which 19 were waited for; matrix products, arithmetic and copies ran while one was open for 2% of the time, Pallas kernels for 24%

profile of v6, /device:TPU:1, one launch (start us, length us, event | category | flops | bytes accessed | tf_op | source)
XLA Modules:
  0.0 396.6 jit_solution(4274763182938697047)
XLA Ops:
  8.0 6.0 %all-to-all-start = ((bf16[8,7,24,512]{3,2,1,0:T(8,128)(2,1)}), bf16[8,7,24,512]{3,2,1,0:T(8,128)(2,1)}, u32[]{:S(2)}, u32[]{:S(2)}) async-start(bf16[8,7,24,512]{3,2,1,0:T(8,128)(2,1)} %bitcast.74), calls=%async_computation | async-start | bytes 2752512 | tf_op jit(solution)/shard_map/all_to_all | solution.py:386
  25.2 15.4 %collective-permute-done.refs_2_.refs_0_.refs_1_ = bf16[136,3584]{1,0:T(8,128)(2,1)S(1)} collective-permute-done((bf16[136,3584]{1,0:T(8,128)(2,1)S(1)}, bf16[136,3584]{1,0:T(8,128)(2,1)S(1)}, u32[]{:S(2)}, u32[]{:S(2)}) %collective-permute-start) | collective-permute-done | bytes 974880 | tf_op jit(solution)/shard_map/ppermute | solution.py:391
  58.1 14.8 %collective-permute-done.1.refs_0_.refs_4_.refs_1_ = bf16[136,3584]{1,0:T(8,128)(2,1)} collective-permute-done((bf16[136,3584]{1,0:T(8,128)(2,1)S(1)}, bf16[136,3584]{1,0:T(8,128)(2,1)}, u32[]{:S(2)}, u32[]{:S(2)}) %collective-permute-start.1) | collective-permute-done | bytes 974880 | tf_op jit(solution)/shard_map/ppermute | solution.py:391
  77.2 7.6 %all-to-all-done.3 = bf16[8,14,24,512]{3,2,1,0:T(8,128)(2,1)} async-done(((bf16[8,14,24,512]{3,2,1,0:T(8,128)(2,1)}), bf16[8,14,24,512]{3,2,1,0:T(8,128)(2,1)}, u32[]{:S(2)}, u32[]{:S(2)}) %all-to-all-start.3) | async-done | bytes 2752544 | tf_op jit(solution)/shard_map/all_to_all | solution.py:386
  97.7 14.8 %collective-permute-done.2.refs_6_.refs_0_.refs_1_ = bf16[136,3584]{1,0:T(8,128)(2,1)S(1)} collective-permute-done((bf16[136,3584]{1,0:T(8,128)(2,1)}, bf16[136,3584]{1,0:T(8,128)(2,1)S(1)}, u32[]{:S(2)}, u32[]{:S(2)}) %collective-permute-start.2) | collective-permute-done | bytes 974880 | tf_op jit(solution)/shard_map/ppermute | solution.py:391
  117.6 5.7 %all-to-all-done.1 = bf16[8,14,24,512]{3,2,1,0:T(8,128)(2,1)} async-done(((bf16[8,14,24,512]{3,2,1,0:T(8,128)(2,1)}), bf16[8,14,24,512]{3,2,1,0:T(8,128)(2,1)}, u32[]{:S(2)}, u32[]{:S(2)}) %all-to-all-start.1) | async-done | bytes 2752544 | tf_op jit(solution)/shard_map/all_to_all | solution.py:386
  123.3 5.5 %all-to-all-start.4 = ((bf16[8,14,24,512]{3,2,1,0:T(8,128)(2,1)}), bf16[8,14,24,512]{3,2,1,0:T(8,128)(2,1)}, u32[]{:S(2)}, u32[]{:S(2)}) async-start(bf16[8,14,24,512]{3,2,1,0:T(8,128)(2,1)} %bitcast.70), calls=%async_computation.4 | async-start | bytes 5505024 | tf_op jit(solution)/shard_map/all_to_all | solution.py:386
  136.4 17.8 %collective-permute-done.3.refs_0_.refs_8_.refs_1_ = bf16[136,3584]{1,0:T(8,128)(2,1)} collective-permute-done((bf16[136,3584]{1,0:T(8,128)(2,1)S(1)}, bf16[136,3584]{1,0:T(8,128)(2,1)}, u32[]{:S(2)}, u32[]{:S(2)}) %collective-permute-start.3) | collective-permute-done | bytes 974880 | tf_op jit(solution)/shard_map/ppermute | solution.py:391
  157.5 5.4 %all-to-all-done.4 = bf16[8,14,24,512]{3,2,1,0:T(8,128)(2,1)} async-done(((bf16[8,14,24,512]{3,2,1,0:T(8,128)(2,1)}), bf16[8,14,24,512]{3,2,1,0:T(8,128)(2,1)}, u32[]{:S(2)}, u32[]{:S(2)}) %all-to-all-start.4) | async-done | bytes 2752544 | tf_op jit(solution)/shard_map/all_to_all | solution.py:386
  167.3 5.2 %prepare.7 = (f32[2,192,512]{2,1,0:T(8,128)}, f32[2,192,256]{2,1,0:T(8,128)}, f32[2,192,128]{2,1,0:T(8,128)}) custom-call(s32[3]{0:T(128)} %pad_add_fusion.4.place, bf16[8,2,7,24,512]{4,3,2,1,0:T(8,128)(2,1)} %bitcast.27.rows.refs_3_, bf16[8,8,24,512]{3,2,1,0:T(8,128)(2,1)} %pad_maximum_fusion.preacts.refs_2_, bf16[256,3584]{1,0:T(8,128)(2,1)} %bitcast.63), custom_call_target="tpu_custom_call" | custom-call | tf_op jit(solution)/shard_map/prepare/pallas_call | solution.py:149
  172.4 14.7 %all-to-all-done.2 = bf16[8,29,24,128]{3,2,1,0:T(8,128)(2,1)} async-done(((bf16[8,29,24,128]{3,2,1,0:T(8,128)(2,1)}), bf16[8,29,24,128]{3,2,1,0:T(8,128)(2,1)}, u32[]{:S(2)}, u32[]{:S(2)}) %all-to-all-start.2) | async-done | bytes 1425440 | tf_op jit(solution)/shard_map/all_to_all | solution.py:386
  187.1 7.7 %turn.1 = (f32[1,192,256]{2,1,0:T(8,128)}, bf16[8,1,29,24,128]{4,3,2,1,0:T(8,128)(2,1)}) custom-call(s32[2]{0:T(128)} %pad_add_fusion.1.place, bf16[8,1,29,24,128]{4,3,2,1,0:T(8,128)(2,1)} %bitcast.20.received.last.refs_4_, bf16[8,8,24,512]{3,2,1,0:T(8,128)(2,1)} %pad_maximum_fusion.preacts.refs_2_, bf16[256,3584]{1,0:T(8,128)(2,1)} %bitcast.64, ...), custom_call_target="tpu_custom_call" | custom-call | tf_op jit(solution)/shard_map/turn/pallas_call | solution.py:203
  199.1 5.5 %slice_grad.5.rest_0_ = bf16[8,2,7,24,512]{4,3,2,1,0:T(8,128)(2,1)} custom-call(f32[2,192,512]{2,1,0:T(8,128)} %get-tuple-element.39.sides, bf16[8,1,29,24,128]{4,3,2,1,0:T(8,128)(2,1)} %bitcast.20.received.last.refs_4_, bf16[3584,512]{1,0:T(8,128)(2,1)} %bitcast.52), custom_call_target="tpu_custom_call" | custom-call | tf_op jit(solution)/shard_map/slice_grad/pallas_call | solution.py:252
  207.2 11.8 %all-to-all-done.5 = bf16[8,29,24,128]{3,2,1,0:T(8,128)(2,1)} async-done(((bf16[8,29,24,128]{3,2,1,0:T(8,128)(2,1)}), bf16[8,29,24,128]{3,2,1,0:T(8,128)(2,1)}, u32[]{:S(2)}, u32[]{:S(2)}) %all-to-all-start.5) | async-done | bytes 1425440 | tf_op jit(solution)/shard_map/all_to_all | solution.py:386
  226.4 5.2 %collective-permute-start.7 = (bf16[136,3584]{1,0:T(8,128)(2,1)}, bf16[136,3584]{1,0:T(8,128)(2,1)S(1)}, u32[]{:S(2)}, u32[]{:S(2)}) collective-permute-start(bf16[136,3584]{1,0:T(8,128)(2,1)} %fold_rows.5), channel_id=1, source_target_pairs={{0,7},{1,0},{2,1},{3,2},{4,3},{5,4},{6,5},{7,6},{8,15},{9,8},{10,9... | collective-permute-start | bytes 2924552 | tf_op jit(solution)/shard_map/ppermute | solution.py:391
  231.5 5.5 %slice_grad.6.rest_0_ = bf16[8,2,7,24,512]{4,3,2,1,0:T(8,128)(2,1)} custom-call(f32[2,192,512]{2,1,0:T(8,128)} %get-tuple-element.32.refs_9_.sides, bf16[8,1,29,24,128]{4,3,2,1,0:T(8,128)(2,1)} %bitcast.20.received.last.refs_4_, bf16[3584,512]{1,0:T(8,128)(2,1)} %bitcast.54), custom_call_target="tpu_custom_call" | custom-call | tf_op jit(solution)/shard_map/slice_grad/pallas_call | solution.py:252
  237.1 14.8 %collective-permute-done.7.rest_1_.refs_3_ = bf16[136,3584]{1,0:T(8,128)(2,1)S(1)} collective-permute-done((bf16[136,3584]{1,0:T(8,128)(2,1)}, bf16[136,3584]{1,0:T(8,128)(2,1)S(1)}, u32[]{:S(2)}, u32[]{:S(2)}) %collective-permute-start.7) | collective-permute-done | bytes 974880 | tf_op jit(solution)/shard_map/ppermute | solution.py:391
  257.5 9.0 %all-to-all-start.8 = ((bf16[8,14,24,512]{3,2,1,0:T(8,128)(2,1)}), bf16[8,14,24,512]{3,2,1,0:T(8,128)(2,1)}, u32[]{:S(2)}, u32[]{:S(2)}) async-start(bf16[8,14,24,512]{3,2,1,0:T(8,128)(2,1)} %bitcast.65), calls=%async_computation.8 | async-start | bytes 5505024 | tf_op jit(solution)/shard_map/all_to_all | solution.py:386
  270.8 5.1 %collective-permute-start.8 = (bf16[136,3584]{1,0:T(8,128)(2,1)}, bf16[136,3584]{1,0:T(8,128)(2,1)S(1)}, u32[]{:S(2)}, u32[]{:S(2)}) collective-permute-start(bf16[136,3584]{1,0:T(8,128)(2,1)} %get-tuple-element.40), channel_id=1, source_target_pairs={{0,7},{1,0},{2,1},{3,2},{4,3},{5,4},{6,5},{7,6},{8,15},{9,8},{10,9... | collective-permute-start | bytes 2924552 | tf_op jit(solution)/shard_map/ppermute | solution.py:391
  275.9 5.5 %slice_grad.4.rest_0_ = bf16[8,2,7,24,512]{4,3,2,1,0:T(8,128)(2,1)} custom-call(f32[2,192,512]{2,1,0:T(8,128)} %get-tuple-element.36.refs_2_.sides, bf16[8,1,29,24,128]{4,3,2,1,0:T(8,128)(2,1)} %bitcast.20.received.last.refs_4_, bf16[3584,512]{1,0:T(8,128)(2,1)} %bitcast.56), custom_call_target="tpu_custom_call" | custom-call | tf_op jit(solution)/shard_map/slice_grad/pallas_call | solution.py:252
  281.5 10.3 %down_grads.1.rest_3_ = bf16[256,3584]{1,0:T(8,128)(2,1)} custom-call(bf16[8,1,29,24,128]{4,3,2,1,0:T(8,128)(2,1)} %bitcast.20.received.last.refs_4_, bf16[8,1,7,24,512]{4,3,2,1,0:T(8,128)(2,1)} %bitcast.13.rows.refs_0_, bf16[8,2,7,24,512]{4,3,2,1,0:T(8,128)(2,1)} %bitcast.23.rows.refs_1_, bf16[8,2,7,24,512]{4,3,2,1,0:T(8,128)(2,1)} %bitcast.18.rows.refs_2_, ...), custom_call_target="tpu_custom_call" | custom-call | tf_op jit(solution)/shard_map/down_grads/pallas_call | solution.py:304
  319.2 15.2 %collective-permute-done.10.rest_1_.refs_3_ = bf16[136,3584]{1,0:T(8,128)(2,1)S(1)} collective-permute-done((bf16[136,3584]{1,0:T(8,128)(2,1)}, bf16[136,3584]{1,0:T(8,128)(2,1)S(1)}, u32[]{:S(2)}, u32[]{:S(2)}) %collective-permute-start.10) | collective-permute-done | bytes 974880 | tf_op jit(solution)/shard_map/ppermute | solution.py:391
  353.1 9.3 %collective-permute-start.17 = (bf16[64,3584]{1,0:T(8,128)(2,1)}, bf16[64,3584]{1,0:T(8,128)(2,1)S(1)}, u32[]{:S(2)}, u32[]{:S(2)}) collective-permute-start(bf16[64,3584]{1,0:T(8,128)(2,1)} %get-tuple-element.54), channel_id=1, source_target_pairs={{0,71},{1,64},{2,65},{3,66},{4,67},{5,68},{6,69},{7,70},{64,135},{... | collective-permute-start | bytes 1376264 | tf_op jit(solution)/shard_map/ppermute | solution.py:402
  381.6 6.0 %collective-permute-done.12 = bf16[64,3584]{1,0:T(8,128)(2,1)S(1)} collective-permute-done((bf16[64,3584]{1,0:T(8,128)(2,1)}, bf16[64,3584]{1,0:T(8,128)(2,1)S(1)}, u32[]{:S(2)}, u32[]{:S(2)}) %collective-permute-start.12) | collective-permute-done | bytes 458784 | tf_op jit(solution)/shard_map/ppermute | solution.py:402
  (103 shorter events, 171.9 us)
Async XLA Ops:
  8.0 37.8 %all-to-all-start = ((bf16[8,7,24,512]{3,2,1,0:T(8,128)(2,1)}), bf16[8,7,24,512]{3,2,1,0:T(8,128)(2,1)}, u32[]{:S(2)}, u32[]{:S(2)}) async-start(bf16[8,7,24,512]{3,2,1,0:T(8,128)(2,1)} %bitcast.74), calls=%async_computation | async-start | bytes 2752512 | tf_op jit(solution)/shard_map/all_to_all | solution.py:386
  14.0 26.6 %collective-permute-start = (bf16[136,3584]{1,0:T(8,128)(2,1)S(1)}, bf16[136,3584]{1,0:T(8,128)(2,1)S(1)}, u32[]{:S(2)}, u32[]{:S(2)}) collective-permute-start(bf16[136,3584]{1,0:T(8,128)(2,1)S(1)} %copy-done), channel_id=1, source_target_pairs={{0,1},{1,2},{2,3},{3,4},{4,5},{5,6},{6,7},{7,0},{8,9},{9,10},{10,1... | collective-permute-start | bytes 2924552 | tf_op jit(solution)/shard_map/ppermute | solution.py:391
  15.7 25.9 %collective-permute-start.4 = (bf16[136,3584]{1,0:T(8,128)(2,1)S(1)}, bf16[136,3584]{1,0:T(8,128)(2,1)}, u32[]{:S(2)}, u32[]{:S(2)}) collective-permute-start(bf16[136,3584]{1,0:T(8,128)(2,1)S(1)} %copy-done), channel_id=1, source_target_pairs={{0,7},{1,0},{2,1},{3,2},{4,3},{5,4},{6,5},{7,6},{8,15},{9,8},{10,9... | collective-permute-start | bytes 2924552 | tf_op jit(solution)/shard_map/ppermute | solution.py:391
  45.8 39.0 %all-to-all-start.3 = ((bf16[8,14,24,512]{3,2,1,0:T(8,128)(2,1)}), bf16[8,14,24,512]{3,2,1,0:T(8,128)(2,1)}, u32[]{:S(2)}, u32[]{:S(2)}) async-start(bf16[8,14,24,512]{3,2,1,0:T(8,128)(2,1)} %bitcast.69), calls=%async_computation.3 | async-start | bytes 5505024 | tf_op jit(solution)/shard_map/all_to_all | solution.py:386
  50.7 22.3 %collective-permute-start.1 = (bf16[136,3584]{1,0:T(8,128)(2,1)S(1)}, bf16[136,3584]{1,0:T(8,128)(2,1)}, u32[]{:S(2)}, u32[]{:S(2)}) collective-permute-start(bf16[136,3584]{1,0:T(8,128)(2,1)S(1)} %copy-done.2), channel_id=1, source_target_pairs={{0,1},{1,2},{2,3},{3,4},{4,5},{5,6},{6,7},{7,0},{8,9},{9,10},{10,1... | collective-permute-start | bytes 2924552 | tf_op jit(solution)/shard_map/ppermute | solution.py:391
  50.7 22.2 %collective-permute-start.5 = (bf16[136,3584]{1,0:T(8,128)(2,1)}, bf16[136,3584]{1,0:T(8,128)(2,1)}, u32[]{:S(2)}, u32[]{:S(2)}) collective-permute-start(bf16[136,3584]{1,0:T(8,128)(2,1)} %collective-permute-done.4.refs_3_.refs_1_.refs_2_), channel_id=1, source_target_pairs={{0,7},{1,0},{2,1},{3,2},{4,3},{5,4},{6,5},{7,6},{8,15},{9,8},{10,9... | collective-permute-start | bytes 2924552 | tf_op jit(solution)/shard_map/ppermute | solution.py:391
  84.8 38.5 %all-to-all-start.1 = ((bf16[8,14,24,512]{3,2,1,0:T(8,128)(2,1)}), bf16[8,14,24,512]{3,2,1,0:T(8,128)(2,1)}, u32[]{:S(2)}, u32[]{:S(2)}) async-start(bf16[8,14,24,512]{3,2,1,0:T(8,128)(2,1)} %bitcast.71), calls=%async_computation.1 | async-start | bytes 5505024 | tf_op jit(solution)/shard_map/all_to_all | solution.py:386
  89.2 23.3 %collective-permute-start.2 = (bf16[136,3584]{1,0:T(8,128)(2,1)}, bf16[136,3584]{1,0:T(8,128)(2,1)S(1)}, u32[]{:S(2)}, u32[]{:S(2)}) collective-permute-start(bf16[136,3584]{1,0:T(8,128)(2,1)} %collective-permute-done.1.refs_0_.refs_4_.refs_1_), channel_id=1, source_target_pairs={{0,1},{1,2},{2,3},{3,4},{4,5},{5,6},{6,7},{7,0},{8,9},{9,10},{10,1... | collective-permute-start | bytes 2924552 | tf_op jit(solution)/shard_map/ppermute | solution.py:391
  89.3 23.2 %collective-permute-start.6 = (bf16[136,3584]{1,0:T(8,128)(2,1)}, bf16[136,3584]{1,0:T(8,128)(2,1)}, u32[]{:S(2)}, u32[]{:S(2)}) collective-permute-start(bf16[136,3584]{1,0:T(8,128)(2,1)} %collective-permute-done.5.refs_1_.refs_5_.refs_2_), channel_id=1, source_target_pairs={{0,7},{1,0},{2,1},{3,2},{4,3},{5,4},{6,5},{7,6},{8,15},{9,8},{10,9... | collective-permute-start | bytes 2924552 | tf_op jit(solution)/shard_map/ppermute | solution.py:391
  123.3 39.6 %all-to-all-start.4 = ((bf16[8,14,24,512]{3,2,1,0:T(8,128)(2,1)}), bf16[8,14,24,512]{3,2,1,0:T(8,128)(2,1)}, u32[]{:S(2)}, u32[]{:S(2)}) async-start(bf16[8,14,24,512]{3,2,1,0:T(8,128)(2,1)} %bitcast.70), calls=%async_computation.4 | async-start | bytes 5505024 | tf_op jit(solution)/shard_map/all_to_all | solution.py:386
  128.8 25.3 %collective-permute-start.3 = (bf16[136,3584]{1,0:T(8,128)(2,1)S(1)}, bf16[136,3584]{1,0:T(8,128)(2,1)}, u32[]{:S(2)}, u32[]{:S(2)}) collective-permute-start(bf16[136,3584]{1,0:T(8,128)(2,1)S(1)} %copy-done.4), channel_id=1, source_target_pairs={{0,1},{1,2},{2,3},{3,4},{4,5},{5,6},{6,7},{7,0},{8,9},{9,10},{10,1... | collective-permute-start | bytes 2924552 | tf_op jit(solution)/shard_map/ppermute | solution.py:391
  162.9 24.2 %all-to-all-start.2 = ((bf16[8,29,24,128]{3,2,1,0:T(8,128)(2,1)}), bf16[8,29,24,128]{3,2,1,0:T(8,128)(2,1)}, u32[]{:S(2)}, u32[]{:S(2)}) async-start(bf16[8,29,24,128]{3,2,1,0:T(8,128)(2,1)} %bitcast.73), calls=%async_computation.2 | async-start | bytes 2850816 | tf_op jit(solution)/shard_map/all_to_all | solution.py:386
  194.8 24.2 %all-to-all-start.5 = ((bf16[8,29,24,128]{3,2,1,0:T(8,128)(2,1)}), bf16[8,29,24,128]{3,2,1,0:T(8,128)(2,1)}, u32[]{:S(2)}, u32[]{:S(2)}) async-start(bf16[8,29,24,128]{3,2,1,0:T(8,128)(2,1)} %bitcast.77), calls=%async_computation.5 | async-start | bytes 2850816 | tf_op jit(solution)/shard_map/all_to_all | solution.py:386
  219.0 38.5 %all-to-all-start.6 = ((bf16[8,14,24,512]{3,2,1,0:T(8,128)(2,1)}), bf16[8,14,24,512]{3,2,1,0:T(8,128)(2,1)}, u32[]{:S(2)}, u32[]{:S(2)}) async-start(bf16[8,14,24,512]{3,2,1,0:T(8,128)(2,1)} %bitcast.66), calls=%async_computation.6 | async-start | bytes 5505024 | tf_op jit(solution)/shard_map/all_to_all | solution.py:386
  226.4 25.5 %collective-permute-start.7 = (bf16[136,3584]{1,0:T(8,128)(2,1)}, bf16[136,3584]{1,0:T(8,128)(2,1)S(1)}, u32[]{:S(2)}, u32[]{:S(2)}) collective-permute-start(bf16[136,3584]{1,0:T(8,128)(2,1)} %fold_rows.5), channel_id=1, source_target_pairs={{0,7},{1,0},{2,1},{3,2},{4,3},{5,4},{6,5},{7,6},{8,15},{9,8},{10,9... | collective-permute-start | bytes 2924552 | tf_op jit(solution)/shard_map/ppermute | solution.py:391
  257.5 43.3 %all-to-all-start.8 = ((bf16[8,14,24,512]{3,2,1,0:T(8,128)(2,1)}), bf16[8,14,24,512]{3,2,1,0:T(8,128)(2,1)}, u32[]{:S(2)}, u32[]{:S(2)}) async-start(bf16[8,14,24,512]{3,2,1,0:T(8,128)(2,1)} %bitcast.65), calls=%async_computation.8 | async-start | bytes 5505024 | tf_op jit(solution)/shard_map/all_to_all | solution.py:386
  270.8 24.2 %collective-permute-start.8 = (bf16[136,3584]{1,0:T(8,128)(2,1)}, bf16[136,3584]{1,0:T(8,128)(2,1)S(1)}, u32[]{:S(2)}, u32[]{:S(2)}) collective-permute-start(bf16[136,3584]{1,0:T(8,128)(2,1)} %get-tuple-element.40), channel_id=1, source_target_pairs={{0,7},{1,0},{2,1},{3,2},{4,3},{5,4},{6,5},{7,6},{8,15},{9,8},{10,9... | collective-permute-start | bytes 2924552 | tf_op jit(solution)/shard_map/ppermute | solution.py:391
  275.9 22.2 %collective-permute-start.9 = (bf16[136,3584]{1,0:T(8,128)(2,1)}, bf16[136,3584]{1,0:T(8,128)(2,1)}, u32[]{:S(2)}, u32[]{:S(2)}) collective-permute-start(bf16[136,3584]{1,0:T(8,128)(2,1)} %get-tuple-element.41), channel_id=1, source_target_pairs={{0,1},{1,2},{2,3},{3,4},{4,5},{5,6},{6,7},{7,0},{8,9},{9,10},{10,1... | collective-permute-start | bytes 2924552 | tf_op jit(solution)/shard_map/ppermute | solution.py:391
  300.8 39.1 %all-to-all-start.7 = ((bf16[8,14,24,512]{3,2,1,0:T(8,128)(2,1)}), bf16[8,14,24,512]{3,2,1,0:T(8,128)(2,1)}, u32[]{:S(2)}, u32[]{:S(2)}) async-start(bf16[8,14,24,512]{3,2,1,0:T(8,128)(2,1)} %bitcast.67), calls=%async_computation.7 | async-start | bytes 5505024 | tf_op jit(solution)/shard_map/all_to_all | solution.py:386
  310.1 24.3 %collective-permute-start.10 = (bf16[136,3584]{1,0:T(8,128)(2,1)}, bf16[136,3584]{1,0:T(8,128)(2,1)S(1)}, u32[]{:S(2)}, u32[]{:S(2)}) collective-permute-start(bf16[136,3584]{1,0:T(8,128)(2,1)} %get-tuple-element.47), channel_id=1, source_target_pairs={{0,7},{1,0},{2,1},{3,2},{4,3},{5,4},{6,5},{7,6},{8,15},{9,8},{10,9... | collective-permute-start | bytes 2924552 | tf_op jit(solution)/shard_map/ppermute | solution.py:391
  315.0 22.6 %collective-permute-start.11 = (bf16[136,3584]{1,0:T(8,128)(2,1)}, bf16[136,3584]{1,0:T(8,128)(2,1)}, u32[]{:S(2)}, u32[]{:S(2)}) collective-permute-start(bf16[136,3584]{1,0:T(8,128)(2,1)} %get-tuple-element.48), channel_id=1, source_target_pairs={{0,1},{1,2},{2,3},{3,4},{4,5},{5,6},{6,7},{7,0},{8,9},{9,10},{10,1... | collective-permute-start | bytes 2924552 | tf_op jit(solution)/shard_map/ppermute | solution.py:391
  339.9 24.4 %all-to-all-start.9 = ((bf16[8,7,24,512]{3,2,1,0:T(8,128)(2,1)}), bf16[8,7,24,512]{3,2,1,0:T(8,128)(2,1)}, u32[]{:S(2)}, u32[]{:S(2)}) async-start(bf16[8,7,24,512]{3,2,1,0:T(8,128)(2,1)} %bitcast.68), calls=%async_computation.9 | async-start | bytes 2752512 | tf_op jit(solution)/shard_map/all_to_all | solution.py:386
  353.1 25.7 %collective-permute-start.17 = (bf16[64,3584]{1,0:T(8,128)(2,1)}, bf16[64,3584]{1,0:T(8,128)(2,1)S(1)}, u32[]{:S(2)}, u32[]{:S(2)}) collective-permute-start(bf16[64,3584]{1,0:T(8,128)(2,1)} %get-tuple-element.54), channel_id=1, source_target_pairs={{0,71},{1,64},{2,65},{3,66},{4,67},{5,68},{6,69},{7,70},{64,135},{... | collective-permute-start | bytes 1376264 | tf_op jit(solution)/shard_map/ppermute | solution.py:402
  362.3 18.4 %collective-permute-start.18 = (bf16[64,3584]{1,0:T(8,128)(2,1)}, bf16[64,3584]{1,0:T(8,128)(2,1)S(1)}, u32[]{:S(2)}, u32[]{:S(2)}) collective-permute-start(bf16[64,3584]{1,0:T(8,128)(2,1)} %get-tuple-element.55), channel_id=1, source_target_pairs={{0,65},{1,66},{2,67},{3,68},{4,69},{5,70},{6,71},{7,64},{64,129},{... | collective-permute-start | bytes 1376264 | tf_op jit(solution)/shard_map/ppermute | solution.py:402
  (17 other events, 127.9 us)

commit v7 on v6

--- a/solution.py
+++ b/solution.py
@@ -9,7 +9,8 @@
 
 SHARE = 4
 DEPTH = 2 * SHARE
-GROUPS = ((0,), (-1, 1), (-2, 2), (-3, 3), (-4,))
+GROUPS = ((0, -1, 1), (-2, 2), (-3, 3), (-4,))
+BACK = ((-4,), (-3, 3), (-2, 2), (-1, 1), (0,))
 EXTRA = 128
 HALF = 64
 LANES = 128
@@ -73,6 +74,17 @@
 SMEM = pl.BlockSpec(memory_space=pltpu.SMEM)
 VMEM = pl.BlockSpec(memory_space=pltpu.VMEM)
 ANY = pl.BlockSpec(memory_space=pl.ANY)
+
+
+def ordered(block, *others):
+    return pl.pallas_call(
+        lambda *refs: None,
+        out_shape=jax.ShapeDtypeStruct(block.shape, block.dtype),
+        in_specs=[ANY] * (1 + len(others)),
+        out_specs=ANY,
+        input_output_aliases={0: 0},
+        name="ordered",
+    )(block, *others)
 
 
 def pack_kernel(capacity, count, tagged, width, place, *refs):
@@ -238,38 +250,24 @@
         write_tile(out, 0, k, grad.astype(bf16))
 
 
-def slice_grad(first, sides, last, gate_up, earlier):
-    count, slots, full = sides.shape
+def slice_grad(first, offset, count, sides, last, gate_up):
+    _, slots, full = sides.shape
     columns, _, _, span, _ = last.shape
     width = gate_up.shape[0]
     pieces = width // TILE
-    shape = jax.ShapeDtypeStruct((columns, count, pieces, span, TILE), bf16)
-    most = width - TILE
-    shared = [
-        pl.BlockSpec((1, slots, full), lambda m: (m, 0, 0)),
-        pl.BlockSpec((columns, 1, 1, span, EXTRA), lambda m: (0, 0, width // EXTRA, 0, 0)),
-    ]
-    sending = pl.pallas_call(
+    return pl.pallas_call(
         functools.partial(grad_kernel, first),
-        out_shape=shape,
+        out_shape=jax.ShapeDtypeStruct((columns, count, pieces, span, TILE), bf16),
         grid=(count,),
-        in_specs=shared + [pl.BlockSpec((most, full), lambda m: (0, 0))],
-        out_specs=pl.BlockSpec((columns, 1, pieces - 1, span, TILE), lambda m: (0, m, 0, 0, 0)),
+        in_specs=[
+            pl.BlockSpec((1, slots, full), lambda m: (offset + m, 0, 0)),
+            pl.BlockSpec((columns, 1, 1, span, EXTRA), lambda m: (0, 0, width // EXTRA, 0, 0)),
+            pl.BlockSpec((width, full), lambda m: (0, 0)),
+        ],
+        out_specs=pl.BlockSpec((columns, 1, pieces, span, TILE), lambda m: (0, m, 0, 0, 0)),
         compiler_params=params(),
         name="slice_grad",
     )(sides, last, gate_up)
-    return pl.pallas_call(
-        functools.partial(grad_kernel, first),
-        out_shape=shape,
-        grid=(count,),
-        in_specs=shared
-        + [pl.BlockSpec((TILE, full), lambda m: (most // TILE, 0)), ANY]
-        + [ANY] * len(earlier),
-        out_specs=pl.BlockSpec((columns, 1, 1, span, TILE), lambda m: (0, m, pieces - 1, 0, 0)),
-        input_output_aliases={3: 0},
-        compiler_params=params(),
-        name="slice_grad_end",
-    )(sides, last, gate_up, sending, *earlier)
 
 
 def down_kernel(groups, last, *refs):
@@ -427,7 +425,7 @@
         ]
     )
     arrivals = {0: own}
-    for group in GROUPS[1:]:
+    for group in reversed(BACK[:-1]):
         for offset in group:
             toward = 1 if offset < 0 else -1
             arrivals[offset] = hop(arrivals[offset + toward], toward)
@@ -447,6 +445,8 @@
             everyone if last else (),
             earlier,
         )
+        if 1 <= n < len(GROUPS) - 1:
+            sent = ordered(sent, *[arrivals[offset] for offset in GROUPS[n + 1]])
         got = exchange(sent)
         received.append(got)
         if not last:
@@ -458,39 +458,47 @@
     final_hidden, sending = turn(place(GROUPS[-1]), last, preacts, down_proj, gate_up, parts)
     hidden.append(final_hidden)
 
-    first = [sum(len(group) for group in GROUPS[:n]) for n in range(len(GROUPS))]
+    listed = [offset for group in GROUPS for offset in group]
     part_rows = None
     coming = []
-    folded = []
-    down_grad = None
-    for n in reversed(range(len(GROUPS))):
-        group = GROUPS[n]
+    for n, group in enumerate(BACK):
         returned = exchange(sending)
         if part_rows is None:
             part_rows = returned
         earlier = []
-        if n > 0:
+        if n + 1 < len(BACK):
+            following = BACK[n + 1]
+            start = listed.index(following[0])
+            source = [following[0] in g for g in GROUPS].index(True)
             held = list(coming)
-            if n == len(GROUPS) - 3:
+            if n == 2:
                 down_grad = down_grads(received, hidden, width)
                 held.append(down_grad)
-            sending = slice_grad(first[n - 1], sides[n - 1], last, gate_up, held)
+            sending = slice_grad(
+                start,
+                GROUPS[source].index(following[0]),
+                len(following),
+                sides[source],
+                last,
+                gate_up,
+            )
+            sending = ordered(sending, *held) if held else sending
             earlier = [sending]
         folded = fold(
             place(group),
-            first[n],
+            listed.index(group[0]),
             part_rows,
             returned,
             [arrivals[offset] for offset in group],
             coming,
             capacity,
-            n <= 1,
+            n >= len(BACK) - 2,
             earlier,
         )
         along = [-1 if offset < 0 else 1 for offset in group]
-        if n > 1:
+        if n < len(BACK) - 2:
             coming = [hop(block, way) for block, way in zip(folded, along)]
-        elif n == 1:
+        elif n == len(BACK) - 2:
             coming = [hop(folded[3 * m + 2], way) for m, way in enumerate(along)]
             above = [shifted(folded[3 * m], -1, way) for m, way in enumerate(along)]
             below = [shifted(folded[3 * m + 1], 1, way) for m, way in enumerate(along)]

time: 399 us -> 417 us (1.045)
  waiting for transfers between devices: 164 us -> 209 us
  Pallas kernels: 106 us -> 93.6 us
  starting transfers between devices: 107 us -> 95.2 us
    all_to_all x10 -> x9, waiting for transfers between devices: 47.4 us -> 94.4 us  [exchange(): lax.all_to_all(merged, 'column', split_axis=0, concat_axis=0, tiled=True)]
    ppermute x14, starting transfers between devices: 32.8 us -> 16.5 us  [hop(): lax.ppermute(block, 'depth', [(i, (i + distance) % DEPTH) for i in range(...]
    pallas_call x8 -> x9, Pallas kernels: 30.9 us -> 23 us  [the longest x4 23 us: slice_grad(): pl.pallas_call(functools.partial(grad_kernel, first), out_shape=jax.Shape...]
    all_to_all x10 -> x9, starting transfers between devices: 52 us -> 58.6 us  [exchange(): lax.all_to_all(merged, 'column', split_axis=0, concat_axis=0, tiled=True)]
    pallas_call x4 -> x3, Pallas kernels: 19.5 us -> 16.7 us  [prepare(): pl.pallas_call(prepare_kernel, out_shape=[jax.ShapeDtypeStruct((count, sl...]
    pallas_call x5 -> x4, Pallas kernels: 18.9 us -> 17.1 us  [pack(): pl.pallas_call(functools.partial(pack_kernel, capacity, len(arrivals), le...]
  transfers between devices with their start and end apart: 30 -> 29, of which waited for: 19 -> 21; matrix products, arithmetic and copies ran while one was open for 2% -> 2% of each run, Pallas kernels for 24% -> 19%
where the time goes in v7:
time: 417 us; the launch traced here: 415 us
  waiting for transfers between devices  209 us (50%)
  starting transfers between devices  95.2 us (23%)
  Pallas kernels  93.6 us (22%)
  other arithmetic  9.76 us (2%)
  local copies, waits for them, and re-layouts  6.91 us (2%)
    ppermute x14, waiting for transfers between devices, hop(): lax.ppermute(block, 'depth', [(i, (i + distance) % DEPTH) for i in range(...  98.9 us
    all_to_all x9, waiting for transfers between devices, exchange(): lax.all_to_all(merged, 'column', split_axis=0, concat_axis=0, tiled=True)  94.4 us
    all_to_all x9, starting transfers between devices, exchange(): lax.all_to_all(merged, 'column', split_axis=0, concat_axis=0, tiled=True)  58.6 us
    pallas_call x4, Pallas kernels, slice_grad(): pl.pallas_call(functools.partial(grad_kernel, first), out_shape=jax.Shape...  23 us
    ppermute x6, starting transfers between devices, shifted(): return lax.ppermute(block, ('section', 'depth'), route)  20.1 us
    pallas_call x5, Pallas kernels, fold(): pl.pallas_call(functools.partial(fold_kernel, capacity, first, count, len...  19 us
    pallas_call x4, Pallas kernels, pack(): pl.pallas_call(functools.partial(pack_kernel, capacity, len(arrivals), le...  17.1 us
    pallas_call x3, Pallas kernels, prepare(): pl.pallas_call(prepare_kernel, out_shape=[jax.ShapeDtypeStruct((count, sl...  16.7 us
  transfers between devices with their start and end apart: 29, of which 21 were waited for; matrix products, arithmetic and copies ran while one was open for 2% of the time, Pallas kernels for 19%

profile of v7, /device:TPU:1, one launch (start us, length us, event | category | flops | bytes accessed | tf_op | source)
XLA Modules:
  0.0 415.4 jit_solution(12990526331499776985)
XLA Ops:
  10.6 20.6 %collective-permute-done.refs_2_.refs_1_ = bf16[136,3584]{1,0:T(8,128)(2,1)S(1)} collective-permute-done((bf16[136,3584]{1,0:T(8,128)(2,1)S(1)}, bf16[136,3584]{1,0:T(8,128)(2,1)S(1)}, u32[]{:S(2)}, u32[]{:S(2)}) %collective-permute-start) | collective-permute-done | bytes 974880 | tf_op jit(solution)/shard_map/ppermute | solution.py:389
  45.6 20.2 %collective-permute-done.1.refs_0_.refs_4_.refs_1_ = bf16[136,3584]{1,0:T(8,128)(2,1)} collective-permute-done((bf16[136,3584]{1,0:T(8,128)(2,1)S(1)}, bf16[136,3584]{1,0:T(8,128)(2,1)}, u32[]{:S(2)}, u32[]{:S(2)}) %collective-permute-start.1) | collective-permute-done | bytes 974880 | tf_op jit(solution)/shard_map/ppermute | solution.py:389
  77.3 10.7 %collective-permute-done.2.refs_1_.refs_6_.refs_0_ = bf16[136,3584]{1,0:T(8,128)(2,1)S(1)} collective-permute-done((bf16[136,3584]{1,0:T(8,128)(2,1)}, bf16[136,3584]{1,0:T(8,128)(2,1)S(1)}, u32[]{:S(2)}, u32[]{:S(2)}) %collective-permute-start.2) | collective-permute-done | bytes 974880 | tf_op jit(solution)/shard_map/ppermute | solution.py:389
  91.8 13.6 %all-to-all-start = ((bf16[8,14,24,512]{3,2,1,0:T(8,128)(2,1)}), bf16[8,14,24,512]{3,2,1,0:T(8,128)(2,1)}, u32[]{:S(2)}, u32[]{:S(2)}) async-start(bf16[8,14,24,512]{3,2,1,0:T(8,128)(2,1)} %bitcast.60), calls=%async_computation | async-start | bytes 5505024 | tf_op jit(solution)/shard_map/all_to_all | solution.py:384
  106.1 6.6 %prepare.4 = (f32[3,192,512]{2,1,0:T(8,128)}, f32[3,192,256]{2,1,0:T(8,128)}, f32[3,192,128]{2,1,0:T(8,128)}) custom-call(s32[4]{0:T(128)} %pad_add_fusion.3.place, bf16[8,3,7,24,512]{4,3,2,1,0:T(8,128)(2,1)} %bitcast.21.rows.refs_0_, bf16[8,8,24,512]{3,2,1,0:T(8,128)(2,1)} %pad_maximum_fusion.refs_2_.preacts, bf16[256,3584]{1,0:T(8,128)(2,1)} %bitcast.56), custom_call_target="tpu_custom_call" | custom-call | tf_op jit(solution)/shard_map/prepare/pallas_call | solution.py:161
  116.9 10.2 %collective-permute-done.3.refs_0_.refs_8_.refs_1_ = bf16[136,3584]{1,0:T(8,128)(2,1)} collective-permute-done((bf16[136,3584]{1,0:T(8,128)(2,1)S(1)}, bf16[136,3584]{1,0:T(8,128)(2,1)}, u32[]{:S(2)}, u32[]{:S(2)}) %collective-permute-start.3) | collective-permute-done | bytes 974880 | tf_op jit(solution)/shard_map/ppermute | solution.py:389
  127.1 12.5 %all-to-all-done = bf16[8,14,24,512]{3,2,1,0:T(8,128)(2,1)} async-done(((bf16[8,14,24,512]{3,2,1,0:T(8,128)(2,1)}), bf16[8,14,24,512]{3,2,1,0:T(8,128)(2,1)}, u32[]{:S(2)}, u32[]{:S(2)}) %all-to-all-start) | async-done | bytes 2752544 | tf_op jit(solution)/shard_map/all_to_all | solution.py:384
  153.1 25.0 %all-to-all-done.3 = bf16[8,14,24,512]{3,2,1,0:T(8,128)(2,1)} async-done(((bf16[8,14,24,512]{3,2,1,0:T(8,128)(2,1)}), bf16[8,14,24,512]{3,2,1,0:T(8,128)(2,1)}, u32[]{:S(2)}, u32[]{:S(2)}) %all-to-all-start.3) | async-done | bytes 2752544 | tf_op jit(solution)/shard_map/all_to_all | solution.py:384
  178.1 8.9 %all-to-all-start.1 = ((bf16[8,29,24,128]{3,2,1,0:T(8,128)(2,1)}), bf16[8,29,24,128]{3,2,1,0:T(8,128)(2,1)}, u32[]{:S(2)}, u32[]{:S(2)}) async-start(bf16[8,29,24,128]{3,2,1,0:T(8,128)(2,1)} %bitcast.66), calls=%async_computation.1 | async-start | bytes 2850816 | tf_op jit(solution)/shard_map/all_to_all | solution.py:384
  192.0 14.9 %all-to-all-done.1 = bf16[8,29,24,128]{3,2,1,0:T(8,128)(2,1)} async-done(((bf16[8,29,24,128]{3,2,1,0:T(8,128)(2,1)}), bf16[8,29,24,128]{3,2,1,0:T(8,128)(2,1)}, u32[]{:S(2)}, u32[]{:S(2)}) %all-to-all-start.1) | async-done | bytes 1425440 | tf_op jit(solution)/shard_map/all_to_all | solution.py:384
  206.9 7.6 %turn.1 = (f32[1,192,256]{2,1,0:T(8,128)}, bf16[8,1,29,24,128]{4,3,2,1,0:T(8,128)(2,1)}) custom-call(s32[2]{0:T(128)} %pad_add_fusion.1.place, bf16[8,1,29,24,128]{4,3,2,1,0:T(8,128)(2,1)} %bitcast.17.received.last.refs_3_, bf16[8,8,24,512]{3,2,1,0:T(8,128)(2,1)} %pad_maximum_fusion.refs_2_.preacts, bf16[256,3584]{1,0:T(8,128)(2,1)} %bitcast.59, ...), custom_call_target="tpu_custom_call" | custom-call | tf_op jit(solution)/shard_map/turn/pallas_call | solution.py:215
  218.7 6.1 %slice_grad.5.refs_2_ = bf16[8,2,7,24,512]{4,3,2,1,0:T(8,128)(2,1)} custom-call(f32[2,192,512]{2,1,0:T(8,128)} %get-tuple-element.34.sides, bf16[8,1,29,24,128]{4,3,2,1,0:T(8,128)(2,1)} %bitcast.17.received.last.refs_3_, bf16[3584,512]{1,0:T(8,128)(2,1)} %bitcast.50), custom_call_target="tpu_custom_call" | custom-call | tf_op jit(solution)/shard_map/slice_grad/pallas_call | solution.py:258
  224.9 13.8 %all-to-all-done.4 = bf16[8,29,24,128]{3,2,1,0:T(8,128)(2,1)} async-done(((bf16[8,29,24,128]{3,2,1,0:T(8,128)(2,1)}), bf16[8,29,24,128]{3,2,1,0:T(8,128)(2,1)}, u32[]{:S(2)}, u32[]{:S(2)}) %all-to-all-start.4) | async-done | bytes 1425440 | tf_op jit(solution)/shard_map/all_to_all | solution.py:384
  246.1 6.1 %slice_grad.6.refs_0_ = bf16[8,2,7,24,512]{4,3,2,1,0:T(8,128)(2,1)} custom-call(f32[2,192,512]{2,1,0:T(8,128)} %get-tuple-element.28.refs_9_.sides, bf16[8,1,29,24,128]{4,3,2,1,0:T(8,128)(2,1)} %bitcast.17.received.last.refs_3_, bf16[3584,512]{1,0:T(8,128)(2,1)} %bitcast.51), custom_call_target="tpu_custom_call" | custom-call | tf_op jit(solution)/shard_map/slice_grad/pallas_call | solution.py:258
  252.2 16.5 %collective-permute-done.7.refs_1_.refs_3_ = bf16[136,3584]{1,0:T(8,128)(2,1)S(1)} collective-permute-done((bf16[136,3584]{1,0:T(8,128)(2,1)}, bf16[136,3584]{1,0:T(8,128)(2,1)S(1)}, u32[]{:S(2)}, u32[]{:S(2)}) %collective-permute-start.7) | collective-permute-done | bytes 974880 | tf_op jit(solution)/shard_map/ppermute | solution.py:389
  269.6 7.6 %all-to-all-done.5 = bf16[8,14,24,512]{3,2,1,0:T(8,128)(2,1)} async-done(((bf16[8,14,24,512]{3,2,1,0:T(8,128)(2,1)}), bf16[8,14,24,512]{3,2,1,0:T(8,128)(2,1)}, u32[]{:S(2)}, u32[]{:S(2)}) %all-to-all-start.5) | async-done | bytes 2752544 | tf_op jit(solution)/shard_map/all_to_all | solution.py:384
  277.2 9.0 %all-to-all-start.7 = ((bf16[8,14,24,512]{3,2,1,0:T(8,128)(2,1)}), bf16[8,14,24,512]{3,2,1,0:T(8,128)(2,1)}, u32[]{:S(2)}, u32[]{:S(2)}) async-start(bf16[8,14,24,512]{3,2,1,0:T(8,128)(2,1)} %bitcast.55), calls=%async_computation.7 | async-start | bytes 5505024 | tf_op jit(solution)/shard_map/all_to_all | solution.py:384
  291.9 6.1 %slice_grad.4.refs_0_ = bf16[8,2,7,24,512]{4,3,2,1,0:T(8,128)(2,1)} custom-call(f32[3,192,512]{2,1,0:T(8,128)} %get-tuple-element.31.refs_2_.sides, bf16[8,1,29,24,128]{4,3,2,1,0:T(8,128)(2,1)} %bitcast.17.received.last.refs_3_, bf16[3584,512]{1,0:T(8,128)(2,1)} %bitcast.52), custom_call_target="tpu_custom_call" | custom-call | tf_op jit(solution)/shard_map/slice_grad/pallas_call | solution.py:258
  298.0 10.2 %down_grads.1.refs_3_ = bf16[256,3584]{1,0:T(8,128)(2,1)} custom-call(bf16[8,1,29,24,128]{4,3,2,1,0:T(8,128)(2,1)} %bitcast.17.received.last.refs_3_, bf16[8,3,7,24,512]{4,3,2,1,0:T(8,128)(2,1)} %bitcast.21.rows.refs_0_, bf16[8,2,7,24,512]{4,3,2,1,0:T(8,128)(2,1)} %bitcast.14.rows.refs_1_, bf16[8,2,7,24,512]{4,3,2,1,0:T(8,128)(2,1)} %bitcast.25.rows.refs_2_, ...), custom_call_target="tpu_custom_call" | custom-call | tf_op jit(solution)/shard_map/down_grads/pallas_call | solution.py:302
  312.7 7.6 %all-to-all-done.7 = bf16[8,14,24,512]{3,2,1,0:T(8,128)(2,1)} async-done(((bf16[8,14,24,512]{3,2,1,0:T(8,128)(2,1)}), bf16[8,14,24,512]{3,2,1,0:T(8,128)(2,1)}, u32[]{:S(2)}, u32[]{:S(2)}) %all-to-all-start.7) | async-done | bytes 2752544 | tf_op jit(solution)/shard_map/all_to_all | solution.py:384
  335.4 15.3 %collective-permute-done.10.refs_1_.refs_3_ = bf16[136,3584]{1,0:T(8,128)(2,1)S(1)} collective-permute-done((bf16[136,3584]{1,0:T(8,128)(2,1)}, bf16[136,3584]{1,0:T(8,128)(2,1)S(1)}, u32[]{:S(2)}, u32[]{:S(2)}) %collective-permute-start.10) | collective-permute-done | bytes 974880 | tf_op jit(solution)/shard_map/ppermute | solution.py:389
  351.7 7.2 %all-to-all-done.6 = bf16[8,14,24,512]{3,2,1,0:T(8,128)(2,1)} async-done(((bf16[8,14,24,512]{3,2,1,0:T(8,128)(2,1)}), bf16[8,14,24,512]{3,2,1,0:T(8,128)(2,1)}, u32[]{:S(2)}, u32[]{:S(2)}) %all-to-all-start.6) | async-done | bytes 2752544 | tf_op jit(solution)/shard_map/all_to_all | solution.py:384
  370.2 7.8 %collective-permute-start.17 = (bf16[64,3584]{1,0:T(8,128)(2,1)}, bf16[64,3584]{1,0:T(8,128)(2,1)S(1)}, u32[]{:S(2)}, u32[]{:S(2)}) collective-permute-start(bf16[64,3584]{1,0:T(8,128)(2,1)} %get-tuple-element.48), channel_id=1, source_target_pairs={{0,71},{1,64},{2,65},{3,66},{4,67},{5,68},{6,69},{7,70},{64,135},{... | collective-permute-start | bytes 1376264 | tf_op jit(solution)/shard_map/ppermute | solution.py:400
  398.7 8.6 %collective-permute-done.12 = bf16[64,3584]{1,0:T(8,128)(2,1)S(1)} collective-permute-done((bf16[64,3584]{1,0:T(8,128)(2,1)}, bf16[64,3584]{1,0:T(8,128)(2,1)S(1)}, u32[]{:S(2)}, u32[]{:S(2)}) %collective-permute-start.12) | collective-permute-done | bytes 458784 | tf_op jit(solution)/shard_map/ppermute | solution.py:400
  (99 shorter events, 142.0 us)
Async XLA Ops:
  3.4 27.8 %collective-permute-start = (bf16[136,3584]{1,0:T(8,128)(2,1)S(1)}, bf16[136,3584]{1,0:T(8,128)(2,1)S(1)}, u32[]{:S(2)}, u32[]{:S(2)}) collective-permute-start(bf16[136,3584]{1,0:T(8,128)(2,1)S(1)} %pad_maximum_fusion.1.refs_1_.refs_0_), channel_id=1, source_target_pairs={{0,1},{1,2},{2,3},{3,4},{4,5},{5,6},{6,7},{7,0},{8,9},{9,10},{10,1... | collective-permute-start | bytes 2924552 | tf_op jit(solution)/shard_map/ppermute | solution.py:389
  6.0 26.3 %collective-permute-start.4 = (bf16[136,3584]{1,0:T(8,128)(2,1)S(1)}, bf16[136,3584]{1,0:T(8,128)(2,1)}, u32[]{:S(2)}, u32[]{:S(2)}) collective-permute-start(bf16[136,3584]{1,0:T(8,128)(2,1)S(1)} %pad_maximum_fusion.1.refs_1_.refs_0_), channel_id=1, source_target_pairs={{0,7},{1,0},{2,1},{3,2},{4,3},{5,4},{6,5},{7,6},{8,15},{9,8},{10,9... | collective-permute-start | bytes 2924552 | tf_op jit(solution)/shard_map/ppermute | solution.py:389
  37.7 54.1 %all-to-all-start.2 = ((bf16[8,21,24,512]{3,2,1,0:T(8,128)(2,1)}), bf16[8,21,24,512]{3,2,1,0:T(8,128)(2,1)}, u32[]{:S(2)}, u32[]{:S(2)}) async-start(bf16[8,21,24,512]{3,2,1,0:T(8,128)(2,1)} %bitcast.64), calls=%async_computation.2 | async-start | bytes 8257536 | tf_op jit(solution)/shard_map/all_to_all | solution.py:384
  42.9 23.0 %collective-permute-start.1 = (bf16[136,3584]{1,0:T(8,128)(2,1)S(1)}, bf16[136,3584]{1,0:T(8,128)(2,1)}, u32[]{:S(2)}, u32[]{:S(2)}) collective-permute-start(bf16[136,3584]{1,0:T(8,128)(2,1)S(1)} %copy-done.4), channel_id=1, source_target_pairs={{0,1},{1,2},{2,3},{3,4},{4,5},{5,6},{6,7},{7,0},{8,9},{9,10},{10,1... | collective-permute-start | bytes 2924552 | tf_op jit(solution)/shard_map/ppermute | solution.py:389
  43.0 22.9 %collective-permute-start.5 = (bf16[136,3584]{1,0:T(8,128)(2,1)}, bf16[136,3584]{1,0:T(8,128)(2,1)}, u32[]{:S(2)}, u32[]{:S(2)}) collective-permute-start(bf16[136,3584]{1,0:T(8,128)(2,1)} %collective-permute-done.4.refs_3_.refs_2_), channel_id=1, source_target_pairs={{0,7},{1,0},{2,1},{3,2},{4,3},{5,4},{6,5},{7,6},{8,15},{9,8},{10,9... | collective-permute-start | bytes 2924552 | tf_op jit(solution)/shard_map/ppermute | solution.py:389
  65.8 22.2 %collective-permute-start.2 = (bf16[136,3584]{1,0:T(8,128)(2,1)}, bf16[136,3584]{1,0:T(8,128)(2,1)S(1)}, u32[]{:S(2)}, u32[]{:S(2)}) collective-permute-start(bf16[136,3584]{1,0:T(8,128)(2,1)} %collective-permute-done.1.refs_0_.refs_4_.refs_1_), channel_id=1, source_target_pairs={{0,1},{1,2},{2,3},{3,4},{4,5},{5,6},{6,7},{7,0},{8,9},{9,10},{10,1... | collective-permute-start | bytes 2924552 | tf_op jit(solution)/shard_map/ppermute | solution.py:389
  65.8 22.2 %collective-permute-start.6 = (bf16[136,3584]{1,0:T(8,128)(2,1)}, bf16[136,3584]{1,0:T(8,128)(2,1)}, u32[]{:S(2)}, u32[]{:S(2)}) collective-permute-start(bf16[136,3584]{1,0:T(8,128)(2,1)} %collective-permute-done.5.refs_1_.refs_5_.refs_2_), channel_id=1, source_target_pairs={{0,7},{1,0},{2,1},{3,2},{4,3},{5,4},{6,5},{7,6},{8,15},{9,8},{10,9... | collective-permute-start | bytes 2924552 | tf_op jit(solution)/shard_map/ppermute | solution.py:389
  91.8 47.8 %all-to-all-start = ((bf16[8,14,24,512]{3,2,1,0:T(8,128)(2,1)}), bf16[8,14,24,512]{3,2,1,0:T(8,128)(2,1)}, u32[]{:S(2)}, u32[]{:S(2)}) async-start(bf16[8,14,24,512]{3,2,1,0:T(8,128)(2,1)} %bitcast.60), calls=%async_computation | async-start | bytes 5505024 | tf_op jit(solution)/shard_map/all_to_all | solution.py:384
  105.4 21.7 %collective-permute-start.3 = (bf16[136,3584]{1,0:T(8,128)(2,1)S(1)}, bf16[136,3584]{1,0:T(8,128)(2,1)}, u32[]{:S(2)}, u32[]{:S(2)}) collective-permute-start(bf16[136,3584]{1,0:T(8,128)(2,1)S(1)} %copy-done.1), channel_id=1, source_target_pairs={{0,1},{1,2},{2,3},{3,4},{4,5},{5,6},{6,7},{7,0},{8,9},{9,10},{10,1... | collective-permute-start | bytes 2924552 | tf_op jit(solution)/shard_map/ppermute | solution.py:389
  139.5 38.5 %all-to-all-start.3 = ((bf16[8,14,24,512]{3,2,1,0:T(8,128)(2,1)}), bf16[8,14,24,512]{3,2,1,0:T(8,128)(2,1)}, u32[]{:S(2)}, u32[]{:S(2)}) async-start(bf16[8,14,24,512]{3,2,1,0:T(8,128)(2,1)} %bitcast.61), calls=%async_computation.3 | async-start | bytes 5505024 | tf_op jit(solution)/shard_map/all_to_all | solution.py:384
  178.1 28.8 %all-to-all-start.1 = ((bf16[8,29,24,128]{3,2,1,0:T(8,128)(2,1)}), bf16[8,29,24,128]{3,2,1,0:T(8,128)(2,1)}, u32[]{:S(2)}, u32[]{:S(2)}) async-start(bf16[8,29,24,128]{3,2,1,0:T(8,128)(2,1)} %bitcast.66), calls=%async_computation.1 | async-start | bytes 2850816 | tf_op jit(solution)/shard_map/all_to_all | solution.py:384
  214.5 24.2 %all-to-all-start.4 = ((bf16[8,29,24,128]{3,2,1,0:T(8,128)(2,1)}), bf16[8,29,24,128]{3,2,1,0:T(8,128)(2,1)}, u32[]{:S(2)}, u32[]{:S(2)}) async-start(bf16[8,29,24,128]{3,2,1,0:T(8,128)(2,1)} %bitcast.69), calls=%async_computation.4 | async-start | bytes 2850816 | tf_op jit(solution)/shard_map/all_to_all | solution.py:384
  238.6 38.6 %all-to-all-start.5 = ((bf16[8,14,24,512]{3,2,1,0:T(8,128)(2,1)}), bf16[8,14,24,512]{3,2,1,0:T(8,128)(2,1)}, u32[]{:S(2)}, u32[]{:S(2)}) async-start(bf16[8,14,24,512]{3,2,1,0:T(8,128)(2,1)} %bitcast.62), calls=%async_computation.5 | async-start | bytes 5505024 | tf_op jit(solution)/shard_map/all_to_all | solution.py:384
  246.1 22.6 %collective-permute-start.7 = (bf16[136,3584]{1,0:T(8,128)(2,1)}, bf16[136,3584]{1,0:T(8,128)(2,1)S(1)}, u32[]{:S(2)}, u32[]{:S(2)}) collective-permute-start(bf16[136,3584]{1,0:T(8,128)(2,1)} %fold_rows.5), channel_id=1, source_target_pairs={{0,7},{1,0},{2,1},{3,2},{4,3},{5,4},{6,5},{7,6},{8,15},{9,8},{10,9... | collective-permute-start | bytes 2924552 | tf_op jit(solution)/shard_map/ppermute | solution.py:389
  277.2 43.2 %all-to-all-start.7 = ((bf16[8,14,24,512]{3,2,1,0:T(8,128)(2,1)}), bf16[8,14,24,512]{3,2,1,0:T(8,128)(2,1)}, u32[]{:S(2)}, u32[]{:S(2)}) async-start(bf16[8,14,24,512]{3,2,1,0:T(8,128)(2,1)} %bitcast.55), calls=%async_computation.7 | async-start | bytes 5505024 | tf_op jit(solution)/shard_map/all_to_all | solution.py:384
  290.4 21.4 %collective-permute-start.8 = (bf16[136,3584]{1,0:T(8,128)(2,1)}, bf16[136,3584]{1,0:T(8,128)(2,1)S(1)}, u32[]{:S(2)}, u32[]{:S(2)}) collective-permute-start(bf16[136,3584]{1,0:T(8,128)(2,1)} %get-tuple-element.35), channel_id=1, source_target_pairs={{0,7},{1,0},{2,1},{3,2},{4,3},{5,4},{6,5},{7,6},{8,15},{9,8},{10,9... | collective-permute-start | bytes 2924552 | tf_op jit(solution)/shard_map/ppermute | solution.py:389
  290.4 22.3 %collective-permute-start.9 = (bf16[136,3584]{1,0:T(8,128)(2,1)}, bf16[136,3584]{1,0:T(8,128)(2,1)}, u32[]{:S(2)}, u32[]{:S(2)}) collective-permute-start(bf16[136,3584]{1,0:T(8,128)(2,1)} %get-tuple-element.36), channel_id=1, source_target_pairs={{0,1},{1,2},{2,3},{3,4},{4,5},{5,6},{6,7},{7,0},{8,9},{9,10},{10,1... | collective-permute-start | bytes 2924552 | tf_op jit(solution)/shard_map/ppermute | solution.py:389
  320.4 38.5 %all-to-all-start.6 = ((bf16[8,14,24,512]{3,2,1,0:T(8,128)(2,1)}), bf16[8,14,24,512]{3,2,1,0:T(8,128)(2,1)}, u32[]{:S(2)}, u32[]{:S(2)}) async-start(bf16[8,14,24,512]{3,2,1,0:T(8,128)(2,1)} %bitcast.54), calls=%async_computation.6 | async-start | bytes 5505024 | tf_op jit(solution)/shard_map/all_to_all | solution.py:384
  329.3 21.4 %collective-permute-start.10 = (bf16[136,3584]{1,0:T(8,128)(2,1)}, bf16[136,3584]{1,0:T(8,128)(2,1)S(1)}, u32[]{:S(2)}, u32[]{:S(2)}) collective-permute-start(bf16[136,3584]{1,0:T(8,128)(2,1)} %get-tuple-element.41), channel_id=1, source_target_pairs={{0,7},{1,0},{2,1},{3,2},{4,3},{5,4},{6,5},{7,6},{8,15},{9,8},{10,9... | collective-permute-start | bytes 2924552 | tf_op jit(solution)/shard_map/ppermute | solution.py:389
  329.3 22.3 %collective-permute-start.11 = (bf16[136,3584]{1,0:T(8,128)(2,1)}, bf16[136,3584]{1,0:T(8,128)(2,1)}, u32[]{:S(2)}, u32[]{:S(2)}) collective-permute-start(bf16[136,3584]{1,0:T(8,128)(2,1)} %get-tuple-element.42), channel_id=1, source_target_pairs={{0,1},{1,2},{2,3},{3,4},{4,5},{5,6},{6,7},{7,0},{8,9},{9,10},{10,1... | collective-permute-start | bytes 2924552 | tf_op jit(solution)/shard_map/ppermute | solution.py:389
  358.9 24.2 %all-to-all-start.8 = ((bf16[8,7,24,512]{3,2,1,0:T(8,128)(2,1)}), bf16[8,7,24,512]{3,2,1,0:T(8,128)(2,1)}, u32[]{:S(2)}, u32[]{:S(2)}) async-start(bf16[8,7,24,512]{3,2,1,0:T(8,128)(2,1)} %bitcast.63), calls=%async_computation.8 | async-start | bytes 2752512 | tf_op jit(solution)/shard_map/all_to_all | solution.py:384
  370.2 25.6 %collective-permute-start.17 = (bf16[64,3584]{1,0:T(8,128)(2,1)}, bf16[64,3584]{1,0:T(8,128)(2,1)S(1)}, u32[]{:S(2)}, u32[]{:S(2)}) collective-permute-start(bf16[64,3584]{1,0:T(8,128)(2,1)} %get-tuple-element.48), channel_id=1, source_target_pairs={{0,71},{1,64},{2,65},{3,66},{4,67},{5,68},{6,69},{7,70},{64,135},{... | collective-permute-start | bytes 1376264 | tf_op jit(solution)/shard_map/ppermute | solution.py:400
  378.0 19.7 %collective-permute-start.18 = (bf16[64,3584]{1,0:T(8,128)(2,1)}, bf16[64,3584]{1,0:T(8,128)(2,1)S(1)}, u32[]{:S(2)}, u32[]{:S(2)}) collective-permute-start(bf16[64,3584]{1,0:T(8,128)(2,1)} %get-tuple-element.49), channel_id=1, source_target_pairs={{0,65},{1,66},{2,67},{3,68},{4,69},{5,70},{6,71},{7,64},{64,129},{... | collective-permute-start | bytes 1376264 | tf_op jit(solution)/shard_map/ppermute | solution.py:400
  395.8 18.6 %collective-permute-start.16 = (bf16[64,3584]{1,0:T(8,128)(2,1)}, bf16[64,3584]{1,0:T(8,128)(2,1)S(1)}, u32[]{:S(2)}, u32[]{:S(2)}) collective-permute-start(bf16[64,3584]{1,0:T(8,128)(2,1)} %get-tuple-element.47), channel_id=1, source_target_pairs={{64,0},{65,1},{66,2},{67,3},{68,4},{69,5},{70,6},{71,7},{128,64},{... | collective-permute-start | bytes 1376264 | tf_op jit(solution)/shard_map/ppermute | solution.py:400
  (15 other events, 129.2 us)

commit v8 on v7

--- a/solution.py
+++ b/solution.py
@@ -9,7 +9,7 @@
 
 SHARE = 4
 DEPTH = 2 * SHARE
-GROUPS = ((0, -1, 1), (-2, 2), (-3, 3), (-4,))
+GROUPS = ((0,), (-1, 1), (-2, 2), (-3, 3), (-4,))
 BACK = ((-4,), (-3, 3), (-2, 2), (-1, 1), (0,))
 EXTRA = 128
 HALF = 64
@@ -445,8 +445,6 @@
             everyone if last else (),
             earlier,
         )
-        if 1 <= n < len(GROUPS) - 1:
-            sent = ordered(sent, *[arrivals[offset] for offset in GROUPS[n + 1]])
         got = exchange(sent)
         received.append(got)
         if not last:

time: 417 us -> 399 us (0.957)
  waiting for transfers between devices: 209 us -> 170 us
  starting transfers between devices: 95.2 us -> 108 us
  Pallas kernels: 93.6 us -> 98.2 us
    all_to_all x9 -> x10, waiting for transfers between devices: 94.4 us -> 56.6 us  [exchange(): lax.all_to_all(merged, 'column', split_axis=0, concat_axis=0, tiled=True)]
    ppermute x14, starting transfers between devices: 16.5 us -> 33.7 us  [hop(): lax.ppermute(block, 'depth', [(i, (i + distance) % DEPTH) for i in range(...]
    all_to_all x9 -> x10, starting transfers between devices: 58.6 us -> 51.5 us  [exchange(): lax.all_to_all(merged, 'column', split_axis=0, concat_axis=0, tiled=True)]
    pallas_call x3 -> x4, Pallas kernels: 16.7 us -> 19.5 us  [prepare(): pl.pallas_call(prepare_kernel, out_shape=[jax.ShapeDtypeStruct((count, sl...]
    pallas_call x4 -> x5, Pallas kernels: 17.1 us -> 18.9 us  [pack(): pl.pallas_call(functools.partial(pack_kernel, capacity, len(arrivals), le...]
  transfers between devices with their start and end apart: 29 -> 30, of which waited for: 21 -> 20; matrix products, arithmetic and copies ran while one was open for 2% -> 2% of each run, Pallas kernels for 19% -> 22%
where the time goes in v8:
time: 399 us; the launch traced here: 396 us
  waiting for transfers between devices  170 us (43%)
  starting transfers between devices  108 us (27%)
  Pallas kernels  98.2 us (25%)
  other arithmetic  11.4 us (3%)
  local copies, waits for them, and re-layouts  6.91 us (2%)
    ppermute x14, waiting for transfers between devices, hop(): lax.ppermute(block, 'depth', [(i, (i + distance) % DEPTH) for i in range(...  101 us
    all_to_all x10, waiting for transfers between devices, exchange(): lax.all_to_all(merged, 'column', split_axis=0, concat_axis=0, tiled=True)  56.6 us
    all_to_all x10, starting transfers between devices, exchange(): lax.all_to_all(merged, 'column', split_axis=0, concat_axis=0, tiled=True)  51.5 us
    ppermute x14, starting transfers between devices, hop(): lax.ppermute(block, 'depth', [(i, (i + distance) % DEPTH) for i in range(...  33.7 us
    pallas_call x4, Pallas kernels, slice_grad(): pl.pallas_call(functools.partial(grad_kernel, first), out_shape=jax.Shape...  23 us
    ppermute x6, starting transfers between devices, shifted(): return lax.ppermute(block, ('section', 'depth'), route)  22.8 us
    pallas_call x4, Pallas kernels, prepare(): pl.pallas_call(prepare_kernel, out_shape=[jax.ShapeDtypeStruct((count, sl...  19.5 us
    pallas_call x5, Pallas kernels, fold(): pl.pallas_call(functools.partial(fold_kernel, capacity, first, count, len...  18.9 us
  transfers between devices with their start and end apart: 30, of which 20 were waited for; matrix products, arithmetic and copies ran while one was open for 2% of the time, Pallas kernels for 22%

profile of v8, /device:TPU:1, one launch (start us, length us, event | category | flops | bytes accessed | tf_op | source)
XLA Modules:
  0.0 395.8 jit_solution(1607180992762118851)
XLA Ops:
  8.0 6.0 %all-to-all-start = ((bf16[8,7,24,512]{3,2,1,0:T(8,128)(2,1)}), bf16[8,7,24,512]{3,2,1,0:T(8,128)(2,1)}, u32[]{:S(2)}, u32[]{:S(2)}) async-start(bf16[8,7,24,512]{3,2,1,0:T(8,128)(2,1)} %bitcast.70), calls=%async_computation | async-start | bytes 2752512 | tf_op jit(solution)/shard_map/all_to_all | solution.py:384
  25.2 15.4 %collective-permute-done.refs_2_.refs_0_.refs_1_ = bf16[136,3584]{1,0:T(8,128)(2,1)S(1)} collective-permute-done((bf16[136,3584]{1,0:T(8,128)(2,1)S(1)}, bf16[136,3584]{1,0:T(8,128)(2,1)S(1)}, u32[]{:S(2)}, u32[]{:S(2)}) %collective-permute-start) | collective-permute-done | bytes 974880 | tf_op jit(solution)/shard_map/ppermute | solution.py:389
  58.1 14.8 %collective-permute-done.1.refs_0_.refs_4_.refs_1_ = bf16[136,3584]{1,0:T(8,128)(2,1)} collective-permute-done((bf16[136,3584]{1,0:T(8,128)(2,1)S(1)}, bf16[136,3584]{1,0:T(8,128)(2,1)}, u32[]{:S(2)}, u32[]{:S(2)}) %collective-permute-start.1) | collective-permute-done | bytes 974880 | tf_op jit(solution)/shard_map/ppermute | solution.py:389
  77.2 7.6 %all-to-all-done.3 = bf16[8,14,24,512]{3,2,1,0:T(8,128)(2,1)} async-done(((bf16[8,14,24,512]{3,2,1,0:T(8,128)(2,1)}), bf16[8,14,24,512]{3,2,1,0:T(8,128)(2,1)}, u32[]{:S(2)}, u32[]{:S(2)}) %all-to-all-start.3) | async-done | bytes 2752544 | tf_op jit(solution)/shard_map/all_to_all | solution.py:384
  97.7 14.8 %collective-permute-done.2.refs_6_.refs_0_.refs_1_ = bf16[136,3584]{1,0:T(8,128)(2,1)S(1)} collective-permute-done((bf16[136,3584]{1,0:T(8,128)(2,1)}, bf16[136,3584]{1,0:T(8,128)(2,1)S(1)}, u32[]{:S(2)}, u32[]{:S(2)}) %collective-permute-start.2) | collective-permute-done | bytes 974880 | tf_op jit(solution)/shard_map/ppermute | solution.py:389
  117.6 5.7 %all-to-all-done.1 = bf16[8,14,24,512]{3,2,1,0:T(8,128)(2,1)} async-done(((bf16[8,14,24,512]{3,2,1,0:T(8,128)(2,1)}), bf16[8,14,24,512]{3,2,1,0:T(8,128)(2,1)}, u32[]{:S(2)}, u32[]{:S(2)}) %all-to-all-start.1) | async-done | bytes 2752544 | tf_op jit(solution)/shard_map/all_to_all | solution.py:384
  123.3 5.5 %all-to-all-start.4 = ((bf16[8,14,24,512]{3,2,1,0:T(8,128)(2,1)}), bf16[8,14,24,512]{3,2,1,0:T(8,128)(2,1)}, u32[]{:S(2)}, u32[]{:S(2)}) async-start(bf16[8,14,24,512]{3,2,1,0:T(8,128)(2,1)} %bitcast.66), calls=%async_computation.4 | async-start | bytes 5505024 | tf_op jit(solution)/shard_map/all_to_all | solution.py:384
  136.4 17.8 %collective-permute-done.3.refs_0_.refs_8_.refs_1_ = bf16[136,3584]{1,0:T(8,128)(2,1)} collective-permute-done((bf16[136,3584]{1,0:T(8,128)(2,1)S(1)}, bf16[136,3584]{1,0:T(8,128)(2,1)}, u32[]{:S(2)}, u32[]{:S(2)}) %collective-permute-start.3) | collective-permute-done | bytes 974880 | tf_op jit(solution)/shard_map/ppermute | solution.py:389
  157.5 5.4 %all-to-all-done.4 = bf16[8,14,24,512]{3,2,1,0:T(8,128)(2,1)} async-done(((bf16[8,14,24,512]{3,2,1,0:T(8,128)(2,1)}), bf16[8,14,24,512]{3,2,1,0:T(8,128)(2,1)}, u32[]{:S(2)}, u32[]{:S(2)}) %all-to-all-start.4) | async-done | bytes 2752544 | tf_op jit(solution)/shard_map/all_to_all | solution.py:384
  167.3 5.2 %prepare.7 = (f32[2,192,512]{2,1,0:T(8,128)}, f32[2,192,256]{2,1,0:T(8,128)}, f32[2,192,128]{2,1,0:T(8,128)}) custom-call(s32[3]{0:T(128)} %pad_add_fusion.4.place, bf16[8,2,7,24,512]{4,3,2,1,0:T(8,128)(2,1)} %bitcast.27.rows.refs_3_, bf16[8,8,24,512]{3,2,1,0:T(8,128)(2,1)} %pad_maximum_fusion.preacts.refs_2_, bf16[256,3584]{1,0:T(8,128)(2,1)} %bitcast.59), custom_call_target="tpu_custom_call" | custom-call | tf_op jit(solution)/shard_map/prepare/pallas_call | solution.py:161
  172.4 14.7 %all-to-all-done.2 = bf16[8,29,24,128]{3,2,1,0:T(8,128)(2,1)} async-done(((bf16[8,29,24,128]{3,2,1,0:T(8,128)(2,1)}), bf16[8,29,24,128]{3,2,1,0:T(8,128)(2,1)}, u32[]{:S(2)}, u32[]{:S(2)}) %all-to-all-start.2) | async-done | bytes 1425440 | tf_op jit(solution)/shard_map/all_to_all | solution.py:384
  187.1 7.7 %turn.1 = (f32[1,192,256]{2,1,0:T(8,128)}, bf16[8,1,29,24,128]{4,3,2,1,0:T(8,128)(2,1)}) custom-call(s32[2]{0:T(128)} %pad_add_fusion.1.place, bf16[8,1,29,24,128]{4,3,2,1,0:T(8,128)(2,1)} %bitcast.20.received.last.refs_4_, bf16[8,8,24,512]{3,2,1,0:T(8,128)(2,1)} %pad_maximum_fusion.preacts.refs_2_, bf16[256,3584]{1,0:T(8,128)(2,1)} %bitcast.60, ...), custom_call_target="tpu_custom_call" | custom-call | tf_op jit(solution)/shard_map/turn/pallas_call | solution.py:215
  199.1 6.1 %slice_grad.5.refs_2_ = bf16[8,2,7,24,512]{4,3,2,1,0:T(8,128)(2,1)} custom-call(f32[2,192,512]{2,1,0:T(8,128)} %get-tuple-element.39.sides, bf16[8,1,29,24,128]{4,3,2,1,0:T(8,128)(2,1)} %bitcast.20.received.last.refs_4_, bf16[3584,512]{1,0:T(8,128)(2,1)} %bitcast.52), custom_call_target="tpu_custom_call" | custom-call | tf_op jit(solution)/shard_map/slice_grad/pallas_call | solution.py:258
  205.2 13.8 %all-to-all-done.5 = bf16[8,29,24,128]{3,2,1,0:T(8,128)(2,1)} async-done(((bf16[8,29,24,128]{3,2,1,0:T(8,128)(2,1)}), bf16[8,29,24,128]{3,2,1,0:T(8,128)(2,1)}, u32[]{:S(2)}, u32[]{:S(2)}) %all-to-all-start.5) | async-done | bytes 1425440 | tf_op jit(solution)/shard_map/all_to_all | solution.py:384
  226.4 5.2 %collective-permute-start.7 = (bf16[136,3584]{1,0:T(8,128)(2,1)}, bf16[136,3584]{1,0:T(8,128)(2,1)S(1)}, u32[]{:S(2)}, u32[]{:S(2)}) collective-permute-start(bf16[136,3584]{1,0:T(8,128)(2,1)} %fold_rows.5), channel_id=1, source_target_pairs={{0,7},{1,0},{2,1},{3,2},{4,3},{5,4},{6,5},{7,6},{8,15},{9,8},{10,9... | collective-permute-start | bytes 2924552 | tf_op jit(solution)/shard_map/ppermute | solution.py:389
  231.5 6.1 %slice_grad.6.refs_0_ = bf16[8,2,7,24,512]{4,3,2,1,0:T(8,128)(2,1)} custom-call(f32[2,192,512]{2,1,0:T(8,128)} %get-tuple-element.32.refs_9_.sides, bf16[8,1,29,24,128]{4,3,2,1,0:T(8,128)(2,1)} %bitcast.20.received.last.refs_4_, bf16[3584,512]{1,0:T(8,128)(2,1)} %bitcast.53), custom_call_target="tpu_custom_call" | custom-call | tf_op jit(solution)/shard_map/slice_grad/pallas_call | solution.py:258
  237.7 14.3 %collective-permute-done.7.refs_1_.refs_3_ = bf16[136,3584]{1,0:T(8,128)(2,1)S(1)} collective-permute-done((bf16[136,3584]{1,0:T(8,128)(2,1)}, bf16[136,3584]{1,0:T(8,128)(2,1)S(1)}, u32[]{:S(2)}, u32[]{:S(2)}) %collective-permute-start.7) | collective-permute-done | bytes 974880 | tf_op jit(solution)/shard_map/ppermute | solution.py:389
  257.5 9.0 %all-to-all-start.8 = ((bf16[8,14,24,512]{3,2,1,0:T(8,128)(2,1)}), bf16[8,14,24,512]{3,2,1,0:T(8,128)(2,1)}, u32[]{:S(2)}, u32[]{:S(2)}) async-start(bf16[8,14,24,512]{3,2,1,0:T(8,128)(2,1)} %bitcast.62), calls=%async_computation.8 | async-start | bytes 5505024 | tf_op jit(solution)/shard_map/all_to_all | solution.py:384
  275.9 6.1 %slice_grad.4.refs_0_ = bf16[8,2,7,24,512]{4,3,2,1,0:T(8,128)(2,1)} custom-call(f32[2,192,512]{2,1,0:T(8,128)} %get-tuple-element.36.refs_2_.sides, bf16[8,1,29,24,128]{4,3,2,1,0:T(8,128)(2,1)} %bitcast.20.received.last.refs_4_, bf16[3584,512]{1,0:T(8,128)(2,1)} %bitcast.54), custom_call_target="tpu_custom_call" | custom-call | tf_op jit(solution)/shard_map/slice_grad/pallas_call | solution.py:258
  282.0 10.3 %down_grads.1.refs_3_ = bf16[256,3584]{1,0:T(8,128)(2,1)} custom-call(bf16[8,1,29,24,128]{4,3,2,1,0:T(8,128)(2,1)} %bitcast.20.received.last.refs_4_, bf16[8,1,7,24,512]{4,3,2,1,0:T(8,128)(2,1)} %bitcast.13.rows.refs_0_, bf16[8,2,7,24,512]{4,3,2,1,0:T(8,128)(2,1)} %bitcast.23.rows.refs_1_, bf16[8,2,7,24,512]{4,3,2,1,0:T(8,128)(2,1)} %bitcast.18.rows.refs_2_, ...), custom_call_target="tpu_custom_call" | custom-call | tf_op jit(solution)/shard_map/down_grads/pallas_call | solution.py:302
  309.6 5.2 %collective-permute-start.10 = (bf16[136,3584]{1,0:T(8,128)(2,1)}, bf16[136,3584]{1,0:T(8,128)(2,1)S(1)}, u32[]{:S(2)}, u32[]{:S(2)}) collective-permute-start(bf16[136,3584]{1,0:T(8,128)(2,1)} %get-tuple-element.47), channel_id=1, source_target_pairs={{0,7},{1,0},{2,1},{3,2},{4,3},{5,4},{6,5},{7,6},{8,15},{9,8},{10,9... | collective-permute-start | bytes 2924552 | tf_op jit(solution)/shard_map/ppermute | solution.py:389
  319.4 14.5 %collective-permute-done.10.refs_1_.refs_3_ = bf16[136,3584]{1,0:T(8,128)(2,1)S(1)} collective-permute-done((bf16[136,3584]{1,0:T(8,128)(2,1)}, bf16[136,3584]{1,0:T(8,128)(2,1)S(1)}, u32[]{:S(2)}, u32[]{:S(2)}) %collective-permute-start.10) | collective-permute-done | bytes 974880 | tf_op jit(solution)/shard_map/ppermute | solution.py:389
  353.0 9.3 %collective-permute-start.17 = (bf16[64,3584]{1,0:T(8,128)(2,1)}, bf16[64,3584]{1,0:T(8,128)(2,1)S(1)}, u32[]{:S(2)}, u32[]{:S(2)}) collective-permute-start(bf16[64,3584]{1,0:T(8,128)(2,1)} %get-tuple-element.54), channel_id=1, source_target_pairs={{0,71},{1,64},{2,65},{3,66},{4,67},{5,68},{6,69},{7,70},{64,135},{... | collective-permute-start | bytes 1376264 | tf_op jit(solution)/shard_map/ppermute | solution.py:400
  385.4 6.8 %collective-permute-done.13 = bf16[64,3584]{1,0:T(8,128)(2,1)S(1)} collective-permute-done((bf16[64,3584]{1,0:T(8,128)(2,1)}, bf16[64,3584]{1,0:T(8,128)(2,1)S(1)}, u32[]{:S(2)}, u32[]{:S(2)}) %collective-permute-start.13) | collective-permute-done | bytes 458784 | tf_op jit(solution)/shard_map/ppermute | solution.py:400
  (102 shorter events, 167.6 us)
Async XLA Ops:
  8.0 37.8 %all-to-all-start = ((bf16[8,7,24,512]{3,2,1,0:T(8,128)(2,1)}), bf16[8,7,24,512]{3,2,1,0:T(8,128)(2,1)}, u32[]{:S(2)}, u32[]{:S(2)}) async-start(bf16[8,7,24,512]{3,2,1,0:T(8,128)(2,1)} %bitcast.70), calls=%async_computation | async-start | bytes 2752512 | tf_op jit(solution)/shard_map/all_to_all | solution.py:384
  14.0 26.6 %collective-permute-start = (bf16[136,3584]{1,0:T(8,128)(2,1)S(1)}, bf16[136,3584]{1,0:T(8,128)(2,1)S(1)}, u32[]{:S(2)}, u32[]{:S(2)}) collective-permute-start(bf16[136,3584]{1,0:T(8,128)(2,1)S(1)} %copy-done), channel_id=1, source_target_pairs={{0,1},{1,2},{2,3},{3,4},{4,5},{5,6},{6,7},{7,0},{8,9},{9,10},{10,1... | collective-permute-start | bytes 2924552 | tf_op jit(solution)/shard_map/ppermute | solution.py:389
  15.7 25.9 %collective-permute-start.4 = (bf16[136,3584]{1,0:T(8,128)(2,1)S(1)}, bf16[136,3584]{1,0:T(8,128)(2,1)}, u32[]{:S(2)}, u32[]{:S(2)}) collective-permute-start(bf16[136,3584]{1,0:T(8,128)(2,1)S(1)} %copy-done), channel_id=1, source_target_pairs={{0,7},{1,0},{2,1},{3,2},{4,3},{5,4},{6,5},{7,6},{8,15},{9,8},{10,9... | collective-permute-start | bytes 2924552 | tf_op jit(solution)/shard_map/ppermute | solution.py:389
  45.8 39.0 %all-to-all-start.3 = ((bf16[8,14,24,512]{3,2,1,0:T(8,128)(2,1)}), bf16[8,14,24,512]{3,2,1,0:T(8,128)(2,1)}, u32[]{:S(2)}, u32[]{:S(2)}) async-start(bf16[8,14,24,512]{3,2,1,0:T(8,128)(2,1)} %bitcast.65), calls=%async_computation.3 | async-start | bytes 5505024 | tf_op jit(solution)/shard_map/all_to_all | solution.py:384
  50.7 22.3 %collective-permute-start.1 = (bf16[136,3584]{1,0:T(8,128)(2,1)S(1)}, bf16[136,3584]{1,0:T(8,128)(2,1)}, u32[]{:S(2)}, u32[]{:S(2)}) collective-permute-start(bf16[136,3584]{1,0:T(8,128)(2,1)S(1)} %copy-done.2), channel_id=1, source_target_pairs={{0,1},{1,2},{2,3},{3,4},{4,5},{5,6},{6,7},{7,0},{8,9},{9,10},{10,1... | collective-permute-start | bytes 2924552 | tf_op jit(solution)/shard_map/ppermute | solution.py:389
  50.7 22.2 %collective-permute-start.5 = (bf16[136,3584]{1,0:T(8,128)(2,1)}, bf16[136,3584]{1,0:T(8,128)(2,1)}, u32[]{:S(2)}, u32[]{:S(2)}) collective-permute-start(bf16[136,3584]{1,0:T(8,128)(2,1)} %collective-permute-done.4.refs_3_.refs_1_.refs_2_), channel_id=1, source_target_pairs={{0,7},{1,0},{2,1},{3,2},{4,3},{5,4},{6,5},{7,6},{8,15},{9,8},{10,9... | collective-permute-start | bytes 2924552 | tf_op jit(solution)/shard_map/ppermute | solution.py:389
  84.8 38.5 %all-to-all-start.1 = ((bf16[8,14,24,512]{3,2,1,0:T(8,128)(2,1)}), bf16[8,14,24,512]{3,2,1,0:T(8,128)(2,1)}, u32[]{:S(2)}, u32[]{:S(2)}) async-start(bf16[8,14,24,512]{3,2,1,0:T(8,128)(2,1)} %bitcast.67), calls=%async_computation.1 | async-start | bytes 5505024 | tf_op jit(solution)/shard_map/all_to_all | solution.py:384
  89.2 23.3 %collective-permute-start.2 = (bf16[136,3584]{1,0:T(8,128)(2,1)}, bf16[136,3584]{1,0:T(8,128)(2,1)S(1)}, u32[]{:S(2)}, u32[]{:S(2)}) collective-permute-start(bf16[136,3584]{1,0:T(8,128)(2,1)} %collective-permute-done.1.refs_0_.refs_4_.refs_1_), channel_id=1, source_target_pairs={{0,1},{1,2},{2,3},{3,4},{4,5},{5,6},{6,7},{7,0},{8,9},{9,10},{10,1... | collective-permute-start | bytes 2924552 | tf_op jit(solution)/shard_map/ppermute | solution.py:389
  89.3 23.2 %collective-permute-start.6 = (bf16[136,3584]{1,0:T(8,128)(2,1)}, bf16[136,3584]{1,0:T(8,128)(2,1)}, u32[]{:S(2)}, u32[]{:S(2)}) collective-permute-start(bf16[136,3584]{1,0:T(8,128)(2,1)} %collective-permute-done.5.refs_1_.refs_5_.refs_2_), channel_id=1, source_target_pairs={{0,7},{1,0},{2,1},{3,2},{4,3},{5,4},{6,5},{7,6},{8,15},{9,8},{10,9... | collective-permute-start | bytes 2924552 | tf_op jit(solution)/shard_map/ppermute | solution.py:389
  123.3 39.6 %all-to-all-start.4 = ((bf16[8,14,24,512]{3,2,1,0:T(8,128)(2,1)}), bf16[8,14,24,512]{3,2,1,0:T(8,128)(2,1)}, u32[]{:S(2)}, u32[]{:S(2)}) async-start(bf16[8,14,24,512]{3,2,1,0:T(8,128)(2,1)} %bitcast.66), calls=%async_computation.4 | async-start | bytes 5505024 | tf_op jit(solution)/shard_map/all_to_all | solution.py:384
  128.8 25.3 %collective-permute-start.3 = (bf16[136,3584]{1,0:T(8,128)(2,1)S(1)}, bf16[136,3584]{1,0:T(8,128)(2,1)}, u32[]{:S(2)}, u32[]{:S(2)}) collective-permute-start(bf16[136,3584]{1,0:T(8,128)(2,1)S(1)} %copy-done.4), channel_id=1, source_target_pairs={{0,1},{1,2},{2,3},{3,4},{4,5},{5,6},{6,7},{7,0},{8,9},{9,10},{10,1... | collective-permute-start | bytes 2924552 | tf_op jit(solution)/shard_map/ppermute | solution.py:389
  162.9 24.2 %all-to-all-start.2 = ((bf16[8,29,24,128]{3,2,1,0:T(8,128)(2,1)}), bf16[8,29,24,128]{3,2,1,0:T(8,128)(2,1)}, u32[]{:S(2)}, u32[]{:S(2)}) async-start(bf16[8,29,24,128]{3,2,1,0:T(8,128)(2,1)} %bitcast.69), calls=%async_computation.2 | async-start | bytes 2850816 | tf_op jit(solution)/shard_map/all_to_all | solution.py:384
  194.8 24.2 %all-to-all-start.5 = ((bf16[8,29,24,128]{3,2,1,0:T(8,128)(2,1)}), bf16[8,29,24,128]{3,2,1,0:T(8,128)(2,1)}, u32[]{:S(2)}, u32[]{:S(2)}) async-start(bf16[8,29,24,128]{3,2,1,0:T(8,128)(2,1)} %bitcast.73), calls=%async_computation.5 | async-start | bytes 2850816 | tf_op jit(solution)/shard_map/all_to_all | solution.py:384
  219.0 38.5 %all-to-all-start.6 = ((bf16[8,14,24,512]{3,2,1,0:T(8,128)(2,1)}), bf16[8,14,24,512]{3,2,1,0:T(8,128)(2,1)}, u32[]{:S(2)}, u32[]{:S(2)}) async-start(bf16[8,14,24,512]{3,2,1,0:T(8,128)(2,1)} %bitcast.63), calls=%async_computation.6 | async-start | bytes 5505024 | tf_op jit(solution)/shard_map/all_to_all | solution.py:384
  226.4 25.5 %collective-permute-start.7 = (bf16[136,3584]{1,0:T(8,128)(2,1)}, bf16[136,3584]{1,0:T(8,128)(2,1)S(1)}, u32[]{:S(2)}, u32[]{:S(2)}) collective-permute-start(bf16[136,3584]{1,0:T(8,128)(2,1)} %fold_rows.5), channel_id=1, source_target_pairs={{0,7},{1,0},{2,1},{3,2},{4,3},{5,4},{6,5},{7,6},{8,15},{9,8},{10,9... | collective-permute-start | bytes 2924552 | tf_op jit(solution)/shard_map/ppermute | solution.py:389
  257.5 43.2 %all-to-all-start.8 = ((bf16[8,14,24,512]{3,2,1,0:T(8,128)(2,1)}), bf16[8,14,24,512]{3,2,1,0:T(8,128)(2,1)}, u32[]{:S(2)}, u32[]{:S(2)}) async-start(bf16[8,14,24,512]{3,2,1,0:T(8,128)(2,1)} %bitcast.62), calls=%async_computation.8 | async-start | bytes 5505024 | tf_op jit(solution)/shard_map/all_to_all | solution.py:384
  270.8 24.2 %collective-permute-start.8 = (bf16[136,3584]{1,0:T(8,128)(2,1)}, bf16[136,3584]{1,0:T(8,128)(2,1)S(1)}, u32[]{:S(2)}, u32[]{:S(2)}) collective-permute-start(bf16[136,3584]{1,0:T(8,128)(2,1)} %get-tuple-element.40), channel_id=1, source_target_pairs={{0,7},{1,0},{2,1},{3,2},{4,3},{5,4},{6,5},{7,6},{8,15},{9,8},{10,9... | collective-permute-start | bytes 2924552 | tf_op jit(solution)/shard_map/ppermute | solution.py:389
  275.9 22.2 %collective-permute-start.9 = (bf16[136,3584]{1,0:T(8,128)(2,1)}, bf16[136,3584]{1,0:T(8,128)(2,1)}, u32[]{:S(2)}, u32[]{:S(2)}) collective-permute-start(bf16[136,3584]{1,0:T(8,128)(2,1)} %get-tuple-element.41), channel_id=1, source_target_pairs={{0,1},{1,2},{2,3},{3,4},{4,5},{5,6},{6,7},{7,0},{8,9},{9,10},{10,1... | collective-permute-start | bytes 2924552 | tf_op jit(solution)/shard_map/ppermute | solution.py:389
  300.7 38.5 %all-to-all-start.7 = ((bf16[8,14,24,512]{3,2,1,0:T(8,128)(2,1)}), bf16[8,14,24,512]{3,2,1,0:T(8,128)(2,1)}, u32[]{:S(2)}, u32[]{:S(2)}) async-start(bf16[8,14,24,512]{3,2,1,0:T(8,128)(2,1)} %bitcast.61), calls=%async_computation.7 | async-start | bytes 5505024 | tf_op jit(solution)/shard_map/all_to_all | solution.py:384
  309.6 24.4 %collective-permute-start.10 = (bf16[136,3584]{1,0:T(8,128)(2,1)}, bf16[136,3584]{1,0:T(8,128)(2,1)S(1)}, u32[]{:S(2)}, u32[]{:S(2)}) collective-permute-start(bf16[136,3584]{1,0:T(8,128)(2,1)} %get-tuple-element.47), channel_id=1, source_target_pairs={{0,7},{1,0},{2,1},{3,2},{4,3},{5,4},{6,5},{7,6},{8,15},{9,8},{10,9... | collective-permute-start | bytes 2924552 | tf_op jit(solution)/shard_map/ppermute | solution.py:389
  314.8 22.4 %collective-permute-start.11 = (bf16[136,3584]{1,0:T(8,128)(2,1)}, bf16[136,3584]{1,0:T(8,128)(2,1)}, u32[]{:S(2)}, u32[]{:S(2)}) collective-permute-start(bf16[136,3584]{1,0:T(8,128)(2,1)} %get-tuple-element.48), channel_id=1, source_target_pairs={{0,1},{1,2},{2,3},{3,4},{4,5},{5,6},{6,7},{7,0},{8,9},{9,10},{10,1... | collective-permute-start | bytes 2924552 | tf_op jit(solution)/shard_map/ppermute | solution.py:389
  339.2 25.0 %all-to-all-start.9 = ((bf16[8,7,24,512]{3,2,1,0:T(8,128)(2,1)}), bf16[8,7,24,512]{3,2,1,0:T(8,128)(2,1)}, u32[]{:S(2)}, u32[]{:S(2)}) async-start(bf16[8,7,24,512]{3,2,1,0:T(8,128)(2,1)} %bitcast.64), calls=%async_computation.9 | async-start | bytes 2752512 | tf_op jit(solution)/shard_map/all_to_all | solution.py:384
  353.0 25.8 %collective-permute-start.17 = (bf16[64,3584]{1,0:T(8,128)(2,1)}, bf16[64,3584]{1,0:T(8,128)(2,1)S(1)}, u32[]{:S(2)}, u32[]{:S(2)}) collective-permute-start(bf16[64,3584]{1,0:T(8,128)(2,1)} %get-tuple-element.54), channel_id=1, source_target_pairs={{0,71},{1,64},{2,65},{3,66},{4,67},{5,68},{6,69},{7,70},{64,135},{... | collective-permute-start | bytes 1376264 | tf_op jit(solution)/shard_map/ppermute | solution.py:400
  362.3 18.4 %collective-permute-start.18 = (bf16[64,3584]{1,0:T(8,128)(2,1)}, bf16[64,3584]{1,0:T(8,128)(2,1)S(1)}, u32[]{:S(2)}, u32[]{:S(2)}) collective-permute-start(bf16[64,3584]{1,0:T(8,128)(2,1)} %get-tuple-element.55), channel_id=1, source_target_pairs={{0,65},{1,66},{2,67},{3,68},{4,69},{5,70},{6,71},{7,64},{64,129},{... | collective-permute-start | bytes 1376264 | tf_op jit(solution)/shard_map/ppermute | solution.py:400
  (17 other events, 126.4 us)
